TPU v7x, 32 devices: a whole 2x2x4 slice. The times are simulated.
32 devices in a mesh: seq: 8 (over y, x, core), tp: 4 (over z).
Axes of the slice: x: 2, y: 2, z: 4, core: 2. Of those that a mesh axis runs over, the one named last changes fastest.
Arguments:
- patches: bfloat16 [2048, 1024], P('seq', 'tp'), may hold values from -6 to 6
- byte_embed: bfloat16 [16384, 1024], P('seq', 'tp'), may hold values from -6 to 6
- seq_lengths: int32 [6], replicated, may hold values from 1 to 1024, 2048 in all
- norm_global: float32 [1024], replicated, may hold values from 0.5 to 1.5
- proj_gate: bfloat16 [1024, 2048], P(None, 'tp'), may hold values from -0.1875 to 0.1875
- proj_inner: bfloat16 [1024, 2048], P(None, 'tp'), may hold values from -0.1875 to 0.1875
- proj_state: bfloat16 [1024, 256], replicated, may hold values from -0.1875 to 0.1875
- proj_step: bfloat16 [1024, 32], P(None, 'tp'), may hold values from -0.1875 to 0.1875
- step_bias: float32 [32], P('tp'), may hold values from -3 to 0.5
- decay_log: float32 [32], P('tp'), may hold values from -7 to -1
- conv_inner: float32 [4, 2048], P(None, 'tp'), may hold values from -3 to 3
- conv_state: float32 [4, 256], replicated, may hold values from -3 to 3
- skip_gain: float32 [32], P('tp'), may hold values from 0.5 to 1.5
- mixer_gain: float32 [2048], P('tp'), may hold values from 0.5 to 1.5
- proj_mixer: bfloat16 [2048, 1024], P('tp'), may hold values from -0.125 to 0.125
- norm_attn: float32 [1024], replicated, may hold values from 0.5 to 1.5
- attn_input: bfloat16 [3, 1024, 1024], P(None, None, 'tp'), may hold values from -0.1875 to 0.1875
- attn_output: bfloat16 [1024, 1024], P('tp'), may hold values from -0.375 to 0.375
- norm_ffn: float32 [1024], replicated, may hold values from 0.5 to 1.5
- expand_weight: bfloat16 [2, 1024, 4096], P(None, None, 'tp'), may hold values from -0.1875 to 0.1875
- shrink_weight: bfloat16 [4096, 1024], P('tp'), may hold values from -0.09375 to 0.09375
- grad_output: bfloat16 [16384, 1024], P('seq', 'tp'), may hold values from -6 to 6
Outputs:
- layer_output: bfloat16 [16384, 1024], P('seq', 'tp')
- embed_grad: float32 [16384, 1024], P('seq', 'tp')
- patch_grad: float32 [2048, 1024], P('seq', 'tp')
- norm_global_grad: float32 [1024], replicated
- proj_gate_grad: float32 [1024, 2048], P(None, 'tp')
- proj_inner_grad: float32 [1024, 2048], P(None, 'tp')
- proj_state_grad: float32 [1024, 256], replicated
- proj_step_grad: float32 [1024, 32], P(None, 'tp')
- step_bias_grad: float32 [32], P('tp')
- decay_log_grad: float32 [32], P('tp')
- conv_inner_grad: float32 [4, 2048], P(None, 'tp')
- conv_state_grad: float32 [4, 256], replicated
- skip_gain_grad: float32 [32], P('tp')
- mixer_gain_grad: float32 [2048], P('tp')
- proj_mixer_grad: float32 [2048, 1024], P('tp')
- norm_attn_grad: float32 [1024], replicated
- attn_input_grad: float32 [3, 1024, 1024], P(None, None, 'tp')
- attn_output_grad: float32 [1024, 1024], P('tp')
- norm_ffn_grad: float32 [1024], replicated
- expand_grad: float32 [2, 1024, 4096], P(None, None, 'tp')
- shrink_grad: float32 [4096, 1024], P('tp')
Inputs may be any that keep to these rules, and one draw needn't show every extreme that they name: `seq_lengths`: lengths of the packed sequences in patches; they sum to 2048 and the longest is exactly 1024.
All inputs are finite; a program needn't handle non-finite values.
Results may differ from a plain program's by a relative error of at most 0.023.
The roundings to bfloat16 on the way count: a program that leaves them out, or rounds other values in their place, can miss the bound.
Values may be sent and summed in bfloat16 or wider, within the bound.
No kernel may reach another device: no remote copies, remote signals or barrier semaphores. Data moves between devices by JAX's collectives and lax.ppermute only.
A program may use at most 256 MiB of HBM per device.

v0:
```python
import jax
import jax.numpy as jnp
from jax import lax
from jax.sharding import PartitionSpec as P

D = 1024
HEAD_DIM = 64
STATE = 128
HEADS_A = 16
CONV = 4
PATCH = 8
DI = 2048


epsilon = 1e-05
highest = lax.Precision.HIGHEST


def shifted(block, axis, distance):
    devices = range(lax.axis_size(axis))
    route = [(i - distance, i) for i in devices if i - distance in devices]
    return lax.ppermute(block, axis, route)


def entering(part, axis, combine, identity, reverse):
    count = lax.axis_size(axis)
    place = lax.axis_index(axis)
    ahead = count - 1 - place if reverse else place
    gathered = jax.tree.map(lambda a: lax.all_gather(a, axis), part)
    state = jax.tree.map(lambda a, e: jnp.zeros_like(a) + jnp.asarray(e, a.dtype), part, identity)

    def one(lap, state):
        source = count - 1 - lap if reverse else lap
        return combine(
            state, jax.tree.map(lambda a: lax.dynamic_index_in_dim(a, source, 0, False), gathered)
        )

    return lax.fori_loop(0, ahead, one, state)


def rms_scale(values):
    return values * lax.rsqrt(jnp.mean(values * values, axis=-1, keepdims=True) + epsilon)


def sequence_first(positions, lengths):
    offsets = jnp.cumsum(lengths) - lengths
    chosen = jnp.where(offsets[None, :] <= positions[:, None], offsets[None, :], 0)
    return jnp.max(chosen, axis=1)


def causal_conv(padded, weight, positions, first):
    count = positions.shape[0]
    total = jnp.zeros((count, padded.shape[1]), jnp.float32)
    for offset in range(CONV):
        lag = CONV - 1 - offset
        keep = (positions - lag >= first).astype(jnp.float32)[:, None]
        total = total + weight[offset][None, :] * padded[offset : offset + count] * keep
    return total


def front_part(padded, step_raw, conv_weight, step_bias, decay_log, positions, first):
    activated = jax.nn.silu(causal_conv(padded, conv_weight, positions, first))
    inner = activated.shape[1] - 2 * STATE
    count = positions.shape[0]
    inner_vals = activated[:, :inner].reshape(count, inner // HEAD_DIM, HEAD_DIM)
    bmatrix = activated[:, inner : inner + STATE]
    cmatrix = activated[:, inner + STATE :]
    steps = jax.nn.softplus(step_raw + step_bias[None, :])
    rates = -jnp.exp(decay_log)
    return (inner_vals, bmatrix, cmatrix, steps, rates)


def block_summary(inner_vals, bmatrix, steps, rates, positions, first):
    logs = jnp.cumsum(steps * rates[None, :], axis=0)
    final = logs[-1]
    in_last = (first == first[-1]).astype(jnp.float32)[:, None]
    weights = jnp.exp(final[None, :] - logs) * in_last * steps
    carried = jnp.exp(final) * (first[-1] < positions[0]).astype(jnp.float32)
    states = jnp.einsum("sh,shp,sn->hpn", weights, inner_vals, bmatrix, precision=highest)
    return (carried, states)


def block_output(inner_vals, bmatrix, cmatrix, steps, rates, skip_gain, incoming, positions, first):
    logs = jnp.cumsum(steps * rates[None, :], axis=0)
    count = positions.shape[0]
    same = (first[:, None] == first[None, :]) & (positions[None, :] <= positions[:, None])
    diff = logs.T[:, :, None] - logs.T[:, None, :]
    decay = jnp.where(same[None], jnp.exp(jnp.where(same[None], diff, 0.0)), 0.0)
    inner_prod = jnp.dot(cmatrix, bmatrix.T, precision=highest, preferred_element_type=jnp.float32)
    mixing = decay * inner_prod[None] * steps.T[:, None, :]
    within = jnp.einsum("hts,shp->thp", mixing, inner_vals, precision=highest)
    carry = jnp.exp(logs) * (first < positions[0]).astype(jnp.float32)[:, None]
    remote = jnp.einsum("tn,hpn->thp", cmatrix, incoming, precision=highest) * carry[:, :, None]
    result = within + remote + skip_gain[None, :, None] * inner_vals
    return result.reshape(count, -1)


def gather_parts(values):
    return lax.all_gather(values, "tp", axis=1, tiled=True)


def reduce_parts(values):
    return lax.psum_scatter(values, "tp", scatter_dimension=1, tiled=True)


def row_totals(values):
    return lax.psum(values, "tp")


def product(left, right, form):
    return jnp.einsum(form, left, right, preferred_element_type=jnp.float32)


def forward_chain(earlier, later):
    return (earlier[0] * later[0], later[0][:, None, None] * earlier[1] + later[1])


def backward_chain(earlier, later):
    return (earlier[0] * later[0], later[1] + later[0][:, None, None] * earlier[1])


def norm_backward(grad, values, gain):
    scale = lax.rsqrt(jnp.mean(values * values, axis=-1, keepdims=True) + epsilon)
    normed = values * scale
    scaled = grad * gain[None, :]
    result = scale * (scaled - normed * jnp.mean(scaled * normed, axis=-1, keepdims=True))
    return (result, jnp.sum(grad * normed, axis=0))


def shards(
    patches,
    byte_embed,
    seq_lengths,
    norm_global,
    proj_gate,
    proj_inner,
    proj_state,
    proj_step,
    step_bias,
    decay_log,
    conv_inner,
    conv_state,
    skip_gain,
    mixer_gain,
    proj_mixer,
    norm_attn,
    attn_input,
    attn_output,
    norm_ffn,
    expand_weight,
    shrink_weight,
    grad_output,
):
    count = patches.shape[0]
    quarter = patches.shape[1]
    tail = CONV - 1
    inner_width = proj_inner.shape[1]
    positions = lax.axis_index("seq") * count + jnp.arange(count, dtype=jnp.int32)
    first = sequence_first(positions, seq_lengths)
    global_in = gather_parts(patches).astype(jnp.float32)
    normed = (rms_scale(global_in) * norm_global[None, :]).astype(jnp.bfloat16)
    gate_vals = product(normed, proj_gate, "rd,dc->rc")
    inner_raw = product(normed, proj_inner, "rd,dc->rc")
    state_raw = product(normed, proj_state, "rd,dc->rc")
    step_raw = product(normed, proj_step, "rd,dc->rc")
    raw = jnp.concatenate([inner_raw, state_raw], axis=1)
    before = shifted(raw[count - tail :], "seq", 1)
    padded = jnp.concatenate([before, raw], axis=0)
    conv_weight = jnp.concatenate([conv_inner, conv_state], axis=1)

    def front_local(padded_in, step_in, conv_in, bias_in, decay_in):
        return front_part(padded_in, step_in, conv_in, bias_in, decay_in, positions, first)

    def summary_local(inner_in, bmat_in, steps_in, rates_in):
        return block_summary(inner_in, bmat_in, steps_in, rates_in, positions, first)

    def output_local(inner_in, bmat_in, cmat_in, steps_in, rates_in, skip_in, incoming_in):
        return block_output(
            inner_in, bmat_in, cmat_in, steps_in, rates_in, skip_in, incoming_in, positions, first
        )

    front_vals, front_pull = jax.vjp(
        front_local, padded, step_raw, conv_weight, step_bias, decay_log
    )
    inner_vals, bmatrix, cmatrix, steps, rates = front_vals
    summary, summary_pull = jax.vjp(summary_local, inner_vals, bmatrix, steps, rates)
    carried, states = summary
    prefix = entering(
        (carried, states),
        "seq",
        forward_chain,
        (jnp.ones_like(carried), jnp.zeros_like(states)),
        False,
    )
    incoming = prefix[1]
    mixed, output_pull = jax.vjp(
        output_local, inner_vals, bmatrix, cmatrix, steps, rates, skip_gain, incoming
    )
    gate_act = jax.nn.silu(gate_vals)
    gated = mixed * gate_act
    row_scale = lax.rsqrt(row_totals(jnp.sum(gated * gated, axis=1)) / DI + epsilon)[:, None]
    normed_mix = gated * row_scale
    mix_low = (normed_mix * mixer_gain[None, :]).astype(jnp.bfloat16)
    global_out = patches.astype(jnp.float32) + reduce_parts(
        product(mix_low, proj_mixer, "rc,cd->rd")
    )
    rows_in = byte_embed.astype(jnp.float32) + jnp.broadcast_to(
        global_out[:, None, :], (count, PATCH, quarter)
    ).reshape(-1, quarter)
    total_rows = rows_in.shape[0]
    attn_in = gather_parts(rows_in.astype(jnp.bfloat16)).astype(jnp.float32)
    attn_normed = (rms_scale(attn_in) * norm_attn[None, :]).astype(jnp.bfloat16)
    qkv_vals = product(attn_normed, attn_input, "rd,kde->kre").astype(jnp.bfloat16)
    head_size = D // HEADS_A
    shape_four = (total_rows // PATCH, PATCH, quarter // head_size, head_size)
    query = qkv_vals[0].reshape(shape_four)
    keys = qkv_vals[1].reshape(shape_four)
    values = qkv_vals[2].reshape(shape_four)
    scaling = head_size ** (-0.5)
    scores = product(query, keys, "bqhd,bkhd->bhqk") * scaling
    causal = jnp.arange(PATCH)[:, None] >= jnp.arange(PATCH)[None, :]
    masked = jnp.where(causal, scores, -1e30)
    expo = jnp.exp(masked - jnp.max(masked, axis=-1, keepdims=True))
    probs = expo / jnp.sum(expo, axis=-1, keepdims=True)
    probs_low = probs.astype(jnp.bfloat16)
    context = (
        product(probs_low, values, "bhqk,bkhd->bqhd")
        .astype(jnp.bfloat16)
        .reshape(total_rows, quarter)
    )
    hidden_in = rows_in + reduce_parts(product(context, attn_output, "re,ed->rd"))
    ffn_in = gather_parts(hidden_in.astype(jnp.bfloat16)).astype(jnp.float32)
    ffn_normed = (rms_scale(ffn_in) * norm_ffn[None, :]).astype(jnp.bfloat16)
    gate_ffn = product(ffn_normed, expand_weight[0], "rd,df->rf")
    up_ffn = product(ffn_normed, expand_weight[1], "rd,df->rf")
    sigma = jax.nn.sigmoid(gate_ffn)
    activ = (gate_ffn * sigma * up_ffn).astype(jnp.bfloat16)
    layer_output = (hidden_in + reduce_parts(product(activ, shrink_weight, "rf,fd->rd"))).astype(
        jnp.bfloat16
    )
    down_in = gather_parts(grad_output)
    shrink_grad = product(activ, down_in, "rf,rd->fd")
    activ_grad = product(down_in, shrink_weight, "rd,fd->rf")
    gate_low = (activ_grad * up_ffn * sigma * (1.0 + gate_ffn * (1.0 - sigma))).astype(jnp.bfloat16)
    up_low = (activ_grad * gate_ffn * sigma).astype(jnp.bfloat16)
    expand_grad = jnp.stack(
        [product(ffn_normed, gate_low, "rd,rf->df"), product(ffn_normed, up_low, "rd,rf->df")]
    )
    ffn_normed_grad = product(gate_low, expand_weight[0], "rf,df->rd") + product(
        up_low, expand_weight[1], "rf,df->rd"
    )
    ffn_in_grad, norm_ffn_part = norm_backward(ffn_normed_grad, ffn_in, norm_ffn)
    hidden_grad = grad_output.astype(jnp.float32) + reduce_parts(ffn_in_grad)
    attn_back_in = gather_parts(hidden_grad.astype(jnp.bfloat16))
    attn_output_grad = product(context, attn_back_in, "re,rd->ed")
    context_grad = (
        product(attn_back_in, attn_output, "rd,ed->re").astype(jnp.bfloat16).reshape(shape_four)
    )
    probs_grad = product(context_grad, values, "bqhd,bkhd->bhqk")
    values_grad = product(probs_low, context_grad, "bhqk,bqhd->bkhd")
    scores_grad = (
        probs * (probs_grad - jnp.sum(probs_grad * probs, axis=-1, keepdims=True))
    ).astype(jnp.bfloat16)
    query_grad = product(scores_grad, keys, "bhqk,bkhd->bqhd") * scaling
    keys_grad = product(scores_grad, query, "bhqk,bqhd->bkhd") * scaling
    qkv_grad = (
        jnp.stack([query_grad, keys_grad, values_grad])
        .reshape(3, total_rows, quarter)
        .astype(jnp.bfloat16)
    )
    attn_input_grad = product(attn_normed, qkv_grad, "rd,kre->kde")
    attn_normed_grad = product(qkv_grad, attn_input, "kre,kde->rd")
    attn_in_grad, norm_attn_part = norm_backward(attn_normed_grad, attn_in, norm_attn)
    embed_grad = hidden_grad + reduce_parts(attn_in_grad)
    global_grad = embed_grad.reshape(count, PATCH, quarter).sum(axis=1)
    mix_back_in = gather_parts(global_grad.astype(jnp.bfloat16))
    proj_mixer_grad = product(mix_low, mix_back_in, "rc,rd->cd")
    mix_low_grad = product(mix_back_in, proj_mixer, "rd,cd->rc")
    mixer_gain_grad = jnp.sum(mix_low_grad * normed_mix, axis=0)
    scaled_grad = mix_low_grad * mixer_gain[None, :]
    row_dot = row_totals(jnp.sum(scaled_grad * normed_mix, axis=1))[:, None] / DI
    gated_grad = row_scale * (scaled_grad - normed_mix * row_dot)
    mixed_grad = gated_grad * gate_act
    sigma_gate = jax.nn.sigmoid(gate_vals)
    gate_vals_grad = gated_grad * mixed * sigma_gate * (1.0 + gate_vals * (1.0 - sigma_gate))
    inner_one, bmat_one, cmat_one, steps_one, rates_one, skip_gain_grad, incoming_grad = (
        output_pull(mixed_grad)
    )
    later = entering(
        (carried, incoming_grad),
        "seq",
        backward_chain,
        (jnp.ones_like(carried), jnp.zeros_like(incoming_grad)),
        True,
    )
    later_grad = later[1]
    carried_grad = jnp.sum(later_grad * incoming, axis=(1, 2))
    inner_two, bmat_two, steps_two, rates_two = summary_pull((carried_grad, later_grad))
    padded_grad, step_raw_grad, conv_grad, step_bias_grad, decay_log_grad = front_pull(
        (
            inner_one + inner_two,
            bmat_one + bmat_two,
            cmat_one,
            steps_one + steps_two,
            rates_one + rates_two,
        )
    )
    tail_grad = shifted(padded_grad[:tail], "seq", -1)
    raw_grad = padded_grad[tail:]
    raw_grad = jnp.concatenate(
        [raw_grad[: count - tail], raw_grad[count - tail :] + tail_grad], axis=0
    )
    gate_back = gate_vals_grad.astype(jnp.bfloat16)
    inner_back = raw_grad[:, :inner_width].astype(jnp.bfloat16)
    step_back = step_raw_grad.astype(jnp.bfloat16)
    normed_grad_part = (
        product(gate_back, proj_gate, "rc,dc->rd")
        + product(inner_back, proj_inner, "rc,dc->rd")
        + product(step_back, proj_step, "rc,dc->rd")
    )
    part_in_grad, norm_global_part = norm_backward(normed_grad_part, global_in, norm_global)
    state_sum, conv_state_grad, norm_attn_grad, norm_ffn_grad, norm_global_total = lax.psum(
        (
            raw_grad[:, inner_width:],
            conv_grad[:, inner_width:],
            norm_attn_part,
            norm_ffn_part,
            norm_global_part,
        ),
        "tp",
    )
    state_back = state_sum.astype(jnp.bfloat16)
    shared_in_grad, norm_global_shared = norm_backward(
        product(state_back, proj_state, "rs,ds->rd"), global_in, norm_global
    )
    own_columns = lax.dynamic_slice_in_dim(
        shared_in_grad, lax.axis_index("tp") * quarter, quarter, 1
    )
    patch_grad = global_grad + reduce_parts(part_in_grad) + own_columns
    norm_global_grad = norm_global_total + norm_global_shared
    proj_gate_grad = product(normed, gate_back, "rd,rc->dc")
    proj_inner_grad = product(normed, inner_back, "rd,rc->dc")
    proj_state_grad = product(normed, state_back, "rd,rc->dc")
    proj_step_grad = product(normed, step_back, "rd,rc->dc")
    conv_inner_grad = conv_grad[:, :inner_width]
    (
        norm_global_grad,
        proj_gate_grad,
        proj_inner_grad,
        proj_state_grad,
        proj_step_grad,
        step_bias_grad,
        decay_log_grad,
        conv_inner_grad,
        conv_state_grad,
        skip_gain_grad,
        mixer_gain_grad,
        proj_mixer_grad,
        norm_attn_grad,
        attn_input_grad,
        attn_output_grad,
        norm_ffn_grad,
        expand_grad,
        shrink_grad,
    ) = lax.psum(
        (
            norm_global_grad,
            proj_gate_grad,
            proj_inner_grad,
            proj_state_grad,
            proj_step_grad,
            step_bias_grad,
            decay_log_grad,
            conv_inner_grad,
            conv_state_grad,
            skip_gain_grad,
            mixer_gain_grad,
            proj_mixer_grad,
            norm_attn_grad,
            attn_input_grad,
            attn_output_grad,
            norm_ffn_grad,
            expand_grad,
            shrink_grad,
        ),
        "seq",
    )
    return (
        layer_output,
        embed_grad,
        patch_grad,
        norm_global_grad,
        proj_gate_grad,
        proj_inner_grad,
        proj_state_grad,
        proj_step_grad,
        step_bias_grad,
        decay_log_grad,
        conv_inner_grad,
        conv_state_grad,
        skip_gain_grad,
        mixer_gain_grad,
        proj_mixer_grad,
        norm_attn_grad,
        attn_input_grad,
        attn_output_grad,
        norm_ffn_grad,
        expand_grad,
        shrink_grad,
    )


def solution(mesh):
    placed = (
        P("seq", "tp"),
        P("seq", "tp"),
        P(),
        P(),
        P(None, "tp"),
        P(None, "tp"),
        P(),
        P(None, "tp"),
        P("tp"),
        P("tp"),
        P(None, "tp"),
        P(),
        P("tp"),
        P("tp"),
        P("tp", None),
        P(),
        P(None, None, "tp"),
        P("tp", None),
        P(),
        P(None, None, "tp"),
        P("tp", None),
        P("seq", "tp"),
    )
    return jax.shard_map(
        shards,
        mesh=mesh,
        in_specs=placed,
        out_specs=(
            P("seq", "tp"),
            P("seq", "tp"),
            P("seq", "tp"),
            P(),
            P(None, "tp"),
            P(None, "tp"),
            P(),
            P(None, "tp"),
            P("tp"),
            P("tp"),
            P(None, "tp"),
            P(),
            P("tp"),
            P("tp"),
            P("tp", None),
            P(),
            P(None, None, "tp"),
            P("tp", None),
            P(),
            P(None, None, "tp"),
            P("tp", None),
        ),
        check_vma=False,
    )
```

profile of v0, /device:TPU:0, one launch (start us, length us, event | category | flops | bytes accessed | tf_op | source)
XLA Modules:
  0.0 1633.5 jit_solution(15725093108737520940)
XLA Ops:
  7.3 17.7 %all_gather.36 = bf16[256,1024]{1,0:T(8,128)(2,1)S(1)} all-gather(bf16[256,256]{1,0:T(8,128)(2,1)} %param.26), channel_id=1, replica_groups=mesh['seq'=8,'tp'=4] {'tp'}, dimensions={1}, use_global_device_ids=true | all-gather | bytes 655360 | tf_op jit(solution)/shard_map/all_gather | solution.py:99
  45.8 9.4 all-gather.2
  56.5 20.0 %all-gather.18.cloned.1.call-done = f32[64,64,128]{2,1,0:T(8,128)} async-done(((f32[8,64,128]{2,1,0:T(8,128)}), f32[64,64,128]{2,1,0:T(8,128)}) %all-gather.18.cloned.1.call-update) | async-done | bytes 2097168 | tf_op jit(solution)/shard_map/all_gather | solution.py:29
  78.3 4.5 fusion.87
  87.0 11.8 psum.175
  101.8 31.1 %reduce-scatter.7.cloned.1.call-done = f32[256,256]{1,0:T(8,128)} async-done(((f32[256,1024]{1,0:T(8,128)}), f32[256,256]{1,0:T(8,128)}) %reduce-scatter.7.cloned.1.call-update) | async-done | bytes 262160 | tf_op jit(solution)/shard_map/reduce_scatter | solution.py:103
  135.2 79.3 %all-gather.10.cloned.1.call-done = bf16[2048,1024]{1,0:T(8,128)(2,1)} async-done(((bf16[2048,256]{1,0:T(8,128)(2,1)}), bf16[2048,1024]{1,0:T(8,128)(2,1)}) %all-gather.10.cloned.1.call-update) | async-done | bytes 4194320 | tf_op jit(solution)/shard_map/all_gather | solution.py:99
  218.0 5.4 fusion.23
  225.1 4.4 reshape_squeeze.9
  229.5 4.4 reshape_squeeze.11
  233.9 4.4 reshape_squeeze.10
  241.8 15.7 fusion.209
  262.0 4.3 reshape.381
  266.4 6.0 fusion.212
  272.4 142.8 %reduce-scatter.9.cloned.1.call-done = f32[2048,256]{1,0:T(8,128)} async-done(((f32[2048,1024]{1,0:T(8,128)}), f32[2048,256]{1,0:T(8,128)}) %reduce-scatter.9.cloned.1.call-update) | async-done | bytes 2097168 | tf_op jit(solution)/shard_map/reduce_scatter | solution.py:103
  419.2 80.4 %all-gather.12.cloned.1.call-done = bf16[2048,1024]{1,0:T(8,128)(2,1)} async-done(((bf16[2048,256]{1,0:T(8,128)(2,1)}), bf16[2048,1024]{1,0:T(8,128)(2,1)}) %all-gather.12.cloned.1.call-update) | async-done | bytes 4194320 | tf_op jit(solution)/shard_map/all_gather | solution.py:99
  503.0 8.6 fusion.32
  511.6 6.8 fusion.28
  518.4 61.4 %all-gather.14.cloned.1.call-done = bf16[2048,1024]{1,0:T(8,128)(2,1)} async-done(((bf16[2048,256]{1,0:T(8,128)(2,1)}), bf16[2048,1024]{1,0:T(8,128)(2,1)}) %all-gather.14.cloned.1.call-update) | async-done | bytes 4194320 | tf_op jit(solution)/shard_map/all_gather | solution.py:99
  579.8 15.4 multiply_convert_fusion
  595.2 7.1 fusion.30
  602.3 9.8 fusion.19
  612.1 4.3 fusion.18
  616.5 142.8 %reduce-scatter.13.cloned.1.call-done = f32[2048,256]{1,0:T(8,128)} async-done(((f32[2048,1024]{1,0:T(8,128)}), f32[2048,256]{1,0:T(8,128)}) %reduce-scatter.13.cloned.1.call-update) | async-done | bytes 2097168 | tf_op jit(solution)/shard_map/reduce_scatter | solution.py:103
  762.1 81.4 %all-gather.16.cloned.1.call-done = bf16[2048,1024]{1,0:T(8,128)(2,1)} async-done(((bf16[2048,256]{1,0:T(8,128)(2,1)}), bf16[2048,1024]{1,0:T(8,128)(2,1)}) %all-gather.16.cloned.1.call-update) | async-done | bytes 4194320 | tf_op jit(solution)/shard_map/all_gather | solution.py:99
  848.9 6.1 multiply_reduce_fusion
  882.1 4.3 stack.23
  889.8 8.6 fusion.13
  898.4 4.3 fusion.12
  902.8 142.7 %reduce-scatter.15.cloned.1.call-done = f32[2048,256]{1,0:T(8,128)} async-done(((f32[2048,1024]{1,0:T(8,128)}), f32[2048,256]{1,0:T(8,128)}) %reduce-scatter.15.cloned.1.call-update) | async-done | bytes 2097168 | tf_op jit(solution)/shard_map/reduce_scatter | solution.py:103
  1045.5 4.2 bitcast_reduce_fusion
  1049.8 16.4 %all_gather.44 = bf16[256,1024]{1,0:T(8,128)(2,1)S(1)} all-gather(bf16[256,256]{1,0:T(8,128)(2,1)S(1)} %convert_element_type.162), channel_id=1, replica_groups=mesh['seq'=8,'tp'=4] {'tp'}, dimensions={1}, use_global_device_ids=true | all-gather | bytes 655360 | tf_op jit(solution)/shard_map/all_gather | solution.py:99
  1069.9 10.7 psum.176
  1088.6 8.9 fusion.213
  1097.7 8.2 convolution_bitcast_fusion
  1105.9 5.0 convolution_bitcast_fusion.1
  1110.9 5.1 pad_maximum_fusion
  1117.4 6.1 fusion.216
  1123.7 4.2 fusion.97
  1138.1 12.4 while.27
  1176.2 31.6 %all-reduce.19 = bf16[256,256]{1,0:T(8,128)(2,1)S(1)} all-reduce(f32[256,256]{1,0:T(8,128)} %pad_maximum_fusion.2), channel_id=1, replica_groups=mesh['seq'=8,'tp'=4] {'tp'}, use_global_device_ids=true, to_apply=%region_39.40 | all-reduce | flops 65536 | bytes 393216 | tf_op jit(solution)/shard_map/psum | solution.py:322
  1215.0 4.9 fusion.215
  1220.0 5.3 fusion.46
  1232.6 37.8 %reduce-scatter.11.cloned.1.call-done = f32[2048,256]{1,0:T(8,128)} async-done(((f32[2048,1024]{1,0:T(8,128)}), f32[2048,256]{1,0:T(8,128)}) %reduce-scatter.11.cloned.1.call-update) | async-done | bytes 2097168 | tf_op jit(solution)/shard_map/reduce_scatter | solution.py:103
  1275.0 18.5 %all-reduce.14 = (f32[1024]{0:T(1024)S(1)}, f32[4,256]{1,0:T(4,128)S(1)}, f32[1024]{0:T(1024)S(1)}, f32[1024]{0:T(1024)S(1)}) all-reduce(f32[1024]{0:T(1024)S(1)} %copy-done.127, f32[4,256]{1,0:T(4,128)S(1)} %pad_add_fusion.3, f32[1024]{0:T(1024)S(1)} %copy-done.126, f32[1024]{0:T(1024)S(1)} %copy-done.125), channel_id=1, replica_groups=mesh['seq'=8,'tp'=4] {'tp'}, use_global_device_ids=true, to_apply=%region_42.43 | all-reduce | flops 4096 | bytes 32768 | tf_op jit(solution)/shard_map/psum | solution.py:322
  1293.6 23.8 %all-reduce.12 = (f32[1024]{0:T(1024)}, f32[1024,8]{0,1:T(8,128)}, f32[8]{0:T(128)}, f32[8]{0:T(128)}, f32[4,512]{1,0:T(4,128)}, /*index=5*/f32[4,256]{1,0:T(4,1...) all-reduce(f32[1024]{0:T(1024)S(1)} %add.343, ...), channel_id=1, replica_groups=mesh['seq'=8,'tp'=4] {'seq'}, use_global_device_ids=true, to_apply=%region_44.45 | all-reduce | flops 14872 | bytes 118976 | tf_op jit(solution)/shard_map/psum | solution.py:365
  1319.4 287.7 %all-reduce.18.cloned.1.call-done = (f32[1024,512]{1,0:T(8,128)}, f32[1024,512]{1,0:T(8,128)}, f32[1024,256]{1,0:T(8,128)}, f32[512,1024]{1,0:T(8,128)}, f32[3,1...) async-done(((f32[1024,512]{1,0:T(8,128)}, f32[1024,512]{1,0:T(8,128)}, f32[1024,256]{1,0:T(8,128)}, ...) | async-done | bytes 24117264 | tf_op jit(solution)/shard_map/psum | solution.py:365
  1619.3 4.3 copy.209
  (485 shorter events, 187.7 us)
Async XLA Ops:
  7.2 572.6 %copy-start = (bf16[1024,1024]{1,0:T(8,128)(2,1)S(1)}, bf16[1024,1024]{1,0:T(8,128)(2,1)}, u32[]{:S(2)}) copy-start(bf16[1024,1024]{1,0:T(8,128)(2,1)} %param.46) | copy-start | bytes 6291460
  7.3 69.2 %all-gather.18.cloned.1.call-start = ((), (), s32[]{:S(2)}) async-start(), calls=%async_computation.16 | async-start | bytes 2359296 | tf_op jit(solution)/shard_map/all_gather | solution.py:29
  25.0 59.0 %copy-start.7 = (bf16[256,1024]{1,0:T(8,128)(2,1)}, bf16[256,1024]{1,0:T(8,128)(2,1)S(1)}, u32[]{:S(2)}) copy-start(bf16[256,1024]{1,0:T(8,128)(2,1)S(1)} %all_gather.36) | copy-start | bytes 1572868
  25.2 58.8 %copy-start.70 = (f32[256]{0:T(256)}, f32[256]{0:T(256)S(1)}, u32[]{:S(2)}) copy-start(f32[256]{0:T(256)S(1)} %add_rsqrt_fusion.3) | copy-start | bytes 3076
  28.5 8.1 collective-permute-start
  35.8 42.5 %copy-start.64 = (f32[256,8]{0,1:T(8,128)}, f32[256,8]{0,1:T(8,128)S(1)}, u32[]{:S(2)}) copy-start(f32[256,8]{0,1:T(8,128)S(1)} %get-tuple-element.317) | copy-start | bytes 24580
  45.7 87.2 %reduce-scatter.7.cloned.1.call-start = ((), (), s32[]{:S(2)}) async-start(), calls=%async_computation.6 | async-start | bytes 1310720 | tf_op jit(solution)/shard_map/reduce_scatter | solution.py:103
  84.0 48.9 %copy-start.55 = (bf16[256,256]{1,0:T(8,128)(2,1)S(1)}, bf16[256,256]{1,0:T(8,128)(2,1)}, u32[]{:S(2)}) copy-start(bf16[256,256]{1,0:T(8,128)(2,1)} %param.26) | copy-start | bytes 393220
  87.0 46.9 %copy-start.24 = (bf16[2048,256]{1,0:T(8,128)(2,1)S(1)}, bf16[2048,256]{1,0:T(8,128)(2,1)}, u32[]{:S(2)}) copy-start(bf16[2048,256]{1,0:T(8,128)(2,1)} %param.27) | copy-start | bytes 3145732
  98.9 118.9 %copy-start.89 = (f32[256]{0:T(256)}, f32[256]{0:T(256)S(1)}, u32[]{:S(2)}) copy-start(f32[256]{0:T(256)S(1)} %add_rsqrt_fusion.2) | copy-start | bytes 3076
  101.8 116.0 %copy-start.119 = (f32[1024]{0:T(1024)S(1)}, f32[1024]{0:T(1024)}, u32[]{:S(2)}) copy-start(f32[1024]{0:T(1024)} %param.41) | copy-start | bytes 12292
  101.8 112.7 %all-gather.10.cloned.1.call-start = ((), (), s32[]{:S(2)}) async-start(), calls=%async_computation.7 | async-start | bytes 5242880 | tf_op jit(solution)/shard_map/all_gather | solution.py:99
  133.9 281.3 %copy-start.33 = (f32[256,256]{1,0:T(8,128)}, f32[256,256]{1,0:T(8,128)S(1)}, u32[]{:S(2)}) copy-start(f32[256,256]{1,0:T(8,128)S(1)} %convert_add_fusion.1) | copy-start | bytes 786436
  135.1 280.1 %reduce-scatter.9.cloned.1.call-start = ((), (), s32[]{:S(2)}) async-start(), calls=%async_computation.8 | async-start | bytes 10485760 | tf_op jit(solution)/shard_map/reduce_scatter | solution.py:103
  218.0 680.4 %copy-start.82 = (f32[2048]{0:T(1024)}, f32[2048]{0:T(1024)S(1)}, u32[]{:S(2)}) copy-start(f32[2048]{0:T(1024)S(1)} %add_rsqrt_fusion.1) | copy-start | bytes 24580
  272.4 227.1 %all-gather.12.cloned.1.call-start = ((), (), s32[]{:S(2)}) async-start(), calls=%async_computation.9 | async-start | bytes 5242880 | tf_op jit(solution)/shard_map/all_gather | solution.py:99
  418.1 84.7 %copy-start.118 = (f32[1024]{0:T(1024)S(1)}, f32[1024]{0:T(1024)}, u32[]{:S(2)}) copy-start(f32[1024]{0:T(1024)} %param.44) | copy-start | bytes 12292
  418.1 161.7 %all-gather.14.cloned.1.call-start = ((), (), s32[]{:S(2)}) async-start(), calls=%async_computation.11 | async-start | bytes 5242880 | tf_op jit(solution)/shard_map/all_gather | solution.py:99
  418.7 340.6 %reduce-scatter.13.cloned.1.call-start = ((), (), s32[]{:S(2)}) async-start(), calls=%async_computation.12 | async-start | bytes 10485760 | tf_op jit(solution)/shard_map/reduce_scatter | solution.py:103
  616.4 142.8 %copy-start.25 = (bf16[2048,256]{1,0:T(8,128)(2,1)S(1)}, bf16[2048,256]{1,0:T(8,128)(2,1)}, u32[]{:S(2)}) copy-start(bf16[2048,256]{1,0:T(8,128)(2,1)} %param.47) | copy-start | bytes 3145732
  616.4 227.1 %all-gather.16.cloned.1.call-start = ((), (), s32[]{:S(2)}) async-start(), calls=%async_computation.13 | async-start | bytes 5242880 | tf_op jit(solution)/shard_map/all_gather | solution.py:99
  762.0 283.5 %reduce-scatter.15.cloned.1.call-start = ((), (), s32[]{:S(2)}) async-start(), calls=%async_computation.14 | async-start | bytes 10485760 | tf_op jit(solution)/shard_map/reduce_scatter | solution.py:103
  902.7 164.3 %copy-start.87 = (f32[512]{0:T(512)S(1)}, f32[512]{0:T(512)}, u32[]{:S(2)}) copy-start(f32[512]{0:T(512)} %param.39) | copy-start | bytes 6148
  902.8 164.3 %copy-start.90 = (f32[256]{0:T(256)S(1)}, f32[256]{0:T(256)}, u32[]{:S(2)}) copy-start(f32[256]{0:T(256)} %copy-done.89) | copy-start | bytes 3076
  902.8 177.9 %copy-start.23 = (f32[256,768]{1,0:T(8,128)S(1)}, f32[256,768]{1,0:T(8,128)}, u32[]{:S(2)}) copy-start(f32[256,768]{1,0:T(8,128)} %copy-done.22) | copy-start | bytes 2359300
  902.8 235.3 %all-gather.20.cloned.1.call-start = ((), (), s32[]{:S(2)}) async-start(), calls=%async_computation.17 | async-start | bytes 2359296 | tf_op jit(solution)/shard_map/all_gather | solution.py:29
  1083.9 51.5 %copy-start.40 = (bf16[256,512]{1,0:T(8,128)(2,1)}, bf16[256,512]{1,0:T(8,128)(2,1)S(1)}, u32[]{:S(2)}) copy-start(bf16[256,512]{1,0:T(8,128)(2,1)S(1)} %get-tuple-element.327) | copy-start | bytes 786436
  1088.4 182.0 %reduce-scatter.11.cloned.1.call-start = ((), (), s32[]{:S(2)}) async-start(), calls=%async_computation.10 | async-start | bytes 10485760 | tf_op jit(solution)/shard_map/reduce_scatter | solution.py:103
  1097.6 219.8 %reduce-scatter.17.cloned.1.call-start = ((), (), s32[]{:S(2)}) async-start(), calls=%async_computation.15 | async-start | bytes 1310720 | tf_op jit(solution)/shard_map/reduce_scatter | solution.py:103
  1166.6 8.0 collective-permute-start.1
  1214.9 392.2 %all-reduce.18.cloned.1.call-start = ((), (), s32[]{:S(2)}) async-start(), calls=%async_computation.18 | async-start | bytes 48234496 | tf_op jit(solution)/shard_map/psum | solution.py:365
  1232.4 42.1 %copy-start.97 = (f32[768]{0:T(1024)S(1)}, f32[768]{0:T(1024)}, u32[]{:S(2)}) copy-start(f32[768]{0:T(1024)} %get-tuple-element.245) | copy-start | bytes 9220
  1232.4 42.1 %copy-start.96 = (f32[768]{0:T(1024)S(1)}, f32[768]{0:T(1024)}, u32[]{:S(2)}) copy-start(f32[768]{0:T(1024)} %get-tuple-element.244) | copy-start | bytes 9220
  1232.4 42.1 %copy-start.95 = (f32[768]{0:T(1024)S(1)}, f32[768]{0:T(1024)}, u32[]{:S(2)}) copy-start(f32[768]{0:T(1024)} %get-tuple-element.243) | copy-start | bytes 9220
  1232.4 42.1 %copy-start.94 = (f32[768]{0:T(1024)S(1)}, f32[768]{0:T(1024)}, u32[]{:S(2)}) copy-start(f32[768]{0:T(1024)} %get-tuple-element.250) | copy-start | bytes 9220
  1232.4 42.2 %copy-start.131 = (f32[8]{0:T(128)S(1)}, f32[8]{0:T(128)}, u32[]{:S(2)}) copy-start(f32[8]{0:T(128)} %get-tuple-element.259) | copy-start | bytes 100
  1232.4 42.2 %copy-start.132 = (f32[8]{0:T(128)S(1)}, f32[8]{0:T(128)}, u32[]{:S(2)}) copy-start(f32[8]{0:T(128)} %get-tuple-element.260) | copy-start | bytes 100
  1232.5 42.2 %copy-start.135 = (f32[8]{0:T(128)S(1)}, f32[8]{0:T(128)}, u32[]{:S(2)}) copy-start(f32[8]{0:T(128)} %param.35) | copy-start | bytes 100
  1232.5 42.2 %copy-start.73 = (f32[256]{0:T(256)S(1)}, f32[256]{0:T(256)}, u32[]{:S(2)}) copy-start(f32[256]{0:T(256)} %copy-done.70) | copy-start | bytes 3076
  1232.5 42.2 %copy-start.93 = (bf16[256,8]{0,1:T(8,128)(2,1)S(1)}, bf16[256,8]{0,1:T(8,128)(2,1)}, u32[]{:S(2)}) copy-start(bf16[256,8]{0,1:T(8,128)(2,1)} %get-tuple-element.335) | copy-start | bytes 12292
  1232.5 42.5 %copy-start.125 = (f32[1024]{0:T(1024)S(1)}, f32[1024]{0:T(1024)}, u32[]{:S(2)}) copy-start(f32[1024]{0:T(1024)} %get-tuple-element.235) | copy-start | bytes 12292
  1232.5 42.5 %copy-start.126 = (f32[1024]{0:T(1024)S(1)}, f32[1024]{0:T(1024)}, u32[]{:S(2)}) copy-start(f32[1024]{0:T(1024)} %get-tuple-element.237) | copy-start | bytes 12292
  1232.5 42.5 %copy-start.127 = (f32[1024]{0:T(1024)S(1)}, f32[1024]{0:T(1024)}, u32[]{:S(2)}) copy-start(f32[1024]{0:T(1024)} %get-tuple-element.254) | copy-start | bytes 12292
  1232.5 61.0 %copy-start.122 = (f32[1024]{0:T(1024)S(1)}, f32[1024]{0:T(1024)}, u32[]{:S(2)}) copy-start(f32[1024]{0:T(1024)} %get-tuple-element.251) | copy-start | bytes 12292
  1232.5 61.0 %copy-start.117 = (f32[512]{0:T(512)S(1)}, f32[512]{0:T(512)}, u32[]{:S(2)}) copy-start(f32[512]{0:T(512)} %get-tuple-element.248) | copy-start | bytes 6148
  1232.6 61.0 %copy-start.128 = (f32[8]{0:T(128)S(1)}, f32[8]{0:T(128)}, u32[]{:S(2)}) copy-start(f32[8]{0:T(128)} %get-tuple-element.334) | copy-start | bytes 100
  1232.6 84.8 %copy-start.133 = (f32[256]{0:T(256)S(1)}, f32[256]{0:T(256)}, u32[]{:S(2)}) copy-start(f32[256]{0:T(256)} %get-tuple-element.252) | copy-start | bytes 3076
  1232.6 84.8 %copy-start.43 = (f32[256,256]{1,0:T(8,128)S(1)}, f32[256,256]{1,0:T(8,128)}, u32[]{:S(2)}) copy-start(f32[256,256]{1,0:T(8,128)} %copy-done.42) | copy-start | bytes 786436
  (116 other events, 1170.4 us)
Sparse Core Ops, SparseCore 0:
  45.9 30.5 all-gather.17
  101.9 30.9 reduce-scatter.6
  135.3 79.2 all-gather.9
  272.5 142.6 reduce-scatter.8
  418.2 81.2 all-gather.11
  501.0 78.7 all-gather.13
  616.5 142.6 reduce-scatter.12
  762.2 81.2 all-gather.15
  902.9 142.6 reduce-scatter.14
  1088.5 25.9 all-gather.19
  1117.6 152.7 reduce-scatter.10
  1272.7 28.1 reduce-scatter.16
  1307.6 299.4 all-reduce.17
where the time goes:
time: 1640 us; the launch traced here: 1630 us
  waiting for transfers between devices  1110 us (68%)
  matrix products  185 us (11%)
  blocking collectives  140 us (9%)
  local copies, waits for them, and re-layouts  91.5 us (6%)
  other arithmetic  87.6 us (5%)
  between operations  17.6 us (1%)
    reduce_scatter x6, waiting for transfers between devices, reduce_parts(): return lax.psum_scatter(values, 'tp', scatter_dimension=1, tiled=True)  497 us
    all_gather x4, waiting for transfers between devices, gather_parts(): return lax.all_gather(values, 'tp', axis=1, tiled=True)  302 us
    psum x1, waiting for transfers between devices, shards(): lax.psum((norm_global_grad, proj_gate_grad, proj_inner_grad, proj_state_g...  288 us
    dot_general x36, matrix products, product(): return jnp.einsum(form, left, right, preferred_element_type=jnp.float32)  155 us
    psum x2, blocking collectives, shards(): lax.psum((raw_grad[:, inner_width:], conv_grad[:, inner_width:], norm_att...  50.1 us
    all_gather x2, blocking collectives, gather_parts(): return lax.all_gather(values, 'tp', axis=1, tiled=True)  34.1 us
  transfers between devices with their start and end apart: 15, of which 11 were waited for; matrix products, arithmetic and copies ran while one was open for 8% of the time, Pallas kernels for 0%

commit v1 on v0

v1 whole, which is shorter than its diff:
```python
import functools

import jax
import jax.numpy as jnp
from jax import lax
from jax.experimental import pallas as pl
from jax.experimental.pallas import tpu as pltpu
from jax.sharding import Mesh, PartitionSpec as P

D = 1024
HEAD_DIM = 64
STATE = 128
HEADS_A = 16
CONV = 4
PATCH = 8
DI = 2048
GROUP = 8
TILE = 128
HIDDEN = 512

epsilon = 1e-05
highest = lax.Precision.HIGHEST
F32 = jnp.float32
BF16 = jnp.bfloat16
SEQ = ("g", "s")


def mm(left, right):
    return lax.dot_general(left, right, (((1,), (0,)), ((), ())), preferred_element_type=F32)


def mm_nt(left, right):
    return lax.dot_general(left, right, (((1,), (1,)), ((), ())), preferred_element_type=F32)


def mm_tn(left, right):
    return lax.dot_general(left, right, (((0,), (0,)), ((), ())), preferred_element_type=F32)


def inverse_rms(values):
    return lax.rsqrt(jnp.mean(values * values, axis=-1, keepdims=True) + epsilon)


def params(limit=60):
    return pltpu.CompilerParams(
        dimension_semantics=("arbitrary",), vmem_limit_bytes=limit * 1024 * 1024
    )


def whole(shape):
    return pl.BlockSpec(shape, lambda j: (0,) * len(shape))


def head_mask(width):
    lane = lax.broadcasted_iota(jnp.int32, (1, width), 1) // (D // HEADS_A)
    return [lane == h for h in range(width // (D // HEADS_A))]


def split_heads(tile, masks):
    zero = jnp.zeros_like(tile)
    return jnp.concatenate([jnp.where(m, tile, zero) for m in masks], axis=0)


def tile_mask(heads):
    row = lax.broadcasted_iota(jnp.int32, (heads * TILE, TILE), 0) % TILE
    col = lax.broadcasted_iota(jnp.int32, (heads * TILE, TILE), 1)
    return (row // PATCH == col // PATCH) & (col <= row)


def tile_probs(query_split, keys, keep):
    scores = mm_nt(query_split, keys) * ((D // HEADS_A) ** -0.5)
    scores = jnp.where(keep, scores, -1e30)
    expo = jnp.exp(scores - jnp.max(scores, axis=-1, keepdims=True))
    return expo / jnp.sum(expo, axis=-1, keepdims=True)


def beside(stacked, heads):
    return jnp.concatenate([stacked[h * TILE : (h + 1) * TILE] for h in range(heads)], axis=1)


def attention_forward_kernel(
    embed_ref, global_ref, gain_ref, weight_ref, hidden_ref, input_ref, normed_ref, qkv_ref, context_ref
):
    step = pl.program_id(0)
    blocks, rows, width = embed_ref.shape
    parts = weight_ref.shape[0]
    deep = D // parts

    @pl.when(step == 0)
    def _():
        embed = jnp.concatenate([embed_ref[i] for i in range(blocks)], axis=1).astype(F32)
        spread = jnp.broadcast_to(global_ref[...], (rows // PATCH, PATCH, D)).reshape(rows, D)
        total = embed + spread
        hidden_ref[...] = total
        low = total.astype(BF16)
        input_ref[...] = low
        values = low.astype(F32)
        normed_ref[...] = (values * inverse_rms(values) * gain_ref[...]).astype(BF16)

    normed = normed_ref[...]
    for k in range(3):
        weight = weight_ref[:, 0, k * deep : (k + 1) * deep, :].reshape(D, width)
        qkv_ref[0, k] = mm(normed, weight).astype(BF16)
    masks = head_mask(width)
    heads = len(masks)
    keep = tile_mask(heads)
    for r in range(rows // TILE):
        at = slice(r * TILE, (r + 1) * TILE)
        query = split_heads(qkv_ref[0, 0, at], masks)
        probs = tile_probs(query, qkv_ref[0, 1, at], keep).astype(BF16)
        values = split_heads(qkv_ref[0, 2, at], masks)
        context_ref[0, at] = mm(beside(probs, heads), values).astype(BF16)
    context = context_ref[0]
    piece = width // parts
    for c in range(D // width):
        low = 3 * deep + c * piece
        weight = weight_ref[:, 0, low : low + piece, :].reshape(width, width)
        cols = slice(c * width, (c + 1) * width)
        hidden_ref[:, cols] += mm(context, weight)


def attention_forward(embed, global_rows, gain, weights):
    blocks, rows, width = embed.shape
    parts, tps, depth, _ = weights.shape
    return pl.pallas_call(
        attention_forward_kernel,
        grid=(tps,),
        in_specs=[
            whole((blocks, rows, width)),
            whole((rows // PATCH, 1, D)),
            whole((1, D)),
            pl.BlockSpec((parts, 1, depth, width), lambda j: (0, j, 0, 0)),
        ],
        out_specs=[
            whole((rows, D)),
            whole((rows, D)),
            whole((rows, D)),
            pl.BlockSpec((1, 3, rows, width), lambda j: (j, 0, 0, 0)),
            pl.BlockSpec((1, rows, width), lambda j: (j, 0, 0)),
        ],
        out_shape=[
            jax.ShapeDtypeStruct((rows, D), F32),
            jax.ShapeDtypeStruct((rows, D), BF16),
            jax.ShapeDtypeStruct((rows, D), BF16),
            jax.ShapeDtypeStruct((tps, 3, rows, width), BF16),
            jax.ShapeDtypeStruct((tps, rows, width), BF16),
        ],
        compiler_params=params(),
        name="attention_forward",
        cost_estimate=pl.CostEstimate(
            flops=2 * rows * D * D * 4, bytes_accessed=14 << 20, transcendentals=rows * 2048
        ),
    )(embed, global_rows, gain, weights)


def feed_forward_kernel(
    hidden_ref,
    cot_ref,
    gain_ref,
    expand_ref,
    shrink_ref,
    layer_ref,
    grad_ref,
    gain_grad_ref,
    expand_grad_ref,
    shrink_grad_ref,
    normed_ref,
    turned_ref,
    cot_scratch,
    out_acc,
    normed_acc,
):
    step = pl.program_id(0)
    rows = hidden_ref.shape[0]
    blocks, _, width = cot_ref.shape
    parts = expand_ref.shape[0]
    deep = D // parts
    wide = expand_ref.shape[-1]

    @pl.when(step == 0)
    def _():
        values = hidden_ref[...].astype(BF16).astype(F32)
        normed = (values * inverse_rms(values) * gain_ref[...]).astype(BF16)
        normed_ref[...] = normed
        turned_ref[...] = normed.astype(F32).T.astype(BF16)
        for i in range(blocks):
            cot_scratch[:, i * width : (i + 1) * width] = cot_ref[i]
        out_acc[...] = jnp.zeros_like(out_acc)
        normed_acc[...] = jnp.zeros_like(normed_acc)

    normed = normed_ref[...]
    cot = cot_scratch[...]
    gate_weight = expand_ref[:, 0, :deep, :].reshape(D, wide)
    up_weight = expand_ref[:, 0, deep:, :].reshape(D, wide)
    down_weight = shrink_ref[...].reshape(wide, D)
    gate = mm(normed, gate_weight)
    up = mm(normed, up_weight)
    sigma = 1.0 / (1.0 + jnp.exp(-gate))
    swish = gate * sigma
    activ = (swish * up).astype(BF16)
    out_acc[...] += mm(activ, down_weight)
    shrink_grad_ref[...] = mm_tn(activ, cot).astype(BF16).reshape(shrink_grad_ref.shape)
    dactiv = mm_nt(cot, down_weight)
    dgate = (dactiv * up * sigma * (1.0 + gate * (1.0 - sigma))).astype(BF16)
    dup = (dactiv * swish).astype(BF16)
    normed_acc[...] += mm_nt(dgate, gate_weight) + mm_nt(dup, up_weight)
    turned = turned_ref[...]
    expand_grad_ref[:, 0, :deep, :] = mm(turned, dgate).astype(BF16).reshape(parts, deep, wide)
    expand_grad_ref[:, 0, deep:, :] = mm(turned, dup).astype(BF16).reshape(parts, deep, wide)

    @pl.when(step == pl.num_programs(0) - 1)
    def _():
        layer = (hidden_ref[...] + out_acc[...]).astype(BF16)
        for i in range(blocks):
            layer_ref[i] = layer[:, i * width : (i + 1) * width]
        values = hidden_ref[...].astype(BF16).astype(F32)
        scale = inverse_rms(values)
        normal = values * scale
        grad = normed_acc[...]
        gain_grad_ref[...] = jnp.sum(grad * normal, axis=0, keepdims=True)
        scaled = grad * gain_ref[...]
        back = scale * (scaled - normal * jnp.mean(scaled * normal, axis=-1, keepdims=True))
        grad_ref[...] = cot_scratch[...].astype(F32) + back


def feed_forward(hidden, cot, gain, weights):
    rows = hidden.shape[0]
    blocks, _, width = cot.shape
    parts, tps, depth, total = weights.shape
    deep = D // parts
    wide = HIDDEN
    count = total // wide
    held = wide // deep
    return pl.pallas_call(
        feed_forward_kernel,
        grid=(tps * count,),
        in_specs=[
            whole((rows, D)),
            whole((blocks, rows, width)),
            whole((1, D)),
            pl.BlockSpec((parts, 1, 2 * deep, wide), lambda j: (0, j // count, 0, j % count)),
            pl.BlockSpec((held, 1, deep, D), lambda j: (j % count, j // count, 2, 0)),
        ],
        out_specs=[
            whole((blocks, rows, width)),
            whole((rows, D)),
            whole((1, D)),
            pl.BlockSpec((parts, 1, 2 * deep, wide), lambda j: (0, j // count, 0, j % count)),
            pl.BlockSpec((held, 1, deep, D), lambda j: (j % count, j // count, 0, 0)),
        ],
        out_shape=[
            jax.ShapeDtypeStruct((blocks, rows, width), BF16),
            jax.ShapeDtypeStruct((rows, D), F32),
            jax.ShapeDtypeStruct((1, D), F32),
            jax.ShapeDtypeStruct((parts, tps, 2 * deep, total), BF16),
            jax.ShapeDtypeStruct((parts, tps, deep, D), BF16),
        ],
        scratch_shapes=[
            pltpu.VMEM((rows, D), BF16),
            pltpu.VMEM((D, rows), BF16),
            pltpu.VMEM((rows, D), BF16),
            pltpu.VMEM((rows, D), F32),
            pltpu.VMEM((rows, D), F32),
        ],
        compiler_params=params(),
        name="feed_forward",
        cost_estimate=pl.CostEstimate(
            flops=18 * rows * D * total * tps, bytes_accessed=56 << 20, transcendentals=rows * total * tps
        ),
    )(hidden, cot, gain, weights, weights)


def attention_backward_kernel(
    grad_ref,
    mixer_ref,
    input_ref,
    normed_ref,
    gain_ref,
    weight_ref,
    qkv_ref,
    context_ref,
    embed_ref,
    global_ref,
    dot_ref,
    gain_grad_ref,
    weight_grad_ref,
    turned_ref,
    low_ref,
    normed_acc,
    context_grad_ref,
    qkv_grad_ref,
):
    step = pl.program_id(0)
    rows = grad_ref.shape[0]
    blocks, _, width = embed_ref.shape
    parts = weight_ref.shape[0]
    deep = D // parts
    scaling = (D // HEADS_A) ** -0.5

    @pl.when(step == 0)
    def _():
        turned_ref[...] = normed_ref[...].astype(F32).T.astype(BF16)
        low_ref[...] = grad_ref[...].astype(BF16)
        normed_acc[...] = jnp.zeros_like(normed_acc)

    low = low_ref[...]
    context = context_ref[0]
    piece = width // parts
    total = jnp.zeros((rows, width), F32)
    for c in range(D // width):
        first = 3 * deep + c * piece
        weight = weight_ref[:, 0, first : first + piece, :].reshape(width, width)
        columns = low[:, c * width : (c + 1) * width]
        total = total + mm_nt(columns, weight)
        grad = mm_tn(context, columns).astype(BF16)
        weight_grad_ref[:, 0, first : first + piece, :] = grad.reshape(parts, piece, width)
    context_grad_ref[...] = total.astype(BF16)
    masks = head_mask(width)
    heads = len(masks)
    keep = tile_mask(heads)
    for r in range(rows // TILE):
        at = slice(r * TILE, (r + 1) * TILE)
        query = split_heads(qkv_ref[0, 0, at], masks)
        keys = qkv_ref[0, 1, at]
        probs = tile_probs(query, keys, keep)
        dcontext = split_heads(context_grad_ref[at], masks)
        dprobs = mm_nt(dcontext, qkv_ref[0, 2, at])
        dvalues = mm_tn(probs.astype(BF16), dcontext)
        inner = jnp.sum(dprobs * probs, axis=-1, keepdims=True)
        dscores = (probs * (dprobs - inner)).astype(BF16)
        dquery = mm(beside(dscores, heads), split_heads(keys, masks)) * scaling
        dkeys = mm_tn(dscores, query) * scaling
        qkv_grad_ref[at, :width] = dquery.astype(BF16)
        qkv_grad_ref[at, width : 2 * width] = dkeys.astype(BF16)
        qkv_grad_ref[at, 2 * width :] = dvalues.astype(BF16)
    turned = turned_ref[...]
    for k in range(3):
        part = qkv_grad_ref[:, k * width : (k + 1) * width]
        weight = weight_ref[:, 0, k * deep : (k + 1) * deep, :].reshape(D, width)
        normed_acc[...] += mm_nt(part, weight)
        grad = mm(turned, part).astype(BF16)
        weight_grad_ref[:, 0, k * deep : (k + 1) * deep, :] = grad.reshape(parts, deep, width)

    @pl.when(step == pl.num_programs(0) - 1)
    def _():
        values = input_ref[...].astype(F32)
        scale = inverse_rms(values)
        normal = values * scale
        grad = normed_acc[...]
        gain_grad_ref[...] = jnp.sum(grad * normal, axis=0, keepdims=True)
        scaled = grad * gain_ref[...]
        back = scale * (scaled - normal * jnp.mean(scaled * normal, axis=-1, keepdims=True))
        result = grad_ref[...] + back
        for i in range(blocks):
            embed_ref[i] = result[:, i * width : (i + 1) * width].astype(BF16)
        patch = jnp.sum(result.reshape(rows // PATCH, PATCH, D), axis=1)
        global_ref[...] = patch
        dot_ref[...] = jnp.sum(patch * mixer_ref[...], axis=1, keepdims=True)


def attention_backward(grad, mixer_rows, inputs, normed, gain, weights, qkv, context):
    rows = grad.shape[0]
    parts, tps, depth, width = weights.shape
    return pl.pallas_call(
        attention_backward_kernel,
        grid=(tps,),
        in_specs=[
            whole((rows, D)),
            whole((rows // PATCH, D)),
            whole((rows, D)),
            whole((rows, D)),
            whole((1, D)),
            pl.BlockSpec((parts, 1, depth, width), lambda j: (0, j, 0, 0)),
            pl.BlockSpec((1, 3, rows, width), lambda j: (j, 0, 0, 0)),
            pl.BlockSpec((1, rows, width), lambda j: (j, 0, 0)),
        ],
        out_specs=[
            whole((tps, rows, width)),
            whole((rows // PATCH, D)),
            whole((rows // PATCH, 1)),
            whole((1, D)),
            pl.BlockSpec((parts, 1, depth, width), lambda j: (0, j, 0, 0)),
        ],
        out_shape=[
            jax.ShapeDtypeStruct((tps, rows, width), BF16),
            jax.ShapeDtypeStruct((rows // PATCH, D), F32),
            jax.ShapeDtypeStruct((rows // PATCH, 1), F32),
            jax.ShapeDtypeStruct((1, D), F32),
            jax.ShapeDtypeStruct((parts, tps, depth, width), BF16),
        ],
        scratch_shapes=[
            pltpu.VMEM((D, rows), BF16),
            pltpu.VMEM((rows, D), BF16),
            pltpu.VMEM((rows, D), F32),
            pltpu.VMEM((rows, width), BF16),
            pltpu.VMEM((rows, 3 * width), BF16),
        ],
        compiler_params=params(),
        name="attention_backward",
        cost_estimate=pl.CostEstimate(
            flops=4 * rows * D * D * 4, bytes_accessed=26 << 20, transcendentals=rows * 2048
        ),
    )(grad, mixer_rows, inputs, normed, gain, weights, qkv, context)


def shifted(block, distance):
    devices = range(lax.axis_size(SEQ))
    route = [(i - distance, i) for i in devices if i - distance in devices]
    return lax.ppermute(block, SEQ, route)


def rms_scale(values):
    return values * inverse_rms(values)


def sequence_first(positions, lengths):
    offsets = jnp.cumsum(lengths) - lengths
    chosen = jnp.where(offsets[None, :] <= positions[:, None], offsets[None, :], 0)
    return jnp.max(chosen, axis=1)


def causal_conv(padded, weight, positions, first):
    count = positions.shape[0]
    total = jnp.zeros((count, padded.shape[1]), jnp.float32)
    for offset in range(CONV):
        lag = CONV - 1 - offset
        keep = (positions - lag >= first).astype(jnp.float32)[:, None]
        total = total + weight[offset][None, :] * padded[offset : offset + count] * keep
    return total


def front_part(padded, step_raw, conv_weight, step_bias, decay_log, positions, first):
    activated = jax.nn.silu(causal_conv(padded, conv_weight, positions, first))
    inner = activated.shape[1] - 2 * STATE
    count = positions.shape[0]
    inner_vals = activated[:, :inner].reshape(count, inner // HEAD_DIM, HEAD_DIM)
    bmatrix = activated[:, inner : inner + STATE]
    cmatrix = activated[:, inner + STATE :]
    steps = jax.nn.softplus(step_raw + step_bias[None, :])
    rates = -jnp.exp(decay_log)
    return (inner_vals, bmatrix, cmatrix, steps, rates)


def block_summary(inner_vals, bmatrix, steps, rates, positions, first):
    logs = jnp.cumsum(steps * rates[None, :], axis=0)
    final = logs[-1]
    in_last = (first == first[-1]).astype(jnp.float32)[:, None]
    weights = jnp.exp(final[None, :] - logs) * in_last * steps
    carried = jnp.exp(final) * (first[-1] < positions[0]).astype(jnp.float32)
    states = jnp.einsum("sh,shp,sn->hpn", weights, inner_vals, bmatrix, precision=highest)
    return (carried, states)


def block_output(inner_vals, bmatrix, cmatrix, steps, rates, skip_gain, incoming, positions, first):
    logs = jnp.cumsum(steps * rates[None, :], axis=0)
    count = positions.shape[0]
    same = (first[:, None] == first[None, :]) & (positions[None, :] <= positions[:, None])
    diff = logs.T[:, :, None] - logs.T[:, None, :]
    decay = jnp.where(same[None], jnp.exp(jnp.where(same[None], diff, 0.0)), 0.0)
    inner_prod = jnp.dot(cmatrix, bmatrix.T, precision=highest, preferred_element_type=jnp.float32)
    mixing = decay * inner_prod[None] * steps.T[:, None, :]
    within = jnp.einsum("hts,shp->thp", mixing, inner_vals, precision=highest)
    carry = jnp.exp(logs) * (first < positions[0]).astype(jnp.float32)[:, None]
    remote = jnp.einsum("tn,hpn->thp", cmatrix, incoming, precision=highest) * carry[:, :, None]
    result = within + remote + skip_gain[None, :, None] * inner_vals
    return result.reshape(count, -1)


def product(left, right, form):
    return jnp.einsum(form, left, right, preferred_element_type=jnp.float32)


def norm_backward(grad, values, gain):
    scale = inverse_rms(values)
    normed = values * scale
    scaled = grad * gain[None, :]
    result = scale * (scaled - normed * jnp.mean(scaled * normed, axis=-1, keepdims=True))
    return (result, jnp.sum(grad * normed, axis=0))


def chained(factors, states, here, reverse):
    count = factors.shape[0]
    order = jnp.arange(count)
    source, between = order[:, None], order[None, :]
    if reverse:
        crossed = (between > here) & (between < source)
        reaching = order > here
    else:
        crossed = (between < here) & (between > source)
        reaching = order < here
    chain = jnp.prod(jnp.where(crossed[:, :, None], factors[None], 1.0), axis=1)
    chain = chain * reaching[:, None].astype(F32)
    return jnp.sum(chain[:, :, None, None] * states, axis=0)


def spread_shard(array):
    size = array.shape[0] // GROUP
    return lax.dynamic_slice_in_dim(array, lax.axis_index("s") * size, size, 0)


def reduce_pieces(grads):
    own = lax.psum_scatter(grads, "s", scatter_dimension=0)
    own = lax.psum_scatter(own, "tp", scatter_dimension=0)
    if lax.axis_size("g") > 1:
        own = lax.psum(own, "g")
    return lax.all_gather(own, "s")


def shards(
    patches,
    byte_embed,
    seq_lengths,
    norm_global,
    proj_gate,
    proj_inner,
    proj_state,
    proj_step,
    step_bias,
    decay_log,
    conv_inner,
    conv_state,
    skip_gain,
    mixer_gain,
    proj_mixer,
    norm_attn,
    attn_input,
    attn_output,
    norm_ffn,
    expand_weight,
    shrink_weight,
    grad_output,
):
    count, quarter = patches.shape
    tps = lax.axis_size("tp")
    mine = lax.axis_index("tp")
    here = lax.axis_index("g") * lax.axis_size("s") + lax.axis_index("s")
    tail = CONV - 1
    inner_width = proj_inner.shape[1]
    share = count // tps
    total_rows = byte_embed.shape[0]
    rows = total_rows // tps

    narrow = D // GROUP
    slot = lax.axis_index("s")
    attn_in_part = lax.dynamic_slice_in_dim(attn_input, slot * narrow, narrow, 1)
    attn_out_part = spread_shard(attn_output)
    attn_out_part = attn_out_part.reshape(-1, tps, quarter).transpose(1, 0, 2)
    attn_part = jnp.concatenate(
        [attn_in_part.reshape(-1, quarter), attn_out_part.reshape(-1, quarter)], axis=0
    )
    attn_weights = lax.all_gather(attn_part, ("s", "tp")).reshape(GROUP, tps, -1, quarter)
    hidden_width = expand_weight.shape[2]
    expand_part = lax.dynamic_slice_in_dim(expand_weight, slot * narrow, narrow, 1)
    ffn_part = jnp.concatenate(
        [expand_part.reshape(-1, hidden_width), spread_shard(shrink_weight)], axis=0
    )
    ffn_weights = lax.all_gather(ffn_part, ("s", "tp")).reshape(GROUP, tps, -1, hidden_width)

    def to_rows(array):
        return lax.all_to_all(array.reshape(tps, rows, quarter), "tp", 0, 0)

    def to_columns(blocks):
        return lax.all_to_all(blocks, "tp", 0, 0).reshape(total_rows, quarter)

    positions = here * count + jnp.arange(count, dtype=jnp.int32)
    first = sequence_first(positions, seq_lengths)
    patch_rows = lax.all_gather(patches, "tp", axis=1, tiled=True)
    embed_rows = to_rows(byte_embed)
    cot_rows = to_rows(grad_output)
    global_in = patch_rows.astype(jnp.float32)
    normed = (rms_scale(global_in) * norm_global[None, :]).astype(jnp.bfloat16)
    gate_vals = product(normed, proj_gate, "rd,dc->rc")
    inner_raw = product(normed, proj_inner, "rd,dc->rc")
    state_raw = product(normed, proj_state, "rd,dc->rc")
    step_raw = product(normed, proj_step, "rd,dc->rc")
    raw = jnp.concatenate([inner_raw, state_raw], axis=1)
    before = shifted(raw[count - tail :], 1)
    padded = jnp.concatenate([before, raw], axis=0)
    conv_weight = jnp.concatenate([conv_inner, conv_state], axis=1)

    def front_local(padded_in, step_in, conv_in, bias_in, decay_in):
        return front_part(padded_in, step_in, conv_in, bias_in, decay_in, positions, first)

    def summary_local(inner_in, bmat_in, steps_in, rates_in):
        return block_summary(inner_in, bmat_in, steps_in, rates_in, positions, first)

    def output_local(inner_in, bmat_in, cmat_in, steps_in, rates_in, skip_in, incoming_in):
        return block_output(
            inner_in, bmat_in, cmat_in, steps_in, rates_in, skip_in, incoming_in, positions, first
        )

    front_vals, front_pull = jax.vjp(
        front_local, padded, step_raw, conv_weight, step_bias, decay_log
    )
    inner_vals, bmatrix, cmatrix, steps, rates = front_vals
    summary, summary_pull = jax.vjp(summary_local, inner_vals, bmatrix, steps, rates)
    carried, states = summary
    all_carried = lax.all_gather(carried, SEQ)
    incoming = chained(all_carried, lax.all_gather(states, SEQ), here, False)
    mixed, output_pull = jax.vjp(
        output_local, inner_vals, bmatrix, cmatrix, steps, rates, skip_gain, incoming
    )
    gate_act = jax.nn.silu(gate_vals)
    gated = mixed * gate_act
    squares = jnp.sum(gated * gated, axis=1, keepdims=True)
    partial = product((gated * mixer_gain[None, :]).astype(BF16), proj_mixer, "rc,cd->rd")
    summed = lax.psum_scatter(
        jnp.concatenate([partial, jnp.broadcast_to(squares, (count, 128))], axis=1),
        "tp",
        scatter_dimension=0,
        tiled=True,
    )
    own_squares = summed[:, D : D + 1]
    mixer_rows = summed[:, :D] * lax.rsqrt(own_squares / DI + epsilon)
    own_patches = lax.dynamic_slice_in_dim(patch_rows, mine * share, share, 0)
    global_out = own_patches.astype(F32) + mixer_rows

    hidden, attn_in, attn_normed, qkv, context = attention_forward(
        embed_rows, global_out[:, None, :], norm_attn[None, :], attn_weights
    )
    layer_blocks, hidden_grad, norm_ffn_part, expand_part, shrink_part = feed_forward(
        hidden, cot_rows, norm_ffn[None, :], ffn_weights
    )
    layer_output = to_columns(layer_blocks)
    embed_blocks, own_grad, row_dot, norm_attn_part, attn_part = attention_backward(
        hidden_grad, mixer_rows, attn_in, attn_normed, norm_attn[None, :], attn_weights, qkv, context
    )
    shrink_grad = reduce_pieces(shrink_part).reshape(-1, D).astype(F32)
    expand_grad = reduce_pieces(expand_part).reshape(GROUP, 2, narrow, hidden_width)
    expand_grad = expand_grad.transpose(1, 0, 2, 3).reshape(2, D, hidden_width).astype(F32)
    attn_grad = reduce_pieces(attn_part)
    attn_input_grad = attn_grad[:, : 3 * narrow].reshape(GROUP, 3, narrow, quarter)
    attn_input_grad = attn_input_grad.transpose(1, 0, 2, 3).reshape(3, D, quarter).astype(F32)
    attn_output_grad = attn_grad[:, 3 * narrow :].reshape(GROUP, tps, -1, quarter)
    attn_output_grad = attn_output_grad.transpose(0, 2, 1, 3).reshape(quarter, D).astype(F32)
    embed_grad = to_columns(embed_blocks).astype(F32)

    extras = jnp.concatenate([own_squares, row_dot], axis=1)
    mix_back_in = lax.all_gather(own_grad.astype(BF16), "tp", axis=0, tiled=True)
    all_extras = lax.all_gather(extras, "tp", axis=0, tiled=True)
    row_scale = lax.rsqrt(all_extras[:, :1] / DI + epsilon)
    row_mean = all_extras[:, 1:] / DI
    normed_mix = gated * row_scale
    mix_low = (normed_mix * mixer_gain[None, :]).astype(jnp.bfloat16)
    proj_mixer_grad = product(mix_low, mix_back_in, "rc,rd->cd")
    mix_low_grad = product(mix_back_in, proj_mixer, "rd,cd->rc")
    mixer_gain_grad = jnp.sum(mix_low_grad * normed_mix, axis=0)
    scaled_grad = mix_low_grad * mixer_gain[None, :]
    gated_grad = row_scale * (scaled_grad - normed_mix * row_mean)
    mixed_grad = gated_grad * gate_act
    sigma_gate = jax.nn.sigmoid(gate_vals)
    gate_vals_grad = gated_grad * mixed * sigma_gate * (1.0 + gate_vals * (1.0 - sigma_gate))
    inner_one, bmat_one, cmat_one, steps_one, rates_one, skip_gain_grad, incoming_grad = (
        output_pull(mixed_grad)
    )
    later_grad = chained(all_carried, lax.all_gather(incoming_grad, SEQ), here, True)
    carried_grad = jnp.sum(later_grad * incoming, axis=(1, 2))
    inner_two, bmat_two, steps_two, rates_two = summary_pull((carried_grad, later_grad))
    padded_grad, step_raw_grad, conv_grad, step_bias_grad, decay_log_grad = front_pull(
        (
            inner_one + inner_two,
            bmat_one + bmat_two,
            cmat_one,
            steps_one + steps_two,
            rates_one + rates_two,
        )
    )
    tail_grad = shifted(padded_grad[:tail], -1)
    raw_grad = padded_grad[tail:]
    raw_grad = jnp.concatenate(
        [raw_grad[: count - tail], raw_grad[count - tail :] + tail_grad], axis=0
    )
    gate_back = gate_vals_grad.astype(jnp.bfloat16)
    inner_back = raw_grad[:, :inner_width].astype(jnp.bfloat16)
    state_back = raw_grad[:, inner_width:].astype(jnp.bfloat16)
    step_back = step_raw_grad.astype(jnp.bfloat16)
    normed_grad_part = (
        product(gate_back, proj_gate, "rc,dc->rd")
        + product(inner_back, proj_inner, "rc,dc->rd")
        + product(step_back, proj_step, "rc,dc->rd")
        + product(state_back, proj_state, "rs,ds->rd")
    )
    part_in_grad, norm_global_part = norm_backward(normed_grad_part, global_in, norm_global)
    part_in_grad = lax.dynamic_update_slice_in_dim(
        part_in_grad,
        lax.dynamic_slice_in_dim(part_in_grad, mine * share, share, 0) + own_grad,
        mine * share,
        0,
    )
    patch_grad = lax.psum_scatter(part_in_grad, "tp", scatter_dimension=1, tiled=True)
    state_all = lax.all_gather(state_back, "tp")
    state_sum = jnp.sum(state_all.astype(F32), axis=0).astype(BF16)
    shared = lax.psum(
        (
            conv_grad[:, inner_width:],
            norm_attn_part[0],
            norm_ffn_part[0],
            norm_global_part,
        ),
        "tp",
    )
    proj_grads = lax.psum(
        (
            product(normed, gate_back, "rd,rc->dc").astype(BF16),
            product(normed, inner_back, "rd,rc->dc").astype(BF16),
            product(normed, state_sum, "rd,rc->dc").astype(BF16),
            proj_mixer_grad.astype(BF16),
        ),
        SEQ,
    )
    proj_gate_grad, proj_inner_grad, proj_state_grad, proj_mixer_grad = (
        g.astype(F32) for g in proj_grads
    )
    (
        conv_state_grad,
        norm_attn_grad,
        norm_ffn_grad,
        norm_global_grad,
        proj_step_grad,
        step_bias_grad,
        decay_log_grad,
        conv_inner_grad,
        skip_gain_grad,
        mixer_gain_grad,
    ) = lax.psum(
        shared
        + (
            product(normed, step_back, "rd,rc->dc"),
            step_bias_grad,
            decay_log_grad,
            conv_grad[:, :inner_width],
            skip_gain_grad,
            mixer_gain_grad,
        ),
        SEQ,
    )
    return (
        layer_output,
        embed_grad,
        patch_grad,
        norm_global_grad,
        proj_gate_grad,
        proj_inner_grad,
        proj_state_grad,
        proj_step_grad,
        step_bias_grad,
        decay_log_grad,
        conv_inner_grad,
        conv_state_grad,
        skip_gain_grad,
        mixer_gain_grad,
        proj_mixer_grad,
        norm_attn_grad,
        attn_input_grad,
        attn_output_grad,
        norm_ffn_grad,
        expand_grad,
        shrink_grad,
    )


def solution(mesh):
    seq, tps = mesh.shape["seq"], mesh.shape["tp"]
    fine = Mesh(mesh.devices.reshape(seq // GROUP, GROUP, tps), ("g", "s", "tp"))
    rows_cols = P(SEQ, "tp")
    last = P(None, "tp")
    lead = P("tp", None)
    return jax.shard_map(
        shards,
        mesh=fine,
        in_specs=(
            rows_cols,
            rows_cols,
            P(),
            P(),
            last,
            last,
            P(),
            last,
            P("tp"),
            P("tp"),
            last,
            P(),
            P("tp"),
            P("tp"),
            lead,
            P(),
            P(None, None, "tp"),
            lead,
            P(),
            P(None, None, "tp"),
            lead,
            rows_cols,
        ),
        out_specs=(
            rows_cols,
            rows_cols,
            rows_cols,
            P(),
            last,
            last,
            P(),
            last,
            P("tp"),
            P("tp"),
            last,
            P(),
            P("tp"),
            P("tp"),
            lead,
            P(),
            P(None, None, "tp"),
            lead,
            P(),
            P(None, None, "tp"),
            lead,
        ),
        check_vma=False,
    )
```

time: 1640 us -> 1080 us (0.66)
  waiting for transfers between devices: 1110 us -> 636 us
  matrix products: 185 us -> 45.8 us
  Pallas kernels: 0 us -> 91.6 us
  local copies, waits for them, and re-layouts: 91.5 us -> 33.6 us
  blocking collectives: 140 us -> 191 us
  other arithmetic: 87.6 us -> 46.2 us
    psum x1, waiting for transfers between devices: 288 us -> 0.01 us  [shards(): lax.psum((product(normed, gate_back, 'rd,rc->dc').astype(BF16), product(n...]
    reduce_scatter x6 -> x8, waiting for transfers between devices: 497 us -> 322 us  [the longest x3 231 us: reduce_pieces(): own = lax.psum_scatter(grads, 's', scatter_dimension=0)]
    dot_general x36 -> x15, matrix products: 155 us -> 21.3 us  [product(): return jnp.einsum(form, left, right, preferred_element_type=jnp.float32)]
    pallas_call x0 -> x3, Pallas kernels: none -> 91.6 us  [the longest x1 50.5 us: feed_forward(): pl.pallas_call(feed_forward_kernel, grid=(tps * count,), in_specs=[whole(...]
    all_to_all x0 -> x2, blocking collectives: none -> 78.9 us  [the longest x1 49.8 us: to_rows(): return lax.all_to_all(array.reshape(tps, rows, quarter), 'tp', 0, 0)]
    psum x5 -> x2, blocking collectives: 96.5 us -> 40.6 us  [the longest x1 23.8 us: shards(): lax.psum(shared + (product(normed, step_back, 'rd,rc->dc'), step_bias_gra...]
    all_gather x6 -> x7, waiting for transfers between devices: 322 us -> 291 us  [the longest x1 141 us: shards(): lax.all_gather(ffn_part, ('s', 'tp')).reshape(GROUP, tps, -1, hidden_width)]
    all_gather x3 -> x5, blocking collectives: 43.5 us -> 71.6 us  [the longest x1 20.3 us: shards(): state_all = lax.all_gather(state_back, 'tp')]
  transfers between devices with their start and end apart: 15 -> 20, of which waited for: 11 -> 14; matrix products, arithmetic and copies ran while one was open for 8% -> 9% of each run, Pallas kernels for 0% -> 1%
where the time goes in v1:
time: 1080 us; the launch traced here: 1070 us
  waiting for transfers between devices  636 us (59%)
  blocking collectives  191 us (18%)
  Pallas kernels  91.6 us (8%)
  other arithmetic  46.2 us (4%)
  matrix products  45.8 us (4%)
  local copies, waits for them, and re-layouts  33.6 us (3%)
  between operations  18.6 us (2%)
  starting transfers between devices  10.9 us (1%)
    reduce_scatter x3, waiting for transfers between devices, reduce_pieces(): own = lax.psum_scatter(grads, 's', scatter_dimension=0)  231 us
    all_gather x1, waiting for transfers between devices, shards(): lax.all_gather(ffn_part, ('s', 'tp')).reshape(GROUP, tps, -1, hidden_width)  141 us
    reduce_scatter x3, waiting for transfers between devices, reduce_pieces(): own = lax.psum_scatter(own, 'tp', scatter_dimension=0)  67.9 us
    all_gather x1, waiting for transfers between devices, shards(): lax.all_gather(attn_part, ('s', 'tp')).reshape(GROUP, tps, -1, quarter)  62.3 us
    all_gather x3, waiting for transfers between devices, reduce_pieces(): return lax.all_gather(own, 's')  51 us
    pallas_call x1, Pallas kernels, feed_forward(): pl.pallas_call(feed_forward_kernel, grid=(tps * count,), in_specs=[whole(...  50.5 us
    all_to_all x1, blocking collectives, to_rows(): return lax.all_to_all(array.reshape(tps, rows, quarter), 'tp', 0, 0)  49.8 us
    all_to_all x1, blocking collectives, to_columns(): return lax.all_to_all(blocks, 'tp', 0, 0).reshape(total_rows, quarter)  29.1 us
  transfers between devices with their start and end apart: 20, of which 14 were waited for; matrix products, arithmetic and copies ran while one was open for 9% of the time, Pallas kernels for 1%

profile of v1, /device:TPU:0, one launch (start us, length us, event | category | flops | bytes accessed | tf_op | source)
XLA Modules:
  0.0 1073.2 jit_solution(3270696616863661641)
XLA Ops:
  8.1 17.7 %all_gather.52 = bf16[256,1024]{1,0:T(8,128)(2,1)S(1)} all-gather(bf16[256,256]{1,0:T(8,128)(2,1)} %param.22), channel_id=1, replica_groups=mesh['seq'=8,'tp'=4] {'tp'}, dimensions={1}, use_global_device_ids=true | all-gather | bytes 655360 | tf_op jit(solution)/shard_map/all_gather | solution.py:567
  37.7 2.6 fusion.51
  42.0 2.1 copy.107
  44.1 2.3 fusion.57
  46.5 9.4 all-gather.5
  58.2 2.1 fusion.79
  60.3 16.9 %all-gather.21.cloned.1.call-done = f32[64,64,128]{2,1,0:T(8,128)} async-done(((f32[8,64,128]{2,1,0:T(8,128)}), f32[64,64,128]{2,1,0:T(8,128)}) %all-gather.21.cloned.1.call-update) | async-done | bytes 2097168 | tf_op jit(solution)/shard_map/all_gather | solution.py:599
  80.8 3.4 fusion.26
  84.1 2.0 copy.108
  86.2 2.8 multiply_reduce_fusion.12
  97.9 49.8 %all_to_all.20.embed_ref = bf16[4,512,256]{2,1,0:T(8,128)(2,1)} all-to-all(bf16[4,512,256]{2,1,0:T(8,128)(2,1)S(1)} %bitcast.214), channel_id=1, replica_groups=mesh['seq'=8,'tp'=4] {'tp'}, dimensions={0} | all-to-all | bytes 2097152 | tf_op jit(solution)/shard_map/all_to_all | solution.py:560
  147.7 3.5 all-to-all-start.1
  155.4 62.3 %all-gather.23.cloned.1.call-done = bf16[16384,256]{1,0:T(8,128)(2,1)} async-done(((bf16[512,256]{1,0:T(8,128)(2,1)}), bf16[16384,256]{1,0:T(8,128)(2,1)}) %all-gather.23.cloned.1.call-update) | async-done | bytes 8388624 | tf_op jit(solution)/shard_map/all_gather | solution.py:551
  217.7 14.7 %attention_forward.1 = (f32[512,1024]{1,0:T(8,128)}, bf16[512,1024]{1,0:T(8,128)(2,1)}, bf16[512,1024]{1,0:T(8,128)(2,1)}, bf16[4,3,512,256]{3,2,1,0:T(8,128)(2,1)}, bf16[4,512,256]{2,1,0:T(8,128)(2,1)}) custom-call(bf16[4,512,256]{2,1,0:T(8,128)(2,1)} %all_to_all.20.embed_ref, f32[64,1,1024]{2,1,0:T(1,128)} %copy.110.global_ref, f32[1,1024]{1,0:T(1,128)} %bitcast.237, ...), custom_call_target="tpu_custom_call" | custom-call | flops 4294967296 | bytes 14680064 | tf_op jit(solution)/shard_map/attention_forward/pallas_call | solution.py:125
  232.4 141.5 %all-gather.25.cloned.1.call-done = bf16[12288,1024]{1,0:T(8,128)(2,1)} async-done(((bf16[384,1024]{1,0:T(8,128)(2,1)}), bf16[12288,1024]{1,0:T(8,128)(2,1)}) %all-gather.25.cloned.1.call-update) | async-done | bytes 25165840 | tf_op jit(solution)/shard_map/all_gather | solution.py:557
  373.9 50.5 %feed_forward.1 = (bf16[4,512,256]{2,1,0:T(8,128)(2,1)}, f32[512,1024]{1,0:T(8,128)}, f32[1,1024]{1,0:T(1,128)}, bf16[8,4,256,1024]{3,2,1,0:T(8,128)(2,1)}, bf16[8,4,128,1024]{3,2,1,0:T(8,128)(2,1)}) custom-call(f32[512,1024]{1,0:T(8,128)} %get-tuple-element.36.hidden_ref, bf16[4,512,256]{2,1,0:T(8,128)(2,1)} %copy-done.30, f32[1,1024]{1,0:T(1,128)} %bitcast.236, ...), custom_call_target="tpu_custom_call" | custom-call | flops 38654705664 | bytes 58720256 | tf_op jit(solution)/shard_map/feed_forward/pallas_call | solution.py:234
  424.3 26.4 %attention_backward.1 = (bf16[4,512,256]{2,1,0:T(8,128)(2,1)}, f32[64,1024]{1,0:T(8,128)}, f32[64,1]{1,0:T(8,128)}, f32[1,1024]{1,0:T(1,128)}, bf16[8,4,512,256]{3,2,1,0:T(8,128)(2,1)}) custom-call(f32[512,1024]{1,0:T(8,128)} %get-tuple-element.38.grad_ref, f32[64,1024]{1,0:T(8,128)} %get-tuple-element.97.mixer_ref, ...), custom_call_target="tpu_custom_call" | custom-call | flops 8589934592 | bytes 27262976 | tf_op jit(solution)/shard_map/attention_backward/pallas_call | solution.py:364
  452.2 8.9 all-gather.6
  461.2 15.3 %all_gather.61 = bf16[256,1024]{1,0:T(8,128)(2,1)S(1)} all-gather(bf16[64,1024]{1,0:T(8,128)(2,1)S(1)} %convert_element_type.175), channel_id=1, replica_groups=mesh['seq'=8,'tp'=4] {'tp'}, dimensions={0}, use_global_device_ids=true | all-gather | bytes 655360 | tf_op jit(solution)/shard_map/all_gather | solution.py:639
  476.6 3.9 multiply_reduce_fusion.10
  483.2 37.2 %reduce-scatter.13.cloned.1.call-done = bf16[1,4,512,256]{3,2,1,0:T(8,128)(2,1)} async-done(((bf16[8,4,512,256]{3,2,1,0:T(8,128)(2,1)}), bf16[1,4,512,256]{3,2,1,0:T(8,128)(2,1)}) %reduce-scatter.13.cloned.1.call-update) | async-done | bytes 1048592 | tf_op jit(solution)/shard_map/reduce_scatter | solution.py:502
  520.4 75.5 %reduce-scatter.21.cloned.1.call-done = bf16[1,4,128,1024]{3,2,1,0:T(8,128)(2,1)} async-done(((bf16[8,4,128,1024]{3,2,1,0:T(8,128)(2,1)}), bf16[1,4,128,1024]{3,2,1,0:T(8,128)(2,1)}) %reduce-scatter.21.cloned.1.call-update) | async-done | bytes 1048592 | tf_op jit(solution)/shard_map/reduce_scatter | solution.py:502
  596.7 118.7 %reduce-scatter.17.cloned.1.call-done = bf16[1,4,256,1024]{3,2,1,0:T(8,128)(2,1)} async-done(((bf16[8,4,256,1024]{3,2,1,0:T(8,128)(2,1)}), bf16[1,4,256,1024]{3,2,1,0:T(8,128)(2,1)}) %reduce-scatter.17.cloned.1.call-update) | async-done | bytes 2097168 | tf_op jit(solution)/shard_map/reduce_scatter | solution.py:502
  715.5 5.2 fusion.30
  725.9 19.7 %all-gather.27.cloned.1.call-done = f32[64,64,128]{2,1,0:T(8,128)} async-done(((f32[8,64,128]{2,1,0:T(8,128)}), f32[64,64,128]{2,1,0:T(8,128)}) %all-gather.27.cloned.1.call-update) | async-done | bytes 2097168 | tf_op jit(solution)/shard_map/all_gather | solution.py:656
  748.7 2.8 fusion.20
  751.5 2.1 copy.116
  756.3 2.4 multiply_reduce_fusion.6
  762.2 20.3 %all-gather.4 = bf16[1024,256]{1,0:T(8,128)(2,1)S(1)} all-gather(bf16[256,256]{1,0:T(8,128)(2,1)S(1)} %maximum_convert_fusion.1), channel_id=6, replica_groups=mesh['seq'=8,'tp'=4] {'tp'}, dimensions={0}, use_global_device_ids=true | all-gather | bytes 655360 | tf_op jit(solution)/shard_map/all_gather | solution.py:691
  786.9 23.1 %reduce-scatter.23.cloned.1.call-done = bf16[1,128,1024]{2,1,0:T(8,128)(2,1)} async-done(((bf16[4,128,1024]{2,1,0:T(8,128)(2,1)}), bf16[1,128,1024]{2,1,0:T(8,128)(2,1)}) %reduce-scatter.23.cloned.1.call-update) | async-done | bytes 262160 | tf_op jit(solution)/shard_map/reduce_scatter | solution.py:503
  810.1 44.8 %reduce-scatter.19.cloned.1.call-done = bf16[1,256,1024]{2,1,0:T(8,128)(2,1)} async-done(((bf16[4,256,1024]{2,1,0:T(8,128)(2,1)}), bf16[1,256,1024]{2,1,0:T(8,128)(2,1)}) %reduce-scatter.19.cloned.1.call-update) | async-done | bytes 524304 | tf_op jit(solution)/shard_map/reduce_scatter | solution.py:503
  854.9 29.1 %all_to_all.21 = bf16[4,512,256]{2,1,0:T(8,128)(2,1)} all-to-all(bf16[4,512,256]{2,1,0:T(8,128)(2,1)S(1)} %copy-done.29), channel_id=1, replica_groups=mesh['seq'=8,'tp'=4] {'tp'}, dimensions={0} | all-to-all | bytes 2097152 | tf_op jit(solution)/shard_map/all_to_all | solution.py:563
  884.0 3.7 all-to-all-start.3
  888.1 2.8 reduce-window.42
  891.0 2.7 fusion.131
  893.8 19.2 %all-to-all-done.3 = bf16[4,512,256]{2,1,0:T(8,128)(2,1)S(1)} async-done(((bf16[4,512,256]{2,1,0:T(8,128)(2,1)}), bf16[4,512,256]{2,1,0:T(8,128)(2,1)S(1)}, u32[]{:S(2)}, u32[]{:S(2)}) %all-to-all-start.3) | async-done | bytes 1048608 | tf_op jit(solution)/shard_map/all_to_all | solution.py:563
  915.3 2.5 reduce-window.44
  918.2 2.2 convolution_add_fusion.2
  923.7 16.8 %all-reduce.13 = (f32[1024]{0:T(1024)S(1)}, f32[4,256]{1,0:T(4,128)S(1)}, f32[1024]{0:T(1024)S(1)}, f32[1024]{0:T(1024)S(1)}) all-reduce(f32[1024]{0:T(1024)S(1)} %get-tuple-element.58, f32[4,256]{1,0:T(4,128)S(1)} %pad_add_fusion.3, f32[1024]{0:T(1024)S(1)} %bitcast.228, f32[1024]{0:T(1024)S(1)} %bitcast.227), channel_id=1, replica_groups=mesh['seq'=8,'tp'=4] {'tp'}, use_global_device_ids=true, to_apply=%region_25.26 | all-reduce | flops 4096 | bytes 32768 | tf_op jit(solution)/shard_map/psum | solution.py:693
  940.5 23.8 %all-reduce.12 = (f32[1024]{0:T(1024)}, f32[1024,8]{0,1:T(8,128)}, f32[8]{0:T(128)}, f32[8]{0:T(128)}, f32[4,512]{1,0:T(4,128)}, /*index=5*/f32[4,256]{1,0:T(4,1...) all-reduce(f32[1024]{0:T(1024)S(1)} %get-tuple-element.81, ...), channel_id=1, replica_groups=mesh['seq'=8,'tp'=4] {'seq'}, use_global_device_ids=true, to_apply=%region_26.27 | all-reduce | flops 14872 | bytes 118976 | tf_op jit(solution)/shard_map/psum | solution.py:725
  964.3 3.0 convert_element_type.180
  978.4 16.5 %all-gather.19.cloned.1.call-done = bf16[8,128,1024]{2,1,0:T(8,128)(2,1)} async-done(((bf16[1,128,1024]{2,1,0:T(8,128)(2,1)}), bf16[8,128,1024]{2,1,0:T(8,128)(2,1)}) %all-gather.19.cloned.1.call-update) | async-done | bytes 2097168 | tf_op jit(solution)/shard_map/all_gather | solution.py:506
  994.9 4.1 bitcast_convert_fusion
  998.9 34.6 %all-gather.17.cloned.1.call-done = bf16[8,256,1024]{2,1,0:T(8,128)(2,1)} async-done(((bf16[1,256,1024]{2,1,0:T(8,128)(2,1)}), bf16[8,256,1024]{2,1,0:T(8,128)(2,1)}) %all-gather.17.cloned.1.call-update) | async-done | bytes 4194320 | tf_op jit(solution)/shard_map/all_gather | solution.py:506
  1033.5 3.2 convert_bitcast_fusion
  1036.7 4.3 copy.121
  1041.0 22.4 %reduce-scatter.11.cloned.1.call-done = f32[256,256]{1,0:T(8,128)} async-done(((f32[256,1024]{1,0:T(8,128)}), f32[256,256]{1,0:T(8,128)}) %reduce-scatter.11.cloned.1.call-update) | async-done | bytes 262160 | tf_op jit(solution)/shard_map/reduce_scatter | solution.py:690
  1063.4 2.3 copy.135
  (372 shorter events, 71.9 us)
Async XLA Ops:
  8.0 87.6 %copy-start = (bf16[1024,1024]{1,0:T(8,128)(2,1)S(1)}, bf16[1024,1024]{1,0:T(8,128)(2,1)}, u32[]{:S(2)}) copy-start(bf16[1024,1024]{1,0:T(8,128)(2,1)} %param.42) | copy-start | bytes 6291460
  8.1 69.1 %all-gather.21.cloned.1.call-start = ((), (), s32[]{:S(2)}) async-start(), calls=%async_computation.23 | async-start | bytes 2359296 | tf_op jit(solution)/shard_map/all_gather | solution.py:599
  28.9 7.6 collective-permute-start
  46.4 105.3 %reduce-scatter.9.cloned.1.call-start = ((), (), s32[]{:S(2)}) async-start(), calls=%async_computation.12 | async-start | bytes 1474560 | tf_op jit(solution)/shard_map/reduce_scatter | solution.py:607
  57.3 691.3 %copy-start.46 = (f32[8,256]{1,0:T(8,128)}, f32[8,256]{1,0:T(8,128)S(1)}, u32[]{:S(2)}) copy-start(f32[8,256]{1,0:T(8,128)S(1)} %add_bitcast_fusion.3) | copy-start | bytes 24580
  58.2 25.9 %copy-start.41 = (pred[256,256]{1,0:T(8,128)(4,1)}, pred[256,256]{1,0:T(8,128)(4,1)S(1)}, u32[]{:S(2)}) copy-start(pred[256,256]{1,0:T(8,128)(4,1)S(1)} %compare_and_fusion) | copy-start | bytes 196612
  91.5 126.2 %all-gather.23.cloned.1.call-start = ((), (), s32[]{:S(2)}) async-start(), calls=%async_computation.24 | async-start | bytes 8650752 | tf_op jit(solution)/shard_map/all_gather | solution.py:551
  95.6 278.3 %all-gather.25.cloned.1.call-start = ((), (), s32[]{:S(2)}) async-start(), calls=%async_computation.25 | async-start | bytes 25952256 | tf_op jit(solution)/shard_map/all_gather | solution.py:557
  147.7 84.7 %all-to-all-start.1 = ((bf16[4,512,256]{2,1,0:T(8,128)(2,1)}), bf16[4,512,256]{2,1,0:T(8,128)(2,1)S(1)}, u32[]{:S(2)}, u32[]{:S(2)}) async-start(bf16[4,512,256]{2,1,0:T(8,128)(2,1)} %bitcast.215), calls=%async_computation.2 | async-start | bytes 2097152 | tf_op jit(solution)/shard_map/all_to_all | solution.py:560
  151.2 369.2 %reduce-scatter.13.cloned.1.call-start = ((), (), s32[]{:S(2)}) async-start(), calls=%async_computation.14 | async-start | bytes 9437184 | tf_op jit(solution)/shard_map/reduce_scatter | solution.py:502
  232.4 141.5 %copy-start.30 = (bf16[4,512,256]{2,1,0:T(8,128)(2,1)}, bf16[4,512,256]{2,1,0:T(8,128)(2,1)S(1)}, u32[]{:S(2)}) copy-start(bf16[4,512,256]{2,1,0:T(8,128)(2,1)S(1)} %all-to-all-done.1.cot_ref) | copy-start | bytes 3145732
  450.8 145.2 %reduce-scatter.21.cloned.1.call-start = ((), (), s32[]{:S(2)}) async-start(), calls=%async_computation.20 | async-start | bytes 9437184 | tf_op jit(solution)/shard_map/reduce_scatter | solution.py:502
  451.4 264.0 %reduce-scatter.17.cloned.1.call-start = ((), (), s32[]{:S(2)}) async-start(), calls=%async_computation.17 | async-start | bytes 18874368 | tf_op jit(solution)/shard_map/reduce_scatter | solution.py:502
  451.4 25.2 %copy-start.7 = (f32[256,768]{1,0:T(8,128)S(1)}, f32[256,768]{1,0:T(8,128)}, u32[]{:S(2)}) copy-start(f32[256,768]{1,0:T(8,128)} %copy-done.6) | copy-start | bytes 2359300
  451.4 25.2 %copy-start.22 = (f32[256,512]{1,0:T(8,128)S(1)}, f32[256,512]{1,0:T(8,128)}, u32[]{:S(2)}) copy-start(f32[256,512]{1,0:T(8,128)} %copy-done.21) | copy-start | bytes 1572868
  451.9 293.6 %all-gather.27.cloned.1.call-start = ((), (), s32[]{:S(2)}) async-start(), calls=%async_computation.26 | async-start | bytes 2359296 | tf_op jit(solution)/shard_map/all_gather | solution.py:656
  480.5 115.6 %copy-start.62 = (f32[8,8]{1,0:T(8,128)S(1)}, f32[8,8]{1,0:T(8,128)}, u32[]{:S(2)}) copy-start(f32[8,8]{1,0:T(8,128)} %get-tuple-element.69) | copy-start | bytes 772
  483.1 303.1 %reduce-scatter.15.cloned.1.call-start = ((), (), s32[]{:S(2)}) async-start(), calls=%async_computation.15 | async-start | bytes 1310720 | tf_op jit(solution)/shard_map/reduce_scatter | solution.py:503
  520.4 195.1 %copy-start.5 = (f32[256,512]{0,1:T(8,128)S(1)}, f32[256,512]{0,1:T(8,128)}, u32[]{:S(2)}) copy-start(f32[256,512]{0,1:T(8,128)} %copy.107) | copy-start | bytes 1572868
  520.4 195.1 %copy-start.42 = (pred[256,256]{1,0:T(8,128)(4,1)S(1)}, pred[256,256]{1,0:T(8,128)(4,1)}, u32[]{:S(2)}) copy-start(pred[256,256]{1,0:T(8,128)(4,1)} %copy-done.41) | copy-start | bytes 196612
  520.4 289.6 %reduce-scatter.23.cloned.1.call-start = ((), (), s32[]{:S(2)}) async-start(), calls=%async_computation.21 | async-start | bytes 1310720 | tf_op jit(solution)/shard_map/reduce_scatter | solution.py:503
  596.0 258.8 %reduce-scatter.19.cloned.1.call-start = ((), (), s32[]{:S(2)}) async-start(), calls=%async_computation.18 | async-start | bytes 2621440 | tf_op jit(solution)/shard_map/reduce_scatter | solution.py:503
  715.4 248.9 %all-reduce.17.cloned.1.call-start = ((), (), s32[]{:S(2)}) async-start(), calls=%async_computation.27 | async-start | bytes 7340032 | tf_op jit(solution)/shard_map/psum | solution.py:702
  722.8 22.8 %copy-start.58 = (f32[8,8]{1,0:T(8,128)S(1)}, f32[8,8]{1,0:T(8,128)}, u32[]{:S(2)}) copy-start(f32[8,8]{1,0:T(8,128)} %broadcast_multiply_fusion) | copy-start | bytes 772
  725.9 22.7 %copy-start.102 = (f32[8]{0:T(128)S(1)}, f32[8]{0:T(128)}, u32[]{:S(2)}) copy-start(f32[8]{0:T(128)} %param.34) | copy-start | bytes 100
  759.0 3.1 collective-permute-start.1
  762.1 21.1 %copy-start.52 = (f32[1024]{0:T(1024)S(1)}, f32[1024]{0:T(1024)}, u32[]{:S(2)}) copy-start(f32[1024]{0:T(1024)} %param.25) | copy-start | bytes 12292
  762.2 21.1 %copy-start.73 = (f32[256]{0:T(256)S(1)}, f32[256]{0:T(256)}, u32[]{:S(2)}) copy-start(f32[256]{0:T(256)} %copy-done.71) | copy-start | bytes 3076
  786.1 68.8 %copy-start.29 = (bf16[4,512,256]{2,1,0:T(8,128)(2,1)S(1)}, bf16[4,512,256]{2,1,0:T(8,128)(2,1)}, u32[]{:S(2)}) copy-start(bf16[4,512,256]{2,1,0:T(8,128)(2,1)} %get-tuple-element.37) | copy-start | bytes 3145732
  786.1 185.4 %all-gather.15.cloned.1.call-start = ((), (), s32[]{:S(2)}) async-start(), calls=%async_computation.16 | async-start | bytes 2359296 | tf_op jit(solution)/shard_map/all_gather | solution.py:506
  786.9 208.0 %all-gather.19.cloned.1.call-start = ((), (), s32[]{:S(2)}) async-start(), calls=%async_computation.22 | async-start | bytes 2359296 | tf_op jit(solution)/shard_map/all_gather | solution.py:506
  810.0 223.5 %all-gather.17.cloned.1.call-start = ((), (), s32[]{:S(2)}) async-start(), calls=%async_computation.19 | async-start | bytes 4718592 | tf_op jit(solution)/shard_map/all_gather | solution.py:506
  854.9 32.9 %copy-start.95 = (f32[512]{0:T(512)S(1)}, f32[512]{0:T(512)}, u32[]{:S(2)}) copy-start(f32[512]{0:T(512)} %get-tuple-element.89) | copy-start | bytes 6148
  854.9 33.1 %copy-start.20 = (f32[256,8,64]{0,2,1:T(8,128)S(1)}, f32[256,8,64]{0,2,1:T(8,128)}, u32[]{:S(2)}) copy-start(f32[256,8,64]{0,2,1:T(8,128)} %copy-done.19) | copy-start | bytes 1572868
  884.0 28.9 %all-to-all-start.3 = ((bf16[4,512,256]{2,1,0:T(8,128)(2,1)}), bf16[4,512,256]{2,1,0:T(8,128)(2,1)S(1)}, u32[]{:S(2)}, u32[]{:S(2)}) async-start(bf16[4,512,256]{2,1,0:T(8,128)(2,1)} %get-tuple-element.43), calls=%async_computation.4 | async-start | bytes 2097152 | tf_op jit(solution)/shard_map/all_to_all | solution.py:563
  887.7 175.7 %reduce-scatter.11.cloned.1.call-start = ((), (), s32[]{:S(2)}) async-start(), calls=%async_computation.13 | async-start | bytes 1310720 | tf_op jit(solution)/shard_map/reduce_scatter | solution.py:690
  893.7 20.8 %copy-start.11 = (f32[8,64,128]{2,1,0:T(8,128)S(1)}, f32[8,64,128]{2,1,0:T(8,128)}, u32[]{:S(2)}) copy-start(f32[8,64,128]{2,1,0:T(8,128)} %copy-done.9) | copy-start | bytes 786436
  893.7 20.8 %copy-start.13 = (f32[8,64,128]{2,1,0:T(8,128)S(1)}, f32[8,64,128]{2,1,0:T(8,128)}, u32[]{:S(2)}) copy-start(f32[8,64,128]{2,1,0:T(8,128)} %copy-done.12) | copy-start | bytes 786436
  893.7 21.0 %copy-start.57 = (f32[768]{0:T(1024)S(1)}, f32[768]{0:T(1024)}, u32[]{:S(2)}) copy-start(f32[768]{0:T(1024)} %get-tuple-element.55) | copy-start | bytes 9220
  893.7 21.0 %copy-start.56 = (f32[768]{0:T(1024)S(1)}, f32[768]{0:T(1024)}, u32[]{:S(2)}) copy-start(f32[768]{0:T(1024)} %get-tuple-element.56) | copy-start | bytes 9220
  893.7 21.1 %copy-start.55 = (f32[768]{0:T(1024)S(1)}, f32[768]{0:T(1024)}, u32[]{:S(2)}) copy-start(f32[768]{0:T(1024)} %get-tuple-element.57) | copy-start | bytes 9220
  893.7 21.1 %copy-start.54 = (f32[768]{0:T(1024)S(1)}, f32[768]{0:T(1024)}, u32[]{:S(2)}) copy-start(f32[768]{0:T(1024)} %get-tuple-element.60) | copy-start | bytes 9220
  893.7 21.1 %copy-start.40 = (f32[256,8]{0,1:T(8,128)S(1)}, f32[256,8]{0,1:T(8,128)}, u32[]{:S(2)}) copy-start(f32[256,8]{0,1:T(8,128)} %get-tuple-element.125) | copy-start | bytes 24580
  893.7 21.1 %copy-start.60 = (f32[256]{0:T(256)S(1)}, f32[256]{0:T(256)}, u32[]{:S(2)}) copy-start(f32[256]{0:T(256)} %copy-done.59) | copy-start | bytes 3076
  893.7 21.1 %copy-start.79 = (f32[8]{0:T(128)S(1)}, f32[8]{0:T(128)}, u32[]{:S(2)}) copy-start(f32[8]{0:T(128)} %copy-done.78) | copy-start | bytes 100
  893.7 24.2 %copy-start.82 = (f32[8,256]{1,0:T(8,128)S(1)}, f32[8,256]{1,0:T(8,128)}, u32[]{:S(2)}) copy-start(f32[8,256]{1,0:T(8,128)} %get-tuple-element.53) | copy-start | bytes 24580
  893.7 24.2 %copy-start.94 = (f32[8]{0:T(128)S(1)}, f32[8]{0:T(128)}, u32[]{:S(2)}) copy-start(f32[8]{0:T(128)} %copy-done.93) | copy-start | bytes 100
  1036.7 28.9 %copy-start.1 = (bf16[1024,1024]{1,0:T(8,128)(2,1)S(1)}, bf16[1024,1024]{1,0:T(8,128)(2,1)}, u32[]{:S(2)}) copy-start(bf16[1024,1024]{1,0:T(8,128)(2,1)} %param.42) | copy-start | bytes 6291460
  (77 other events, 396.4 us)
Sparse Core Ops, SparseCore 0:
  46.5 30.6 all-gather.20
  91.6 49.3 reduce-scatter.8
  450.9 69.4 reduce-scatter.12
  524.6 71.2 reduce-scatter.20
  599.4 115.9 reduce-scatter.16
  717.7 27.8 all-gather.26
  747.9 31.8 reduce-scatter.14
  782.1 27.8 reduce-scatter.22
  812.3 42.4 reduce-scatter.18
  859.9 75.2 all-reduce.16
  937.1 28.2 all-gather.14
  967.2 27.6 all-gather.18
  996.8 36.7 all-gather.16
  1036.2 27.1 reduce-scatter.10
Sparse Core Ops, SparseCore 1:
  95.7 121.9 all-gather.22
  221.0 152.8 all-gather.24

commit v2 on v1

--- a/solution.py
+++ b/solution.py
@@ -16,13 +16,14 @@
 DI = 2048
 GROUP = 8
 TILE = 128
-HIDDEN = 512
+PIECES = 2
 
 epsilon = 1e-05
 highest = lax.Precision.HIGHEST
 F32 = jnp.float32
 BF16 = jnp.bfloat16
-SEQ = ("g", "s")
+SEQ = ("g", "a", "b", "c")
+INNER = ("a", "b", "c")
 
 
 def mm(left, right):
@@ -49,6 +50,42 @@
 
 def whole(shape):
     return pl.BlockSpec(shape, lambda j: (0,) * len(shape))
+
+
+def scalar_spec():
+    return pl.BlockSpec(memory_space=pltpu.SMEM)
+
+
+def halves_shape(tps, depth, wide):
+    return jax.ShapeDtypeStruct((2, 2, tps, depth, wide), BF16)
+
+
+def halves_spec(depth, wide):
+    return pl.BlockSpec((2, 2, 1, depth, wide), lambda j: (0, 0, j, 0, 0))
+
+
+def anywhere():
+    return pl.BlockSpec(memory_space=pl.ANY)
+
+
+def weight_specs(weights, first):
+    parts, _, _, wide = weights.shape
+    block = (parts, 1, D // GROUP, wide)
+    return [
+        pl.BlockSpec(block, functools.partial(lambda k, j: (0, j, k, 0), first + k))
+        for k in range(3)
+    ]
+
+
+def attention_spec(weights):
+    parts, _, _, wide = weights.shape
+    return pl.BlockSpec((parts, 1, 2 * D // GROUP, wide), lambda j: (0, j, 0, 0))
+
+
+def attention_view(weight_ref, k, width):
+    deep = D // weight_ref.shape[0]
+    rows = slice((k % 2) * deep, (k % 2 + 1) * deep)
+    return weight_ref.at[:, 0, rows, (k // 2) * width : (k // 2 + 1) * width]
 
 
 def head_mask(width):
@@ -84,7 +121,6 @@
     step = pl.program_id(0)
     blocks, rows, width = embed_ref.shape
     parts = weight_ref.shape[0]
-    deep = D // parts
 
     @pl.when(step == 0)
     def _():
@@ -99,7 +135,7 @@
 
     normed = normed_ref[...]
     for k in range(3):
-        weight = weight_ref[:, 0, k * deep : (k + 1) * deep, :].reshape(D, width)
+        weight = attention_view(weight_ref, k, width)[...].reshape(D, width)
         qkv_ref[0, k] = mm(normed, weight).astype(BF16)
     masks = head_mask(width)
     heads = len(masks)
@@ -112,16 +148,16 @@
         context_ref[0, at] = mm(beside(probs, heads), values).astype(BF16)
     context = context_ref[0]
     piece = width // parts
+    outward = attention_view(weight_ref, 3, width)
     for c in range(D // width):
-        low = 3 * deep + c * piece
-        weight = weight_ref[:, 0, low : low + piece, :].reshape(width, width)
+        weight = outward[:, c * piece : (c + 1) * piece].reshape(width, width)
         cols = slice(c * width, (c + 1) * width)
         hidden_ref[:, cols] += mm(context, weight)
 
 
 def attention_forward(embed, global_rows, gain, weights):
     blocks, rows, width = embed.shape
-    parts, tps, depth, _ = weights.shape
+    tps = weights.shape[1]
     return pl.pallas_call(
         attention_forward_kernel,
         grid=(tps,),
@@ -129,7 +165,7 @@
             whole((blocks, rows, width)),
             whole((rows // PATCH, 1, D)),
             whole((1, D)),
-            pl.BlockSpec((parts, 1, depth, width), lambda j: (0, j, 0, 0)),
+            attention_spec(weights),
         ],
         out_specs=[
             whole((rows, D)),
@@ -153,64 +189,150 @@
     )(embed, global_rows, gain, weights)
 
 
-def feed_forward_kernel(
+def core_halves(core, grad):
+    parts = grad.reshape((2, 2, 2, grad.shape[0] // GROUP) + grad.shape[1:])
+    mine = jnp.where(core == 0, parts[:, :, 0], parts[:, :, 1])
+    other = jnp.where(core == 0, parts[:, :, 1], parts[:, :, 0])
+    return mine, other
+
+
+def put_halves(core, grad, own_ref, other_ref, low, high, cols=slice(None)):
+    own, other = core_halves(core, grad.astype(BF16))
+    own_ref[:, :, 0, low:high, cols] = own
+    other_ref[:, :, 0, low:high, cols] = other
+
+
+def put_whole(core, grad, grad_ref, low, high):
+    parts = grad_ref.shape[0]
+    grad_ref[:, 0, low:high] = grad.astype(BF16).reshape((parts, -1) + grad.shape[1:])
+
+
+def feed_forward_step(
+    core_ref, weight_refs, cot, normed_ref, turned_ref, out_acc, normed_acc, put
+):
+    parts, _, _, wide = weight_refs[0].shape
+    deep = D // parts
+    core = core_ref[0]
+    normed = normed_ref[...]
+    gate_weight = weight_refs[0][:, 0].reshape(D, wide)
+    up_weight = weight_refs[1][:, 0].reshape(D, wide)
+    piece = wide // parts
+    folds = D // wide
+    down_weight = jnp.concatenate(
+        [
+            weight_refs[2][:, 0, i * piece : (i + 1) * piece].reshape(wide, wide)
+            for i in range(folds)
+        ],
+        axis=1,
+    )
+    gate = mm(normed, gate_weight)
+    up = mm(normed, up_weight)
+    sigma = 1.0 / (1.0 + jnp.exp(-gate))
+    swish = gate * sigma
+    activ = (swish * up).astype(BF16)
+    out_acc[...] += mm(activ, down_weight)
+    shrink = mm_tn(activ, cot)
+    for i in range(folds):
+        low = 2 * deep + i * piece
+        put(core, shrink[:, i * wide : (i + 1) * wide], low, low + piece)
+    dactiv = mm_nt(cot, down_weight)
+    dgate = (dactiv * up * sigma * (1.0 + gate * (1.0 - sigma))).astype(BF16)
+    dup = (dactiv * swish).astype(BF16)
+    normed_acc[...] += mm_nt(dgate, gate_weight) + mm_nt(dup, up_weight)
+    turned = turned_ref[...]
+    put(core, mm(turned, dgate), 0, deep)
+    put(core, mm(turned, dup), deep, 2 * deep)
+
+
+def feed_forward_first_kernel(
+    core_ref,
     hidden_ref,
     cot_ref,
     gain_ref,
-    expand_ref,
-    shrink_ref,
-    layer_ref,
-    grad_ref,
-    gain_grad_ref,
-    expand_grad_ref,
-    shrink_grad_ref,
+    gate_ref,
+    up_ref,
+    down_ref,
     normed_ref,
     turned_ref,
-    cot_scratch,
+    cot_out,
     out_acc,
     normed_acc,
+    own_ref,
+    other_ref,
 ):
-    step = pl.program_id(0)
-    rows = hidden_ref.shape[0]
     blocks, _, width = cot_ref.shape
-    parts = expand_ref.shape[0]
-    deep = D // parts
-    wide = expand_ref.shape[-1]
-
-    @pl.when(step == 0)
+
+    @pl.when(pl.program_id(0) == 0)
     def _():
         values = hidden_ref[...].astype(BF16).astype(F32)
         normed = (values * inverse_rms(values) * gain_ref[...]).astype(BF16)
         normed_ref[...] = normed
         turned_ref[...] = normed.astype(F32).T.astype(BF16)
         for i in range(blocks):
-            cot_scratch[:, i * width : (i + 1) * width] = cot_ref[i]
-        out_acc[...] = jnp.zeros_like(out_acc)
+            cot_out[:, i * width : (i + 1) * width] = cot_ref[i]
+        out_acc[...] = hidden_ref[...]
         normed_acc[...] = jnp.zeros_like(normed_acc)
 
-    normed = normed_ref[...]
-    cot = cot_scratch[...]
-    gate_weight = expand_ref[:, 0, :deep, :].reshape(D, wide)
-    up_weight = expand_ref[:, 0, deep:, :].reshape(D, wide)
-    down_weight = shrink_ref[...].reshape(wide, D)
-    gate = mm(normed, gate_weight)
-    up = mm(normed, up_weight)
-    sigma = 1.0 / (1.0 + jnp.exp(-gate))
-    swish = gate * sigma
-    activ = (swish * up).astype(BF16)
-    out_acc[...] += mm(activ, down_weight)
-    shrink_grad_ref[...] = mm_tn(activ, cot).astype(BF16).reshape(shrink_grad_ref.shape)
-    dactiv = mm_nt(cot, down_weight)
-    dgate = (dactiv * up * sigma * (1.0 + gate * (1.0 - sigma))).astype(BF16)
-    dup = (dactiv * swish).astype(BF16)
-    normed_acc[...] += mm_nt(dgate, gate_weight) + mm_nt(dup, up_weight)
-    turned = turned_ref[...]
-    expand_grad_ref[:, 0, :deep, :] = mm(turned, dgate).astype(BF16).reshape(parts, deep, wide)
-    expand_grad_ref[:, 0, deep:, :] = mm(turned, dup).astype(BF16).reshape(parts, deep, wide)
+    def put(core, grad, low, high):
+        put_halves(core, grad, own_ref, other_ref, low, high)
+
+    feed_forward_step(
+        core_ref,
+        (gate_ref, up_ref, down_ref),
+        cot_out[...],
+        normed_ref,
+        turned_ref,
+        out_acc,
+        normed_acc,
+        put,
+    )
+
+
+def feed_forward_last_kernel(
+    core_ref,
+    hidden_ref,
+    cot_ref,
+    gain_ref,
+    gate_ref,
+    up_ref,
+    down_ref,
+    normed_ref,
+    turned_ref,
+    out_in,
+    normed_in,
+    token_ref,
+    layer_ref,
+    grad_ref,
+    gain_grad_ref,
+    weight_grad_ref,
+    out_acc,
+    normed_acc,
+):
+    step = pl.program_id(0)
+    blocks, _, width = layer_ref.shape
+
+    @pl.when(step == 0)
+    def _():
+        out_acc[...] = out_in[...]
+        normed_acc[...] = normed_in[...]
+
+    def put(core, grad, low, high):
+        put_whole(core, grad, weight_grad_ref, low, high)
+
+    feed_forward_step(
+        core_ref,
+        (gate_ref, up_ref, down_ref),
+        cot_ref[...],
+        normed_ref,
+        turned_ref,
+        out_acc,
+        normed_acc,
+        put,
+    )
 
     @pl.when(step == pl.num_programs(0) - 1)
     def _():
-        layer = (hidden_ref[...] + out_acc[...]).astype(BF16)
+        layer = out_acc[...].astype(BF16)
         for i in range(blocks):
             layer_ref[i] = layer[:, i * width : (i + 1) * width]
         values = hidden_ref[...].astype(BF16).astype(F32)
@@ -220,57 +342,99 @@
         gain_grad_ref[...] = jnp.sum(grad * normal, axis=0, keepdims=True)
         scaled = grad * gain_ref[...]
         back = scale * (scaled - normal * jnp.mean(scaled * normal, axis=-1, keepdims=True))
-        grad_ref[...] = cot_scratch[...].astype(F32) + back
-
-
-def feed_forward(hidden, cot, gain, weights):
+        grad_ref[...] = cot_ref[...].astype(F32) + back
+
+
+def feed_forward_cost(rows, weights):
+    _, tps, _, wide = weights.shape
+    return pl.CostEstimate(
+        flops=18 * rows * D * wide * tps,
+        bytes_accessed=12 * D * wide * tps + 16 * rows * D,
+        transcendentals=rows * wide * tps,
+    )
+
+
+def feed_forward_first(core, hidden, cot, gain, weights):
     rows = hidden.shape[0]
-    blocks, _, width = cot.shape
-    parts, tps, depth, total = weights.shape
-    deep = D // parts
-    wide = HIDDEN
-    count = total // wide
-    held = wide // deep
+    _, tps, _, wide = weights.shape
+    depth = 3 * D // GROUP
     return pl.pallas_call(
-        feed_forward_kernel,
-        grid=(tps * count,),
+        feed_forward_first_kernel,
+        grid=(tps,),
         in_specs=[
-            whole((rows, D)),
-            whole((blocks, rows, width)),
+            scalar_spec(),
+            whole((rows, D)),
+            whole(cot.shape),
             whole((1, D)),
-            pl.BlockSpec((parts, 1, 2 * deep, wide), lambda j: (0, j // count, 0, j % count)),
-            pl.BlockSpec((held, 1, deep, D), lambda j: (j % count, j // count, 2, 0)),
+            *weight_specs(weights, 2),
         ],
         out_specs=[
-            whole((blocks, rows, width)),
+            whole((rows, D)),
+            whole((D, rows)),
+            whole((rows, D)),
+            whole((rows, D)),
+            whole((rows, D)),
+            halves_spec(depth, wide),
+            halves_spec(depth, wide),
+        ],
+        out_shape=[
+            jax.ShapeDtypeStruct((rows, D), BF16),
+            jax.ShapeDtypeStruct((D, rows), BF16),
+            jax.ShapeDtypeStruct((rows, D), BF16),
+            jax.ShapeDtypeStruct((rows, D), F32),
+            jax.ShapeDtypeStruct((rows, D), F32),
+            halves_shape(tps, depth, wide),
+            halves_shape(tps, depth, wide),
+        ],
+        compiler_params=params(),
+        name="feed_forward_first",
+        cost_estimate=feed_forward_cost(rows, weights),
+    )(core, hidden, cot, gain, weights, weights, weights)
+
+
+def feed_forward_last(
+    core, hidden, cot, gain, weights, normed, turned, out_in, normed_in, token
+):
+    rows = hidden.shape[0]
+    _, tps, _, wide = weights.shape
+    depth = 3 * D // GROUP
+    width = D // tps
+    return pl.pallas_call(
+        feed_forward_last_kernel,
+        grid=(tps,),
+        in_specs=[
+            scalar_spec(),
+            whole((rows, D)),
             whole((rows, D)),
             whole((1, D)),
-            pl.BlockSpec((parts, 1, 2 * deep, wide), lambda j: (0, j // count, 0, j % count)),
-            pl.BlockSpec((held, 1, deep, D), lambda j: (j % count, j // count, 0, 0)),
+            *weight_specs(weights, 0),
+            whole((rows, D)),
+            whole((D, rows)),
+            whole((rows, D)),
+            whole((rows, D)),
+            anywhere(),
+        ],
+        out_specs=[
+            whole((tps, rows, width)),
+            whole((rows, D)),
+            whole((1, D)),
+            pl.BlockSpec((GROUP, 1, depth, wide), lambda j: (0, j, 0, 0)),
         ],
         out_shape=[
-            jax.ShapeDtypeStruct((blocks, rows, width), BF16),
+            jax.ShapeDtypeStruct((tps, rows, width), BF16),
             jax.ShapeDtypeStruct((rows, D), F32),
             jax.ShapeDtypeStruct((1, D), F32),
-            jax.ShapeDtypeStruct((parts, tps, 2 * deep, total), BF16),
-            jax.ShapeDtypeStruct((parts, tps, deep, D), BF16),
-        ],
-        scratch_shapes=[
-            pltpu.VMEM((rows, D), BF16),
-            pltpu.VMEM((D, rows), BF16),
-            pltpu.VMEM((rows, D), BF16),
-            pltpu.VMEM((rows, D), F32),
-            pltpu.VMEM((rows, D), F32),
-        ],
+            jax.ShapeDtypeStruct((GROUP, tps, depth, wide), BF16),
+        ],
+        scratch_shapes=[pltpu.VMEM((rows, D), F32), pltpu.VMEM((rows, D), F32)],
         compiler_params=params(),
-        name="feed_forward",
-        cost_estimate=pl.CostEstimate(
-            flops=18 * rows * D * total * tps, bytes_accessed=56 << 20, transcendentals=rows * total * tps
-        ),
-    )(hidden, cot, gain, weights, weights)
+        name="feed_forward_last",
+        cost_estimate=feed_forward_cost(rows, weights),
+    )(core, hidden, cot, gain, weights, weights, weights, normed, turned, out_in, normed_in, token)
 
 
 def attention_backward_kernel(
+    core_ref,
     grad_ref,
     mixer_ref,
     input_ref,
@@ -279,11 +443,14 @@
     weight_ref,
     qkv_ref,
     context_ref,
+    token_ref,
+    layer_token_ref,
     embed_ref,
     global_ref,
     dot_ref,
     gain_grad_ref,
-    weight_grad_ref,
+    own_ref,
+    other_ref,
     turned_ref,
     low_ref,
     normed_acc,
@@ -296,6 +463,7 @@
     parts = weight_ref.shape[0]
     deep = D // parts
     scaling = (D // HEADS_A) ** -0.5
+    core = core_ref[0]
 
     @pl.when(step == 0)
     def _():
@@ -307,13 +475,21 @@
     context = context_ref[0]
     piece = width // parts
     total = jnp.zeros((rows, width), F32)
+    outward = attention_view(weight_ref, 3, width)
     for c in range(D // width):
-        first = 3 * deep + c * piece
-        weight = weight_ref[:, 0, first : first + piece, :].reshape(width, width)
+        first = deep + c * piece
+        weight = outward[:, c * piece : (c + 1) * piece].reshape(width, width)
         columns = low[:, c * width : (c + 1) * width]
         total = total + mm_nt(columns, weight)
-        grad = mm_tn(context, columns).astype(BF16)
-        weight_grad_ref[:, 0, first : first + piece, :] = grad.reshape(parts, piece, width)
+        put_halves(
+            core,
+            mm_tn(context, columns),
+            own_ref,
+            other_ref,
+            first,
+            first + piece,
+            slice(width, 2 * width),
+        )
     context_grad_ref[...] = total.astype(BF16)
     masks = head_mask(width)
     heads = len(masks)
@@ -336,10 +512,18 @@
     turned = turned_ref[...]
     for k in range(3):
         part = qkv_grad_ref[:, k * width : (k + 1) * width]
-        weight = weight_ref[:, 0, k * deep : (k + 1) * deep, :].reshape(D, width)
+        weight = attention_view(weight_ref, k, width)[...].reshape(D, width)
         normed_acc[...] += mm_nt(part, weight)
-        grad = mm(turned, part).astype(BF16)
-        weight_grad_ref[:, 0, k * deep : (k + 1) * deep, :] = grad.reshape(parts, deep, width)
+        first = (k % 2) * deep
+        put_halves(
+            core,
+            mm(turned, part),
+            own_ref,
+            other_ref,
+            first,
+            first + deep,
+            slice((k // 2) * width, (k // 2 + 1) * width),
+        )
 
     @pl.when(step == pl.num_programs(0) - 1)
     def _():
@@ -358,35 +542,41 @@
         dot_ref[...] = jnp.sum(patch * mixer_ref[...], axis=1, keepdims=True)
 
 
-def attention_backward(grad, mixer_rows, inputs, normed, gain, weights, qkv, context):
+def attention_backward(core, grad, mixer_rows, inputs, normed, gain, weights, qkv, context, tokens):
     rows = grad.shape[0]
-    parts, tps, depth, width = weights.shape
+    tps, _, width = context.shape
+    depth = 2 * D // GROUP
     return pl.pallas_call(
         attention_backward_kernel,
         grid=(tps,),
         in_specs=[
+            scalar_spec(),
             whole((rows, D)),
             whole((rows // PATCH, D)),
             whole((rows, D)),
             whole((rows, D)),
             whole((1, D)),
-            pl.BlockSpec((parts, 1, depth, width), lambda j: (0, j, 0, 0)),
+            attention_spec(weights),
             pl.BlockSpec((1, 3, rows, width), lambda j: (j, 0, 0, 0)),
             pl.BlockSpec((1, rows, width), lambda j: (j, 0, 0)),
+            anywhere(),
+            anywhere(),
         ],
         out_specs=[
             whole((tps, rows, width)),
             whole((rows // PATCH, D)),
             whole((rows // PATCH, 1)),
             whole((1, D)),
-            pl.BlockSpec((parts, 1, depth, width), lambda j: (0, j, 0, 0)),
+            halves_spec(depth, 2 * width),
+            halves_spec(depth, 2 * width),
         ],
         out_shape=[
             jax.ShapeDtypeStruct((tps, rows, width), BF16),
             jax.ShapeDtypeStruct((rows // PATCH, D), F32),
             jax.ShapeDtypeStruct((rows // PATCH, 1), F32),
             jax.ShapeDtypeStruct((1, D), F32),
-            jax.ShapeDtypeStruct((parts, tps, depth, width), BF16),
+            halves_shape(tps, depth, 2 * width),
+            halves_shape(tps, depth, 2 * width),
         ],
         scratch_shapes=[
             pltpu.VMEM((D, rows), BF16),
@@ -400,7 +590,7 @@
         cost_estimate=pl.CostEstimate(
             flops=4 * rows * D * D * 4, bytes_accessed=26 << 20, transcendentals=rows * 2048
         ),
-    )(grad, mixer_rows, inputs, normed, gain, weights, qkv, context)
+    )(core, grad, mixer_rows, inputs, normed, gain, weights, qkv, context, *tokens)
 
 
 def shifted(block, distance):
@@ -478,32 +668,165 @@
     return (result, jnp.sum(grad * normed, axis=0))
 
 
-def chained(factors, states, here, reverse):
-    count = factors.shape[0]
-    order = jnp.arange(count)
-    source, between = order[:, None], order[None, :]
-    if reverse:
-        crossed = (between > here) & (between < source)
-        reaching = order > here
-    else:
-        crossed = (between < here) & (between > source)
-        reaching = order < here
-    chain = jnp.prod(jnp.where(crossed[:, :, None], factors[None], 1.0), axis=1)
-    chain = chain * reaching[:, None].astype(F32)
-    return jnp.sum(chain[:, :, None, None] * states, axis=0)
-
-
-def spread_shard(array):
-    size = array.shape[0] // GROUP
-    return lax.dynamic_slice_in_dim(array, lax.axis_index("s") * size, size, 0)
-
-
-def reduce_pieces(grads):
-    own = lax.psum_scatter(grads, "s", scatter_dimension=0)
-    own = lax.psum_scatter(own, "tp", scatter_dimension=0)
+def high_low(values):
+    high = values.astype(BF16)
+    low = (values - high.astype(F32)).astype(BF16)
+    return high, low
+
+
+def reached(factors, states, distance):
+    count = lax.axis_size(SEQ)
+    heads = factors.shape[0]
+    columns = jnp.broadcast_to(factors[:, None], (heads, STATE))
+    high, low = high_low(columns)
+    packed = jnp.concatenate([states.reshape(-1, STATE).astype(BF16), high, low], axis=0)
+    total = jnp.zeros(states.shape, F32)
+    chain = jnp.ones((heads, 1, 1), F32)
+    for hop in range(1, count // 2 + 1):
+        step = hop * distance
+        route = [(i, i + step) for i in range(count) if 0 <= i + step < count]
+        got = lax.ppermute(packed, SEQ, route).astype(F32)
+        total = total + chain * got[: -2 * heads].reshape(states.shape)
+        factor = (got[-2 * heads : -heads] + got[-heads:])[:, :1]
+        chain = chain * factor[:, :, None]
+    return total
+
+
+def tied(array, *tokens):
+    zero = sum(t[(0,) * t.ndim].astype(F32) * 0.0 for t in tokens)
+    return (array.astype(F32) + zero).astype(array.dtype)
+
+
+def swap(array, axis):
+    return lax.ppermute(array, axis, [(0, 1), (1, 0)])
+
+
+def picked(array, axis, index):
+    return lax.dynamic_index_in_dim(array, index, axis, False)
+
+
+def parallel_params(axes):
+    return pltpu.CompilerParams(
+        dimension_semantics=("arbitrary",) * axes, vmem_limit_bytes=32 * 1024 * 1024
+    )
+
+
+def first_sum_kernel(place_ref, *refs):
+    ins, outs = refs[:8], refs[-4:]
+    for k in range(4):
+        total = ins[2 * k][...].astype(F32) + ins[2 * k + 1][...].astype(F32)
+        outs[k][...] = total.reshape(outs[k].shape).astype(BF16)
+
+
+def first_sum(place, own, got, tokens=()):
+    _, _, tps, rows, cols = own.shape
+    half = rows // 2
+    block = (1, 1, 1, half, cols)
+    maps = [
+        lambda t, i, p: (i, 1 - p[1], t, 0, 0),
+        lambda t, i, p: (i, p[1], t, 0, 0),
+        lambda t, i, p: (1 - p[0], i, t, 1, 0),
+        lambda t, i, p: (p[0], i, t, 1, 0),
+    ]
+    specs = [pl.BlockSpec(block, m) for m in maps for _ in range(2)]
+    return pl.pallas_call(
+        first_sum_kernel,
+        grid_spec=pltpu.PrefetchScalarGridSpec(
+            num_scalar_prefetch=1,
+            grid=(tps, 2),
+            in_specs=specs + [anywhere() for _ in tokens],
+            out_specs=[
+                pl.BlockSpec((1, 1, half, cols), lambda t, i, p: (i, t, 0, 0)) for _ in range(4)
+            ],
+        ),
+        out_shape=[jax.ShapeDtypeStruct((2, tps, half, cols), BF16) for _ in range(4)],
+        compiler_params=parallel_params(2),
+        name="first_sum",
+        cost_estimate=pl.CostEstimate(
+            flops=own.size, bytes_accessed=6 * own.size, transcendentals=0
+        ),
+    )(place, *([own, got] * 4), *tokens)
+
+
+def second_sum_kernel(place_ref, *refs):
+    ins, outs = refs[:8], refs[-4:]
+    for k in range(4):
+        total = ins[2 * k][...].astype(F32) + ins[2 * k + 1][...].astype(F32)
+        outs[k][...] = total.reshape(outs[k].shape).astype(BF16)
+
+
+def second_sum(place, kept_one, got_one, kept_two, got_two, tokens=()):
+    _, tps, half, cols = kept_one.shape
+    block = (1, 1, half, cols)
+    maps = [
+        lambda t, p: (1 - p[0], t, 0, 0),
+        lambda t, p: (p[0], t, 0, 0),
+        lambda t, p: (1 - p[1], t, 0, 0),
+        lambda t, p: (p[1], t, 0, 0),
+    ]
+    return pl.pallas_call(
+        second_sum_kernel,
+        grid_spec=pltpu.PrefetchScalarGridSpec(
+            num_scalar_prefetch=1,
+            grid=(tps,),
+            in_specs=[pl.BlockSpec(block, m) for m in maps for _ in range(2)]
+            + [anywhere() for _ in tokens],
+            out_specs=[pl.BlockSpec((1, half, cols), lambda t, p: (t, 0, 0)) for _ in range(4)],
+        ),
+        out_shape=[jax.ShapeDtypeStruct((tps, half, cols), BF16) for _ in range(4)],
+        compiler_params=parallel_params(1),
+        name="second_sum",
+        cost_estimate=pl.CostEstimate(
+            flops=2 * kept_one.size, bytes_accessed=12 * kept_one.size, transcendentals=0
+        ),
+    )(place, *([kept_one, got_one] * 2), *([kept_two, got_two] * 2), *tokens)
+
+
+def third_sum_kernel(one_ref, two_ref, three_ref, four_ref, *refs):
+    out_ref = refs[-1]
+    half = one_ref.shape[1]
+    out_ref[0, :half] = (one_ref[0].astype(F32) + two_ref[0].astype(F32)).astype(BF16)
+    out_ref[0, half:] = (three_ref[0].astype(F32) + four_ref[0].astype(F32)).astype(BF16)
+
+
+def third_sum(kept_one, got_one, kept_two, got_two, tokens=()):
+    tps, half, cols = kept_one.shape
+    return pl.pallas_call(
+        third_sum_kernel,
+        grid=(tps,),
+        in_specs=[pl.BlockSpec((1, half, cols), lambda t: (t, 0, 0)) for _ in range(4)]
+        + [anywhere() for _ in tokens],
+        out_specs=pl.BlockSpec((1, 2 * half, cols), lambda t: (t, 0, 0)),
+        out_shape=jax.ShapeDtypeStruct((tps, 2 * half, cols), BF16),
+        compiler_params=parallel_params(1),
+        name="third_sum",
+        cost_estimate=pl.CostEstimate(
+            flops=2 * kept_one.size, bytes_accessed=12 * kept_one.size, transcendentals=0
+        ),
+    )(kept_one, got_one, kept_two, got_two, *tokens)
+
+
+def reduce_first(place, own, other, tokens=()):
+    return first_sum(place, own, swap(other, "c"), tokens)
+
+
+def reduce_second(place, sums, tokens=()):
+    send_one, keep_one, send_two, keep_two = sums
+    return second_sum(
+        place, keep_one, swap(send_one, "b"), keep_two, swap(send_two, "a"), tokens
+    )
+
+
+def reduce_third(sums, tokens=()):
+    send_one, keep_one, send_two, keep_two = sums
+    return third_sum(keep_one, swap(send_one, "a"), keep_two, swap(send_two, "b"), tokens)
+
+
+def reduce_last(summed):
+    part = lax.psum_scatter(summed, "tp", scatter_dimension=0)
     if lax.axis_size("g") > 1:
-        own = lax.psum(own, "g")
-    return lax.all_gather(own, "s")
+        part = lax.psum(part, "g")
+    return lax.all_gather(part, INNER)
 
 
 def shards(
@@ -533,7 +856,8 @@
     count, quarter = patches.shape
     tps = lax.axis_size("tp")
     mine = lax.axis_index("tp")
-    here = lax.axis_index("g") * lax.axis_size("s") + lax.axis_index("s")
+    here = lax.axis_index(SEQ)
+    core = lax.axis_index("c").reshape(1)
     tail = CONV - 1
     inner_width = proj_inner.shape[1]
     share = count // tps
@@ -541,20 +865,42 @@
     rows = total_rows // tps
 
     narrow = D // GROUP
-    slot = lax.axis_index("s")
+    slot = lax.axis_index(INNER)
+
+    def gather_weights(part):
+        return lax.all_gather(part, INNER + ("tp",)).reshape((GROUP, tps) + part.shape)
+
+    def folded(array, width):
+        rows_in = array.shape[0]
+        return array.reshape(rows_in, -1, width).transpose(1, 0, 2).reshape(-1, width)
+
+    def unfolded(array, folds):
+        blocks = array.reshape(GROUP, folds, -1, array.shape[-1])
+        return blocks.transpose(0, 2, 1, 3).reshape(-1, folds * array.shape[-1])
+
     attn_in_part = lax.dynamic_slice_in_dim(attn_input, slot * narrow, narrow, 1)
-    attn_out_part = spread_shard(attn_output)
-    attn_out_part = attn_out_part.reshape(-1, tps, quarter).transpose(1, 0, 2)
-    attn_part = jnp.concatenate(
-        [attn_in_part.reshape(-1, quarter), attn_out_part.reshape(-1, quarter)], axis=0
-    )
-    attn_weights = lax.all_gather(attn_part, ("s", "tp")).reshape(GROUP, tps, -1, quarter)
+    out_rows = attn_output.shape[0] // GROUP
+    attn_out_part = lax.dynamic_slice_in_dim(attn_output, slot * out_rows, out_rows, 0)
+    attn_out_part = folded(attn_out_part, quarter)
     hidden_width = expand_weight.shape[2]
-    expand_part = lax.dynamic_slice_in_dim(expand_weight, slot * narrow, narrow, 1)
-    ffn_part = jnp.concatenate(
-        [expand_part.reshape(-1, hidden_width), spread_shard(shrink_weight)], axis=0
-    )
-    ffn_weights = lax.all_gather(ffn_part, ("s", "tp")).reshape(GROUP, tps, -1, hidden_width)
+    wide = hidden_width // PIECES
+    down_rows = wide // GROUP
+    ffn_parts = []
+    for p in range(PIECES):
+        up_part = lax.dynamic_slice(
+            expand_weight, (0, slot * narrow, p * wide), (2, narrow, wide)
+        )
+        down_part = lax.dynamic_slice_in_dim(
+            shrink_weight, p * wide + slot * down_rows, down_rows, 0
+        )
+        ffn_parts.append([up_part.reshape(-1, wide), folded(down_part, wide)])
+    attn_parts = [
+        jnp.concatenate([attn_in_part[0], attn_in_part[2]], axis=1),
+        jnp.concatenate([attn_in_part[1], attn_out_part], axis=1),
+    ]
+    weights = gather_weights(jnp.concatenate(attn_parts + ffn_parts[0], axis=0))
+    last_weights = gather_weights(jnp.concatenate(ffn_parts[1], axis=0))
+    place = jnp.stack([lax.axis_index("a"), lax.axis_index("b")]).astype(jnp.int32)
 
     def to_rows(array):
         return lax.all_to_all(array.reshape(tps, rows, quarter), "tp", 0, 0)
@@ -595,8 +941,7 @@
     inner_vals, bmatrix, cmatrix, steps, rates = front_vals
     summary, summary_pull = jax.vjp(summary_local, inner_vals, bmatrix, steps, rates)
     carried, states = summary
-    all_carried = lax.all_gather(carried, SEQ)
-    incoming = chained(all_carried, lax.all_gather(states, SEQ), here, False)
+    incoming = reached(carried, states, 1)
     mixed, output_pull = jax.vjp(
         output_local, inner_vals, bmatrix, cmatrix, steps, rates, skip_gain, incoming
     )
@@ -604,42 +949,71 @@
     gated = mixed * gate_act
     squares = jnp.sum(gated * gated, axis=1, keepdims=True)
     partial = product((gated * mixer_gain[None, :]).astype(BF16), proj_mixer, "rc,cd->rd")
-    summed = lax.psum_scatter(
-        jnp.concatenate([partial, jnp.broadcast_to(squares, (count, 128))], axis=1),
-        "tp",
-        scatter_dimension=0,
-        tiled=True,
-    )
-    own_squares = summed[:, D : D + 1]
+    square_high, square_low = high_low(jnp.broadcast_to(squares, (count, 64)))
+    partial = partial + embed_rows[0, 0, 0].astype(F32) * 0.0
+    sent = jnp.concatenate([partial.astype(BF16), square_high, square_low], axis=1)
+    summed = jnp.sum(
+        lax.all_to_all(sent.reshape(tps, share, -1), "tp", 0, 0).astype(F32), axis=0
+    )
+    own_squares = summed[:, D : D + 1] + summed[:, D + 64 : D + 65]
     mixer_rows = summed[:, :D] * lax.rsqrt(own_squares / DI + epsilon)
     own_patches = lax.dynamic_slice_in_dim(patch_rows, mine * share, share, 0)
     global_out = own_patches.astype(F32) + mixer_rows
 
     hidden, attn_in, attn_normed, qkv, context = attention_forward(
-        embed_rows, global_out[:, None, :], norm_attn[None, :], attn_weights
-    )
-    layer_blocks, hidden_grad, norm_ffn_part, expand_part, shrink_part = feed_forward(
-        hidden, cot_rows, norm_ffn[None, :], ffn_weights
+        embed_rows, global_out[:, None, :], norm_attn[None, :], weights
+    )
+    ffn_normed, ffn_turned, cot_whole, out_acc, normed_acc, own_first, other_first = (
+        feed_forward_first(core, hidden, cot_rows, norm_ffn[None, :], weights)
+    )
+    first_one = reduce_first(place, own_first, other_first)
+    first_two = reduce_second(place, first_one)
+    layer_blocks, hidden_grad, norm_ffn_part, last_grad = feed_forward_last(
+        core,
+        hidden,
+        cot_whole,
+        norm_ffn[None, :],
+        last_weights,
+        ffn_normed,
+        ffn_turned,
+        out_acc,
+        normed_acc,
+        first_two[0],
     )
     layer_output = to_columns(layer_blocks)
-    embed_blocks, own_grad, row_dot, norm_attn_part, attn_part = attention_backward(
-        hidden_grad, mixer_rows, attn_in, attn_normed, norm_attn[None, :], attn_weights, qkv, context
-    )
-    shrink_grad = reduce_pieces(shrink_part).reshape(-1, D).astype(F32)
-    expand_grad = reduce_pieces(expand_part).reshape(GROUP, 2, narrow, hidden_width)
-    expand_grad = expand_grad.transpose(1, 0, 2, 3).reshape(2, D, hidden_width).astype(F32)
-    attn_grad = reduce_pieces(attn_part)
-    attn_input_grad = attn_grad[:, : 3 * narrow].reshape(GROUP, 3, narrow, quarter)
-    attn_input_grad = attn_input_grad.transpose(1, 0, 2, 3).reshape(3, D, quarter).astype(F32)
-    attn_output_grad = attn_grad[:, 3 * narrow :].reshape(GROUP, tps, -1, quarter)
-    attn_output_grad = attn_output_grad.transpose(0, 2, 1, 3).reshape(quarter, D).astype(F32)
+    first_three = reduce_third(first_two, (hidden_grad,))
+    embed_blocks, own_grad, row_dot, norm_attn_part, own_attn, other_attn = attention_backward(
+        core,
+        hidden_grad,
+        mixer_rows,
+        attn_in,
+        attn_normed,
+        norm_attn[None, :],
+        weights,
+        qkv,
+        context,
+        (first_three, layer_output),
+    )
+    last_three = lax.psum_scatter(last_grad, INNER, scatter_dimension=0)
+    attn_one = reduce_first(place, own_attn, other_attn)
     embed_grad = to_columns(embed_blocks).astype(F32)
 
-    extras = jnp.concatenate([own_squares, row_dot], axis=1)
-    mix_back_in = lax.all_gather(own_grad.astype(BF16), "tp", axis=0, tiled=True)
-    all_extras = lax.all_gather(extras, "tp", axis=0, tiled=True)
-    row_scale = lax.rsqrt(all_extras[:, :1] / DI + epsilon)
-    row_mean = all_extras[:, 1:] / DI
+    extra_high, extra_low = high_low(
+        jnp.concatenate(
+            [jnp.broadcast_to(v, (share, 32)) for v in (own_squares, row_dot)], axis=1
+        )
+    )
+    returned = lax.all_gather(
+        jnp.concatenate([own_grad.astype(BF16), extra_high, extra_low], axis=1),
+        "tp",
+        axis=0,
+        tiled=True,
+    )
+    mix_back_in = returned[:, :D]
+    extras = returned[:, D : D + 64].astype(F32) + returned[:, D + 64 :].astype(F32)
+    all_squares, all_dots = tied(extras[:, :1], attn_one[0]), extras[:, 32:33]
+    row_scale = lax.rsqrt(all_squares / DI + epsilon)
+    row_mean = all_dots / DI
     normed_mix = gated * row_scale
     mix_low = (normed_mix * mixer_gain[None, :]).astype(jnp.bfloat16)
     proj_mixer_grad = product(mix_low, mix_back_in, "rc,rd->cd")
@@ -653,7 +1027,10 @@
     inner_one, bmat_one, cmat_one, steps_one, rates_one, skip_gain_grad, incoming_grad = (
         output_pull(mixed_grad)
     )
-    later_grad = chained(all_carried, lax.all_gather(incoming_grad, SEQ), here, True)
+    attn_two = reduce_second(place, attn_one, (incoming_grad,))
+    attn_three = reduce_third(attn_two)
+    later_grad = reached(carried, tied(incoming_grad, attn_two[0]), -1)
+    later_grad = tied(later_grad, attn_three)
     carried_grad = jnp.sum(later_grad * incoming, axis=(1, 2))
     inner_two, bmat_two, steps_two, rates_two = summary_pull((carried_grad, later_grad))
     padded_grad, step_raw_grad, conv_grad, step_bias_grad, decay_log_grad = front_pull(
@@ -687,27 +1064,53 @@
         mine * share,
         0,
     )
-    patch_grad = lax.psum_scatter(part_in_grad, "tp", scatter_dimension=1, tiled=True)
-    state_all = lax.all_gather(state_back, "tp")
-    state_sum = jnp.sum(state_all.astype(F32), axis=0).astype(BF16)
-    shared = lax.psum(
-        (
-            conv_grad[:, inner_width:],
+    shared = jnp.concatenate(
+        [
+            conv_grad[:, inner_width:].reshape(-1),
             norm_attn_part[0],
             norm_ffn_part[0],
             norm_global_part,
+        ]
+    ).reshape(-1, quarter)
+    shared_high, shared_low = high_low(shared)
+    shared_rows = jnp.concatenate([shared_high, shared_low], axis=0)
+    columns = part_in_grad.astype(BF16).reshape(count, tps, quarter).transpose(1, 0, 2)
+    returned = lax.all_to_all(
+        jnp.concatenate(
+            [columns, jnp.broadcast_to(shared_rows[None], (tps,) + shared_rows.shape)], axis=1
         ),
         "tp",
-    )
-    proj_grads = lax.psum(
+        0,
+        0,
+    )
+    returned = jnp.sum(returned.astype(F32), axis=0)
+    patch_grad = returned[:count]
+    shared = returned[count : count + shared.shape[0]] + returned[count + shared.shape[0] :]
+    shared = shared.reshape(-1)
+    held = conv_state.size
+    shared = (
+        shared[:held].reshape(conv_state.shape),
+        shared[held : held + D],
+        shared[held + D : held + 2 * D],
+        shared[held + 2 * D :],
+    )
+    state_all = lax.all_gather(state_back, "tp")
+    state_sum = jnp.sum(state_all.astype(F32), axis=0).astype(BF16)
+    early_grads = lax.psum(
         (
             product(normed, gate_back, "rd,rc->dc").astype(BF16),
-            product(normed, inner_back, "rd,rc->dc").astype(BF16),
-            product(normed, state_sum, "rd,rc->dc").astype(BF16),
             proj_mixer_grad.astype(BF16),
         ),
         SEQ,
     )
+    late_grads = lax.psum(
+        (
+            product(normed, inner_back, "rd,rc->dc").astype(BF16),
+            product(normed, state_sum, "rd,rc->dc").astype(BF16),
+        ),
+        SEQ,
+    )
+    proj_grads = (early_grads[0], late_grads[0], late_grads[1], early_grads[1])
     proj_gate_grad, proj_inner_grad, proj_state_grad, proj_mixer_grad = (
         g.astype(F32) for g in proj_grads
     )
@@ -734,6 +1137,27 @@
         ),
         SEQ,
     )
+    ffn_depth, attn_depth = 3 * narrow, 2 * narrow
+    all_grads = reduce_last(jnp.concatenate([first_three, last_three, attn_three], axis=1))
+    ffn_grads = [all_grads[:, i * ffn_depth : (i + 1) * ffn_depth] for i in range(PIECES)]
+    attn_grad = all_grads[:, PIECES * ffn_depth :]
+    expand_grad = jnp.concatenate(
+        [
+            g[:, : 2 * narrow].reshape(GROUP, 2, narrow, wide).transpose(1, 0, 2, 3).reshape(2, D, wide)
+            for g in ffn_grads
+        ],
+        axis=2,
+    ).astype(F32)
+    shrink_grad = jnp.concatenate(
+        [unfolded(g[:, 2 * narrow :], D // wide) for g in ffn_grads], axis=0
+    ).astype(F32)
+    attn_input_grad = jnp.stack(
+        [
+            attn_grad[:, (k % 2) * narrow : (k % 2 + 1) * narrow, (k // 2) * quarter : (k // 2 + 1) * quarter]
+            for k in range(3)
+        ]
+    ).reshape(3, D, quarter).astype(F32)
+    attn_output_grad = unfolded(attn_grad[:, narrow:, quarter:], D // quarter).astype(F32)
     return (
         layer_output,
         embed_grad,
@@ -761,7 +1185,7 @@
 
 def solution(mesh):
     seq, tps = mesh.shape["seq"], mesh.shape["tp"]
-    fine = Mesh(mesh.devices.reshape(seq // GROUP, GROUP, tps), ("g", "s", "tp"))
+    fine = Mesh(mesh.devices.reshape(seq // GROUP, 2, 2, 2, tps), SEQ + ("tp",))
     rows_cols = P(SEQ, "tp")
     last = P(None, "tp")
     lead = P("tp", None)

time: 1080 us -> 739 us (0.68)
  waiting for transfers between devices: 636 us -> 292 us
  blocking collectives: 191 us -> 102 us
  starting transfers between devices: 10.9 us -> 50.5 us
  local copies, waits for them, and re-layouts: 33.6 us -> 60.5 us
  Pallas kernels: 91.6 us -> 113 us
    reduce_scatter x8 -> x2, waiting for transfers between devices: 322 us -> 1.77 us  [the longest x1 1.77 us: reduce_last(): part = lax.psum_scatter(summed, 'tp', scatter_dimension=0)]
    all_gather x7 -> x3, waiting for transfers between devices: 291 us -> 128 us  [the longest x2 78.9 us: gather_weights(): lax.all_gather(part, INNER + ('tp',)).reshape((GROUP, tps) + part.shape)]
    ppermute x0 -> x18, waiting for transfers between devices: none -> 125 us  [the longest x10 114 us: swap(): return lax.ppermute(array, axis, [(0, 1), (1, 0)])]
    all_to_all x2 -> x1, blocking collectives: 78.9 us -> 18.9 us  [shards(): lax.all_to_all(sent.reshape(tps, share, -1), 'tp', 0, 0).astype(F32)]
    ppermute x0 -> x18, starting transfers between devices: none -> 26 us  [the longest x8 16.2 us: reached(): got = lax.ppermute(packed, SEQ, route).astype(F32)]
    pallas_call x2 -> x9, Pallas kernels: 76.9 us -> 98 us  [the longest x1 30.2 us: feed_forward_last(): pl.pallas_call(feed_forward_last_kernel, grid=(tps,), in_specs=[scalar_sp...]
    all_gather x3 -> x1, blocking collectives: 33.6 us -> 15.6 us  [shards(): lax.all_gather(jnp.concatenate([own_grad.astype(BF16), extra_high, extra_...]
    psum x1 -> x0, blocking collectives: 16.8 us -> none  [shards(): lax.psum((conv_grad[:, inner_width:], norm_attn_part[0], norm_ffn_part[0]...]
  transfers between devices with their start and end apart: 20 -> 31, of which waited for: 14 -> 22; matrix products, arithmetic and copies ran while one was open for 9% -> 15% of each run, Pallas kernels for 1% -> 11%
where the time goes in v2:
time: 739 us; the launch traced here: 730 us
  waiting for transfers between devices  292 us (40%)
  Pallas kernels  113 us (15%)
  blocking collectives  102 us (14%)
  local copies, waits for them, and re-layouts  60.5 us (8%)
  starting transfers between devices  50.5 us (7%)
  other arithmetic  50.1 us (7%)
  matrix products  41.5 us (6%)
  between operations  20.9 us (3%)
    ppermute x10, waiting for transfers between devices, swap(): return lax.ppermute(array, axis, [(0, 1), (1, 0)])  114 us
    all_gather x2, waiting for transfers between devices, gather_weights(): lax.all_gather(part, INNER + ('tp',)).reshape((GROUP, tps) + part.shape)  78.9 us
    all_gather x1, waiting for transfers between devices, reduce_last(): return lax.all_gather(part, INNER)  48.9 us
    pallas_call x1, Pallas kernels, feed_forward_last(): pl.pallas_call(feed_forward_last_kernel, grid=(tps,), in_specs=[scalar_sp...  30.2 us
    pallas_call x1, Pallas kernels, feed_forward_first(): pl.pallas_call(feed_forward_first_kernel, grid=(tps,), in_specs=[scalar_s...  26.6 us
    pallas_call x1, Pallas kernels, attention_backward(): pl.pallas_call(attention_backward_kernel, grid=(tps,), in_specs=[scalar_s...  26.2 us
    psum x1, blocking collectives, shards(): lax.psum(shared + (product(normed, step_back, 'rd,rc->dc'), step_bias_gra...  24.4 us
    all_gather x1, blocking collectives, shards(): state_all = lax.all_gather(state_back, 'tp')  22.7 us
  transfers between devices with their start and end apart: 31, of which 22 were waited for; matrix products, arithmetic and copies ran while one was open for 15% of the time, Pallas kernels for 11%

profile of v2, /device:TPU:0, one launch (start us, length us, event | category | flops | bytes accessed | tf_op | source)
XLA Modules:
  0.0 729.6 jit_solution(8588392505449545905)
XLA Ops:
  13.3 20.3 %all_gather.27 = bf16[256,1024]{1,0:T(8,128)(2,1)S(1)} all-gather(bf16[256,256]{1,0:T(8,128)(2,1)S(1)} %copy-done.65), channel_id=1, replica_groups=mesh['g'=1,'a'=2,'b'=2,'c'=2,'tp'=4] {'tp'}, dimensions={1}, use_global_device_ids=true | all-gather | bytes 655360 | tf_op jit(solution)/shard_map/all_gather | solution.py:913
  37.5 4.5 all-to-all-start
  52.2 5.0 collective-permute-start.3
  57.3 3.4 collective-permute-start.2
  63.8 5.6 collective-permute-done.2
  71.3 3.4 fusion.27
  76.7 2.4 multiply_reduce_fusion.10
  79.2 7.6 %all-to-all-done.embed_ref = bf16[4,512,256]{2,1,0:T(8,128)(2,1)} async-done(((bf16[4,512,256]{2,1,0:T(8,128)(2,1)}), bf16[4,512,256]{2,1,0:T(8,128)(2,1)}, u32[]{:S(2)}, u32[]{:S(2)}) %all-to-all-start) | async-done | bytes 1048608 | tf_op jit(solution)/shard_map/all_to_all | solution.py:906
  89.6 18.9 %all_to_all.30 = bf16[4,64,1152]{2,1,0:T(8,128)(2,1)S(1)} all-to-all(bf16[4,64,1152]{2,1,0:T(8,128)(2,1)S(1)} %bitcast.253), channel_id=1, replica_groups=mesh['g'=1,'a'=2,'b'=2,'c'=2,'tp'=4] {'tp'}, dimensions={0} | all-to-all | bytes 1179648 | tf_op jit(solution)/shard_map/all_to_all | solution.py:956
  108.5 3.7 all-to-all-start.2
  114.5 78.0 %all-gather.9.cloned.1.call-done = bf16[20480,512]{1,0:T(8,128)(2,1)} async-done(((bf16[640,512]{1,0:T(8,128)(2,1)}), bf16[20480,512]{1,0:T(8,128)(2,1)}) %all-gather.9.cloned.1.call-update) | async-done | bytes 20971536 | tf_op jit(solution)/shard_map/all_gather | solution.py:871
  192.5 14.7 %attention_forward.1 = (f32[512,1024]{1,0:T(8,128)}, bf16[512,1024]{1,0:T(8,128)(2,1)}, bf16[512,1024]{1,0:T(8,128)(2,1)}, bf16[4,3,512,256]{3,2,1,0:T(8,128)(2,1)}, bf16[4,512,256]{2,1,0:T(8,128)(2,1)}) custom-call(bf16[4,512,256]{2,1,0:T(8,128)(2,1)} %all-to-all-done.embed_ref, f32[64,1,1024]{2,1,0:T(1,128)} %copy.149.global_ref, f32[1,1024]{1,0:T(1,128)} %bitcast.286, ...), custom_call_target="tpu_custom_call" | custom-call | flops 4294967296 | bytes 14680064 | tf_op jit(solution)/shard_map/attention_forward/pallas_call | solution.py:161
  208.2 26.6 %feed_forward_first.1 = (bf16[512,1024]{1,0:T(8,128)(2,1)}, bf16[1024,512]{1,0:T(8,128)(2,1)}, bf16[512,1024]{1,0:T(8,128)(2,1)}, f32[512,1024]{1,0:T(8,128)}, f...) custom-call(s32[1]{0:T(128)} %bitcast.core_ref, ...), custom_call_target="tpu_custom_call" | custom-call | flops 19327352832 | bytes 33554432 | tf_op jit(solution)/shard_map/feed_forward_first/pallas_call | solution.py:361
  235.2 10.0 %collective-permute-done.5.refs_1_.refs_3_.refs_5_.refs_7_ = bf16[2,2,4,384,512]{4,3,2,1,0:T(8,128)(2,1)S(1)} collective-permute-done((bf16[2,2,4,384,512]{4,3,2,1,0:T(8,128)(2,1)}, bf16[2,2,4,384,512]{4,3,2,1,0:T(8,128)(2,1)S(1)}, u32[]{:S(2)}, u32[]{:S(2)}) %collective-permute-start.5) | collective-permute-done | bytes 6291488 | tf_op jit(solution)/shard_map/ppermute | solution.py:701
  245.2 2.8 copy-done.1
  250.2 3.2 collective-permute-start.6
  253.5 54.2 %collective-permute-done.6.refs_1_.refs_3_ = bf16[2,4,192,512]{3,2,1,0:T(8,128)(2,1)S(1)} collective-permute-done((bf16[2,4,192,512]{3,2,1,0:T(8,128)(2,1)S(1)}, bf16[2,4,192,512]{3,2,1,0:T(8,128)(2,1)S(1)}, u32[]{:S(2)}, u32[]{:S(2)}) %collective-permute-start.6) | collective-permute-done | bytes 1572896 | tf_op jit(solution)/shard_map/ppermute | solution.py:701
  313.6 30.2 %feed_forward_last.1 = (bf16[4,512,256]{2,1,0:T(8,128)(2,1)}, f32[512,1024]{1,0:T(8,128)}, f32[1,1024]{1,0:T(1,128)}, bf16[8,4,384,512]{3,2,1,0:T(8,128)(2,1)}) custom-call(s32[1]{0:T(128)} %bitcast.core_ref, f32[512,1024]{1,0:T(8,128)} %get-tuple-element.59.hidden_ref, bf16[512,1024]{1,0:T(8,128)(2,1)} %get-tuple-element.60.cot_ref, f32[1,1024]{1,0:T(1,128)} %bitcast.296, ...), custom_call_target="tpu_custom_call" | custom-call | flops 19327352832 | bytes 33554432 | tf_op jit(solution)/shard_map/feed_forward_last/pallas_call | solution.py:402
  343.8 4.4 all-to-all-start.3
  350.4 17.9 %collective-permute-done.8.two_ref = bf16[4,192,512]{2,1,0:T(8,128)(2,1)S(1)} collective-permute-done((bf16[4,192,512]{2,1,0:T(8,128)(2,1)}, bf16[4,192,512]{2,1,0:T(8,128)(2,1)S(1)}, u32[]{:S(2)}, u32[]{:S(2)}) %collective-permute-start.8) | collective-permute-done | bytes 786464 | tf_op jit(solution)/shard_map/ppermute | solution.py:701
  374.7 26.2 %attention_backward.1 = (bf16[4,512,256]{2,1,0:T(8,128)(2,1)}, f32[64,1024]{1,0:T(8,128)}, f32[64,1]{1,0:T(8,128)}, f32[1,1024]{1,0:T(1,128)}, bf16[2,2,4,256,51...) custom-call(s32[1]{0:T(128)} %bitcast.core_ref, f32[512,1024]{1,0:T(8,128)} %get-tuple-element.73.refs_0_.grad_ref, ...), custom_call_target="tpu_custom_call" | custom-call | flops 8589934592 | bytes 27262976 | tf_op jit(solution)/shard_map/attention_backward/pallas_call | solution.py:549
  403.2 5.2 collective-permute-done.10.refs_1_.refs_3_.refs_5_.refs_7_
  408.4 2.3 copy-done.2
  410.7 7.1 first_sum.3
  419.8 15.6 %all_gather.32 = bf16[256,1152]{1,0:T(8,128)(2,1)S(1)} all-gather(bf16[64,1152]{1,0:T(8,128)(2,1)S(1)} %concatenate.75), channel_id=1, replica_groups=mesh['g'=1,'a'=2,'b'=2,'c'=2,'tp'=4] {'tp'}, dimensions={0}, use_global_device_ids=true | all-gather | bytes 737280 | tf_op jit(solution)/shard_map/all_gather | solution.py:1006
  443.5 12.6 %collective-permute-done.11.refs_1_.refs_3_ = bf16[2,4,128,512]{3,2,1,0:T(8,128)(2,1)} collective-permute-done((bf16[2,4,128,512]{3,2,1,0:T(8,128)(2,1)}, bf16[2,4,128,512]{3,2,1,0:T(8,128)(2,1)}, u32[]{:S(2)}, u32[]{:S(2)}) %collective-permute-start.11) | collective-permute-done | bytes 1048608 | tf_op jit(solution)/shard_map/ppermute | solution.py:701
  456.2 3.2 second_sum.3
  461.5 11.6 %collective-permute-done.17.two_ref = bf16[4,128,512]{2,1,0:T(8,128)(2,1)S(1)} collective-permute-done((bf16[4,128,512]{2,1,0:T(8,128)(2,1)S(1)}, bf16[4,128,512]{2,1,0:T(8,128)(2,1)S(1)}, u32[]{:S(2)}, u32[]{:S(2)}) %collective-permute-start.17) | collective-permute-done | bytes 524320 | tf_op jit(solution)/shard_map/ppermute | solution.py:701
  475.6 3.4 pad_maximum_fusion
  488.2 2.5 convolution_convert_fusion.2
  493.1 5.3 fusion.31
  507.7 3.2 collective-permute-done.14
  520.8 2.8 fusion.21
  529.3 2.6 multiply_reduce_fusion.11
  536.9 22.7 %all-gather.2 = bf16[1024,256]{1,0:T(8,128)(2,1)S(1)} all-gather(bf16[256,256]{1,0:T(8,128)(2,1)S(1)} %maximum_convert_fusion.4), channel_id=4, replica_groups=mesh['g'=1,'a'=2,'b'=2,'c'=2,'tp'=4] {'tp'}, dimensions={0}, use_global_device_ids=true | all-gather | bytes 655360 | tf_op jit(solution)/shard_map/all_gather | solution.py:1097
  566.3 4.3 all-to-all-start.4
  571.9 2.5 reduce-window.42
  574.5 2.8 fusion.151
  578.1 2.5 reduce-window.44
  588.0 9.4 %all-to-all-done.4 = bf16[4,512,256]{2,1,0:T(8,128)(2,1)S(1)} async-done(((bf16[4,512,256]{2,1,0:T(8,128)(2,1)}), bf16[4,512,256]{2,1,0:T(8,128)(2,1)S(1)}, u32[]{:S(2)}, u32[]{:S(2)}) %all-to-all-start.4) | async-done | bytes 1048608 | tf_op jit(solution)/shard_map/all_to_all | solution.py:909
  597.3 4.2 all-to-all-start.5
  603.6 14.1 %all-to-all-done.5 = bf16[4,288,256]{2,1,0:T(8,128)(2,1)} async-done(((bf16[4,288,256]{2,1,0:T(8,128)(2,1)}), bf16[4,288,256]{2,1,0:T(8,128)(2,1)}, u32[]{:S(2)}, u32[]{:S(2)}) %all-to-all-start.5) | async-done | bytes 589856 | tf_op jit(solution)/shard_map/all_to_all | solution.py:1078
  619.7 24.4 %all-reduce.12 = (f32[1024]{0:T(1024)}, f32[1024,8]{0,1:T(8,128)}, f32[8]{0:T(128)}, f32[8]{0:T(128)}, f32[4,512]{1,0:T(4,128)}, /*index=5*/f32[4,256]{1,0:T(4,1...) all-reduce(f32[1024]{0:T(1024)S(1)} %bitcast.288, ...), channel_id=1, replica_groups=mesh['g'=1,'a'=2,'b'=2,'c'=2,'tp'=4] {'g','a','b','c'}, use_global_device_ids=true, to_apply=%region_26.27 | all-reduce | flops 14872 | bytes 118976 | tf_op jit(solution)/shard_map/psum | solution.py:1128
  644.1 2.9 all-reduce.16.cloned.1.call-done
  647.0 2.9 convert_element_type.284
  654.2 48.9 %all-gather.7.cloned.1.call-done = bf16[8,1024,512]{2,1,0:T(8,128)(2,1)} async-done(((bf16[1,1024,512]{2,1,0:T(8,128)(2,1)}), bf16[8,1024,512]{2,1,0:T(8,128)(2,1)}) %all-gather.7.cloned.1.call-update) | async-done | bytes 8388624 | tf_op jit(solution)/shard_map/all_gather | solution.py:829
  711.2 2.4 maximum_convert_fusion.1
  713.6 4.6 maximum_convert_fusion
  (534 shorter events, 139.4 us)
Async XLA Ops:
  7.2 81.5 %copy-start = (bf16[512,1024]{1,0:T(8,128)(2,1)S(1)}, bf16[512,1024]{1,0:T(8,128)(2,1)}, u32[]{:S(2)}) copy-start(bf16[512,1024]{1,0:T(8,128)(2,1)} %param.36) | copy-start | bytes 3145732
  7.2 185.3 %all-gather.9.cloned.1.call-start = ((), (), s32[]{:S(2)}) async-start(), calls=%async_computation.11 | async-start | bytes 21626880 | tf_op jit(solution)/shard_map/all_gather | solution.py:871
  12.3 21.5 %copy-start.57 = (bf16[1024,256]{1,0:T(8,128)(2,1)S(1)}, bf16[1024,256]{1,0:T(8,128)(2,1)}, u32[]{:S(2)}) copy-start(bf16[1024,256]{1,0:T(8,128)(2,1)} %param.28) | copy-start | bytes 1572868
  12.3 21.5 %copy-start.89 = (f32[1024]{0:T(1024)S(1)}, f32[1024]{0:T(1024)}, u32[]{:S(2)}) copy-start(f32[1024]{0:T(1024)} %param.25) | copy-start | bytes 12292
  12.3 301.3 %all-gather.11.cloned.1.call-start = ((), (), s32[]{:S(2)}) async-start(), calls=%async_computation.12 | async-start | bytes 12976128 | tf_op jit(solution)/shard_map/all_gather | solution.py:871
  33.6 79.2 %copy-start.16 = (bf16[256,1024]{1,0:T(8,128)(2,1)}, bf16[256,1024]{1,0:T(8,128)(2,1)S(1)}, u32[]{:S(2)}) copy-start(bf16[256,1024]{1,0:T(8,128)(2,1)S(1)} %all_gather.27) | copy-start | bytes 1572868
  33.8 42.9 %copy-start.104 = (f32[256]{0:T(256)}, f32[256]{0:T(256)S(1)}, u32[]{:S(2)}) copy-start(f32[256]{0:T(256)S(1)} %add_rsqrt_fusion) | copy-start | bytes 3076
  36.1 13.4 %collective-permute-start = (f32[3,768]{1,0:T(4,128)S(1)}, f32[3,768]{1,0:T(4,128)S(1)}, u32[]{:S(2)}, u32[]{:S(2)}) collective-permute-start(f32[3,768]{1,0:T(4,128)S(1)} %fusion.105), channel_id=1, source_target_pairs={{0,4},{4,8},{8,12},{12,16},{16,20},{20,24},{24,28},{1,5},{5,9},{9,... | collective-permute-start | bytes 27656 | tf_op jit(solution)/shard_map/ppermute | solution.py:599
  37.5 49.3 %all-to-all-start = ((bf16[4,512,256]{2,1,0:T(8,128)(2,1)}), bf16[4,512,256]{2,1,0:T(8,128)(2,1)}, u32[]{:S(2)}, u32[]{:S(2)}) async-start(bf16[4,512,256]{2,1,0:T(8,128)(2,1)} %bitcast.267), calls=%async_computation | async-start | bytes 2097152 | tf_op jit(solution)/shard_map/all_to_all | solution.py:906
  48.6 22.6 %copy-start.79 = (f32[8,256]{1,0:T(8,128)}, f32[8,256]{1,0:T(8,128)S(1)}, u32[]{:S(2)}) copy-start(f32[8,256]{1,0:T(8,128)S(1)} %add_bitcast_fusion.3) | copy-start | bytes 24580
  49.3 443.7 %copy-start.71 = (pred[256,256]{1,0:T(8,128)(4,1)}, pred[256,256]{1,0:T(8,128)(4,1)S(1)}, u32[]{:S(2)}) copy-start(pred[256,256]{1,0:T(8,128)(4,1)S(1)} %compare_and_fusion) | copy-start | bytes 196612
  51.1 19.5 %copy-start.23 = (f32[256,768]{1,0:T(8,128)}, f32[256,768]{1,0:T(8,128)S(1)}, u32[]{:S(2)}) copy-start(f32[256,768]{1,0:T(8,128)S(1)} %get-tuple-element.152) | copy-start | bytes 2359300
  51.4 19.8 %copy-start.21 = (f32[256,512]{0,1:T(8,128)}, f32[256,512]{0,1:T(8,128)S(1)}, u32[]{:S(2)}) copy-start(f32[256,512]{0,1:T(8,128)S(1)} %copy.145) | copy-start | bytes 1572868
  52.2 11.5 %collective-permute-start.3 = (bf16[528,128]{1,0:T(8,128)(2,1)S(1)}, bf16[528,128]{1,0:T(8,128)(2,1)S(1)}, u32[]{:S(2)}, u32[]{:S(2)}) collective-permute-start(bf16[528,128]{1,0:T(8,128)(2,1)S(1)} %maximum_maximum_fusion.1), channel_id=1, source_target_pairs={{0,12},{4,16},{8,20},{12,24},{16,28},{1,13},{5,17},{9,21},{13,25},... | collective-permute-start | bytes 405512 | tf_op jit(solution)/shard_map/ppermute | solution.py:688
  57.3 12.1 %collective-permute-start.2 = (bf16[528,128]{1,0:T(8,128)(2,1)S(1)}, bf16[528,128]{1,0:T(8,128)(2,1)S(1)}, u32[]{:S(2)}, u32[]{:S(2)}) collective-permute-start(bf16[528,128]{1,0:T(8,128)(2,1)S(1)} %maximum_maximum_fusion.1), channel_id=1, source_target_pairs={{0,8},{4,12},{8,16},{12,20},{16,24},{20,28},{1,9},{5,13},{9,17},{1... | collective-permute-start | bytes 405512 | tf_op jit(solution)/shard_map/ppermute | solution.py:688
  60.7 8.8 %collective-permute-start.1 = (bf16[528,128]{1,0:T(8,128)(2,1)S(1)}, bf16[528,128]{1,0:T(8,128)(2,1)S(1)}, u32[]{:S(2)}, u32[]{:S(2)}) collective-permute-start(bf16[528,128]{1,0:T(8,128)(2,1)S(1)} %maximum_maximum_fusion.1), channel_id=1, source_target_pairs={{0,4},{4,8},{8,12},{12,16},{16,20},{20,24},{24,28},{1,5},{5,9},{9,... | collective-permute-start | bytes 405512 | tf_op jit(solution)/shard_map/ppermute | solution.py:688
  62.0 7.9 %collective-permute-start.4 = (bf16[528,128]{1,0:T(8,128)(2,1)S(1)}, bf16[528,128]{1,0:T(8,128)(2,1)S(1)}, u32[]{:S(2)}, u32[]{:S(2)}) collective-permute-start(bf16[528,128]{1,0:T(8,128)(2,1)S(1)} %maximum_maximum_fusion.1), channel_id=1, source_target_pairs={{0,16},{4,20},{8,24},{12,28},{1,17},{5,21},{9,25},{13,29},{2,18},{... | collective-permute-start | bytes 405512 | tf_op jit(solution)/shard_map/ppermute | solution.py:688
  108.5 98.7 %all-to-all-start.2 = ((bf16[4,512,256]{2,1,0:T(8,128)(2,1)}), bf16[4,512,256]{2,1,0:T(8,128)(2,1)S(1)}, u32[]{:S(2)}, u32[]{:S(2)}) async-start(bf16[4,512,256]{2,1,0:T(8,128)(2,1)} %bitcast.268), calls=%async_computation.2 | async-start | bytes 2097152 | tf_op jit(solution)/shard_map/all_to_all | solution.py:906
  112.2 363.4 %reduce-scatter.3.cloned.1.call-start = ((), (), s32[]{:S(2)}) async-start(), calls=%async_computation.8 | async-start | bytes 14155776 | tf_op jit(solution)/shard_map/reduce_scatter | solution.py:997
  234.8 10.4 %collective-permute-start.5 = (bf16[2,2,4,384,512]{4,3,2,1,0:T(8,128)(2,1)}, bf16[2,2,4,384,512]{4,3,2,1,0:T(8,128)(2,1)S(1)}, u32[]{:S(2)}, u32[]{:S(2)}) collective-permute-start(bf16[2,2,4,384,512]{4,3,2,1,0:T(8,128)(2,1)} %get-tuple-element.66), channel_id=1, source_target_pairs={{0,4},{4,0},{1,5},{5,1},{2,6},{6,2},{3,7},{7,3},{8,12},{12,8},{9,1... | collective-permute-start | bytes 18874376 | tf_op jit(solution)/shard_map/ppermute | solution.py:701
  250.2 57.5 %collective-permute-start.6 = (bf16[2,4,192,512]{3,2,1,0:T(8,128)(2,1)S(1)}, bf16[2,4,192,512]{3,2,1,0:T(8,128)(2,1)S(1)}, u32[]{:S(2)}, u32[]{:S(2)}) collective-permute-start(bf16[2,4,192,512]{3,2,1,0:T(8,128)(2,1)S(1)} %get-tuple-element.68), channel_id=1, source_target_pairs={{0,8},{8,0},{1,9},{9,1},{2,10},{10,2},{3,11},{11,3},{4,12},{12,4},... | collective-permute-start | bytes 4718600 | tf_op jit(solution)/shard_map/ppermute | solution.py:701
  253.4 54.3 %collective-permute-start.7 = (bf16[2,4,192,512]{3,2,1,0:T(8,128)(2,1)S(1)}, bf16[2,4,192,512]{3,2,1,0:T(8,128)(2,1)S(1)}, u32[]{:S(2)}, u32[]{:S(2)}) collective-permute-start(bf16[2,4,192,512]{3,2,1,0:T(8,128)(2,1)S(1)} %get-tuple-element.70), channel_id=1, source_target_pairs={{0,16},{16,0},{1,17},{17,1},{2,18},{18,2},{3,19},{19,3},{4,20},{20... | collective-permute-start | bytes 4718600 | tf_op jit(solution)/shard_map/ppermute | solution.py:701
  343.8 25.4 %copy-start.5 = (f32[512,1024]{1,0:T(8,128)S(1)}, f32[512,1024]{1,0:T(8,128)}, u32[]{:S(2)}) copy-start(f32[512,1024]{1,0:T(8,128)} %get-tuple-element.73.refs_0_.grad_ref) | copy-start | bytes 6291460
  343.8 30.9 %all-to-all-start.3 = ((bf16[4,512,256]{2,1,0:T(8,128)(2,1)}), bf16[4,512,256]{2,1,0:T(8,128)(2,1)}, u32[]{:S(2)}, u32[]{:S(2)}) async-start(bf16[4,512,256]{2,1,0:T(8,128)(2,1)} %get-tuple-element.72), calls=%async_computation.3 | async-start | bytes 2097152 | tf_op jit(solution)/shard_map/all_to_all | solution.py:909
  348.2 216.1 %reduce-scatter.5.cloned.1.call-start = ((), (), s32[]{:S(2)}) async-start(), calls=%async_computation.9 | async-start | bytes 5242880 | tf_op jit(solution)/shard_map/reduce_scatter | solution.py:826
  348.3 20.0 %collective-permute-start.8 = (bf16[4,192,512]{2,1,0:T(8,128)(2,1)}, bf16[4,192,512]{2,1,0:T(8,128)(2,1)S(1)}, u32[]{:S(2)}, u32[]{:S(2)}) collective-permute-start(bf16[4,192,512]{2,1,0:T(8,128)(2,1)} %copy-done.12), channel_id=1, source_target_pairs={{0,16},{16,0},{1,17},{17,1},{2,18},{18,2},{3,19},{19,3},{4,20},{20... | collective-permute-start | bytes 2359304 | tf_op jit(solution)/shard_map/ppermute | solution.py:701
  349.6 19.6 %collective-permute-start.9 = (bf16[4,192,512]{2,1,0:T(8,128)(2,1)}, bf16[4,192,512]{2,1,0:T(8,128)(2,1)S(1)}, u32[]{:S(2)}, u32[]{:S(2)}) collective-permute-start(bf16[4,192,512]{2,1,0:T(8,128)(2,1)} %copy-done.11), channel_id=1, source_target_pairs={{0,8},{8,0},{1,9},{9,1},{2,10},{10,2},{3,11},{11,3},{4,12},{12,4},... | collective-permute-start | bytes 2359304 | tf_op jit(solution)/shard_map/ppermute | solution.py:701
  400.9 7.5 %collective-permute-start.10 = (bf16[2,2,4,256,512]{4,3,2,1,0:T(8,128)(2,1)}, bf16[2,2,4,256,512]{4,3,2,1,0:T(8,128)(2,1)}, u32[]{:S(2)}, u32[]{:S(2)}) collective-permute-start(bf16[2,2,4,256,512]{4,3,2,1,0:T(8,128)(2,1)} %get-tuple-element.85), channel_id=1, source_target_pairs={{0,4},{4,0},{1,5},{5,1},{2,6},{6,2},{3,7},{7,3},{8,12},{12,8},{9,1... | collective-permute-start | bytes 12582920 | tf_op jit(solution)/shard_map/ppermute | solution.py:701
  410.7 26.9 %copy-start.24 = (f32[256,768]{1,0:T(8,128)S(1)}, f32[256,768]{1,0:T(8,128)}, u32[]{:S(2)}) copy-start(f32[256,768]{1,0:T(8,128)} %copy-done.23) | copy-start | bytes 2359300
  410.7 26.9 %copy-start.38 = (f32[256,512]{1,0:T(8,128)S(1)}, f32[256,512]{1,0:T(8,128)}, u32[]{:S(2)}) copy-start(f32[256,512]{1,0:T(8,128)} %copy-done.37) | copy-start | bytes 1572868
  410.7 26.9 %copy-start.56 = (f32[256,512]{1,0:T(8,128)S(1)}, f32[256,512]{1,0:T(8,128)}, u32[]{:S(2)}) copy-start(f32[256,512]{1,0:T(8,128)} %copy.146) | copy-start | bytes 1572868
  410.7 26.9 %copy-start.137 = (f32[256,512]{1,0:T(8,128)S(1)}, f32[256,512]{1,0:T(8,128)}, u32[]{:S(2)}) copy-start(f32[256,512]{1,0:T(8,128)} %get-tuple-element.191) | copy-start | bytes 1572868
  417.8 38.3 %collective-permute-start.11 = (bf16[2,4,128,512]{3,2,1,0:T(8,128)(2,1)}, bf16[2,4,128,512]{3,2,1,0:T(8,128)(2,1)}, u32[]{:S(2)}, u32[]{:S(2)}) collective-permute-start(bf16[2,4,128,512]{3,2,1,0:T(8,128)(2,1)} %get-tuple-element.86), channel_id=1, source_target_pairs={{0,8},{8,0},{1,9},{9,1},{2,10},{10,2},{3,11},{11,3},{4,12},{12,4},... | collective-permute-start | bytes 3145736 | tf_op jit(solution)/shard_map/ppermute | solution.py:701
  419.0 37.1 %collective-permute-start.12 = (bf16[2,4,128,512]{3,2,1,0:T(8,128)(2,1)}, bf16[2,4,128,512]{3,2,1,0:T(8,128)(2,1)}, u32[]{:S(2)}, u32[]{:S(2)}) collective-permute-start(bf16[2,4,128,512]{3,2,1,0:T(8,128)(2,1)} %get-tuple-element.89), channel_id=1, source_target_pairs={{0,16},{16,0},{1,17},{17,1},{2,18},{18,2},{3,19},{19,3},{4,20},{20... | collective-permute-start | bytes 3145736 | tf_op jit(solution)/shard_map/ppermute | solution.py:701
  459.4 13.7 %collective-permute-start.17 = (bf16[4,128,512]{2,1,0:T(8,128)(2,1)S(1)}, bf16[4,128,512]{2,1,0:T(8,128)(2,1)S(1)}, u32[]{:S(2)}, u32[]{:S(2)}) collective-permute-start(bf16[4,128,512]{2,1,0:T(8,128)(2,1)S(1)} %get-tuple-element.90), channel_id=1, source_target_pairs={{0,16},{16,0},{1,17},{17,1},{2,18},{18,2},{3,19},{19,3},{4,20},{20... | collective-permute-start | bytes 1572872 | tf_op jit(solution)/shard_map/ppermute | solution.py:701
  461.0 13.4 %collective-permute-start.18 = (bf16[4,128,512]{2,1,0:T(8,128)(2,1)S(1)}, bf16[4,128,512]{2,1,0:T(8,128)(2,1)S(1)}, u32[]{:S(2)}, u32[]{:S(2)}) collective-permute-start(bf16[4,128,512]{2,1,0:T(8,128)(2,1)S(1)} %get-tuple-element.93), channel_id=1, source_target_pairs={{0,8},{8,0},{1,9},{9,1},{2,10},{10,2},{3,11},{11,3},{4,12},{12,4},... | collective-permute-start | bytes 1572872 | tf_op jit(solution)/shard_map/ppermute | solution.py:701
  479.1 167.9 %all-reduce.16.cloned.1.call-start = ((), (), s32[]{:S(2)}) async-start(), calls=%async_computation.13 | async-start | bytes 7340032 | tf_op jit(solution)/shard_map/psum | solution.py:1099
  501.1 6.5 collective-permute-start.15
  502.4 8.5 %collective-permute-start.14 = (bf16[528,128]{1,0:T(8,128)(2,1)}, bf16[528,128]{1,0:T(8,128)(2,1)S(1)}, u32[]{:S(2)}, u32[]{:S(2)}) collective-permute-start(bf16[528,128]{1,0:T(8,128)(2,1)} %maximum_maximum_fusion.2), channel_id=1, source_target_pairs={{8,0},{12,4},{16,8},{20,12},{24,16},{28,20},{9,1},{13,5},{17,9},{2... | collective-permute-start | bytes 405512 | tf_op jit(solution)/shard_map/ppermute | solution.py:688
  503.7 7.2 collective-permute-start.13
  505.4 10.5 %collective-permute-start.16 = (bf16[528,128]{1,0:T(8,128)(2,1)}, bf16[528,128]{1,0:T(8,128)(2,1)}, u32[]{:S(2)}, u32[]{:S(2)}) collective-permute-start(bf16[528,128]{1,0:T(8,128)(2,1)} %maximum_maximum_fusion.2), channel_id=1, source_target_pairs={{16,0},{20,4},{24,8},{28,12},{17,1},{21,5},{25,9},{29,13},{18,2},{... | collective-permute-start | bytes 405512 | tf_op jit(solution)/shard_map/ppermute | solution.py:688
  533.8 3.1 collective-permute-start.19
  536.9 22.8 %copy-start.91 = (f32[1024]{0:T(1024)S(1)}, f32[1024]{0:T(1024)}, u32[]{:S(2)}) copy-start(f32[1024]{0:T(1024)} %param.25) | copy-start | bytes 12292
  536.9 22.8 %copy-start.105 = (f32[256]{0:T(256)S(1)}, f32[256]{0:T(256)}, u32[]{:S(2)}) copy-start(f32[256]{0:T(256)} %copy-done.104) | copy-start | bytes 3076
  562.5 140.6 %all-gather.7.cloned.1.call-start = ((), (), s32[]{:S(2)}) async-start(), calls=%async_computation.10 | async-start | bytes 9437184 | tf_op jit(solution)/shard_map/all_gather | solution.py:829
  566.3 31.1 %all-to-all-start.4 = ((bf16[4,512,256]{2,1,0:T(8,128)(2,1)}), bf16[4,512,256]{2,1,0:T(8,128)(2,1)S(1)}, u32[]{:S(2)}, u32[]{:S(2)}) async-start(bf16[4,512,256]{2,1,0:T(8,128)(2,1)} %get-tuple-element.81), calls=%async_computation.4 | async-start | bytes 2097152 | tf_op jit(solution)/shard_map/all_to_all | solution.py:909
  597.3 20.4 %all-to-all-start.5 = ((bf16[4,288,256]{2,1,0:T(8,128)(2,1)}), bf16[4,288,256]{2,1,0:T(8,128)(2,1)}, u32[]{:S(2)}, u32[]{:S(2)}) async-start(bf16[4,288,256]{2,1,0:T(8,128)(2,1)} %pad_maximum_fusion.3), calls=%async_computation.5 | async-start | bytes 1179648 | tf_op jit(solution)/shard_map/all_to_all | solution.py:1078
  601.5 18.2 %copy-start.130 = (f32[512]{0:T(512)S(1)}, f32[512]{0:T(512)}, u32[]{:S(2)}) copy-start(f32[512]{0:T(512)} %get-tuple-element.170) | copy-start | bytes 6148
  (121 other events, 660.4 us)
Sparse Core Ops, SparseCore 0:
  12.4 180.0 all-gather.8
  195.4 118.1 all-gather.10
  343.9 104.1 reduce-scatter.2
  479.2 85.0 reduce-scatter.4
  570.0 76.9 all-reduce.15
  648.8 54.2 all-gather.6

commit v3 on v2

--- a/solution.py
+++ b/solution.py
@@ -116,8 +116,9 @@
 
 
 def attention_forward_kernel(
-    embed_ref, global_ref, gain_ref, weight_ref, hidden_ref, input_ref, normed_ref, qkv_ref, context_ref
+    embed_ref, global_ref, gain_ref, weight_ref, *refs
 ):
+    hidden_ref, input_ref, normed_ref, qkv_ref, context_ref = refs[-5:]
     step = pl.program_id(0)
     blocks, rows, width = embed_ref.shape
     parts = weight_ref.shape[0]
@@ -155,7 +156,7 @@
         hidden_ref[:, cols] += mm(context, weight)
 
 
-def attention_forward(embed, global_rows, gain, weights):
+def attention_forward(embed, global_rows, gain, weights, tokens):
     blocks, rows, width = embed.shape
     tps = weights.shape[1]
     return pl.pallas_call(
@@ -166,6 +167,7 @@
             whole((rows // PATCH, 1, D)),
             whole((1, D)),
             attention_spec(weights),
+            *(anywhere() for _ in tokens),
         ],
         out_specs=[
             whole((rows, D)),
@@ -186,7 +188,7 @@
         cost_estimate=pl.CostEstimate(
             flops=2 * rows * D * D * 4, bytes_accessed=14 << 20, transcendentals=rows * 2048
         ),
-    )(embed, global_rows, gain, weights)
+    )(embed, global_rows, gain, weights, *tokens)
 
 
 def core_halves(core, grad):
@@ -443,11 +445,11 @@
     weight_ref,
     qkv_ref,
     context_ref,
+    squares_ref,
     token_ref,
-    layer_token_ref,
     embed_ref,
     global_ref,
-    dot_ref,
+    payload_ref,
     gain_grad_ref,
     own_ref,
     other_ref,
@@ -539,10 +541,15 @@
             embed_ref[i] = result[:, i * width : (i + 1) * width].astype(BF16)
         patch = jnp.sum(result.reshape(rows // PATCH, PATCH, D), axis=1)
         global_ref[...] = patch
-        dot_ref[...] = jnp.sum(patch * mixer_ref[...], axis=1, keepdims=True)
-
-
-def attention_backward(core, grad, mixer_rows, inputs, normed, gain, weights, qkv, context, tokens):
+        dots = jnp.sum(patch * mixer_ref[...], axis=1, keepdims=True)
+        payload_ref[:, :D] = patch.astype(BF16)
+        lane = lax.broadcasted_iota(jnp.int32, (patch.shape[0], 128), 1)
+        values = jnp.where(lane % 64 < 32, squares_ref[...], dots)
+        high = values.astype(BF16).astype(F32)
+        payload_ref[:, D:] = jnp.where(lane < 64, high, values - high).astype(BF16)
+
+
+def attention_backward(core, grad, mixer_rows, inputs, normed, gain, weights, qkv, context, squares, token):
     rows = grad.shape[0]
     tps, _, width = context.shape
     depth = 2 * D // GROUP
@@ -559,13 +566,13 @@
             attention_spec(weights),
             pl.BlockSpec((1, 3, rows, width), lambda j: (j, 0, 0, 0)),
             pl.BlockSpec((1, rows, width), lambda j: (j, 0, 0)),
-            anywhere(),
+            whole(squares.shape),
             anywhere(),
         ],
         out_specs=[
             whole((tps, rows, width)),
             whole((rows // PATCH, D)),
-            whole((rows // PATCH, 1)),
+            whole((rows // PATCH, D + 128)),
             whole((1, D)),
             halves_spec(depth, 2 * width),
             halves_spec(depth, 2 * width),
@@ -573,7 +580,7 @@
         out_shape=[
             jax.ShapeDtypeStruct((tps, rows, width), BF16),
             jax.ShapeDtypeStruct((rows // PATCH, D), F32),
-            jax.ShapeDtypeStruct((rows // PATCH, 1), F32),
+            jax.ShapeDtypeStruct((rows // PATCH, D + 128), BF16),
             jax.ShapeDtypeStruct((1, D), F32),
             halves_shape(tps, depth, 2 * width),
             halves_shape(tps, depth, 2 * width),
@@ -590,7 +597,7 @@
         cost_estimate=pl.CostEstimate(
             flops=4 * rows * D * D * 4, bytes_accessed=26 << 20, transcendentals=rows * 2048
         ),
-    )(core, grad, mixer_rows, inputs, normed, gain, weights, qkv, context, *tokens)
+    )(core, grad, mixer_rows, inputs, normed, gain, weights, qkv, context, squares, token)
 
 
 def shifted(block, distance):
@@ -675,21 +682,26 @@
 
 
 def reached(factors, states, distance):
-    count = lax.axis_size(SEQ)
     heads = factors.shape[0]
     columns = jnp.broadcast_to(factors[:, None], (heads, STATE))
     high, low = high_low(columns)
     packed = jnp.concatenate([states.reshape(-1, STATE).astype(BF16), high, low], axis=0)
-    total = jnp.zeros(states.shape, F32)
+    return reached_from(packed, distance).reshape(states.shape)
+
+
+def reached_from(packed, distance):
+    count = lax.axis_size(SEQ)
+    heads = packed.shape[0] // (HEAD_DIM + 2)
+    total = jnp.zeros((heads, HEAD_DIM, STATE), F32)
     chain = jnp.ones((heads, 1, 1), F32)
     for hop in range(1, count // 2 + 1):
         step = hop * distance
         route = [(i, i + step) for i in range(count) if 0 <= i + step < count]
         got = lax.ppermute(packed, SEQ, route).astype(F32)
-        total = total + chain * got[: -2 * heads].reshape(states.shape)
+        total = total + chain * got[: -2 * heads].reshape(total.shape)
         factor = (got[-2 * heads : -heads] + got[-heads:])[:, :1]
         chain = chain * factor[:, :, None]
-    return total
+    return total.reshape(-1, STATE)
 
 
 def tied(array, *tokens):
@@ -783,27 +795,31 @@
 
 
 def third_sum_kernel(one_ref, two_ref, three_ref, four_ref, *refs):
-    out_ref = refs[-1]
+    out_ref = refs[-2]
     half = one_ref.shape[1]
     out_ref[0, :half] = (one_ref[0].astype(F32) + two_ref[0].astype(F32)).astype(BF16)
     out_ref[0, half:] = (three_ref[0].astype(F32) + four_ref[0].astype(F32)).astype(BF16)
 
 
-def third_sum(kept_one, got_one, kept_two, got_two, tokens=()):
+def third_sum(kept_one, got_one, kept_two, got_two, carried):
     tps, half, cols = kept_one.shape
     return pl.pallas_call(
         third_sum_kernel,
         grid=(tps,),
         in_specs=[pl.BlockSpec((1, half, cols), lambda t: (t, 0, 0)) for _ in range(4)]
-        + [anywhere() for _ in tokens],
-        out_specs=pl.BlockSpec((1, 2 * half, cols), lambda t: (t, 0, 0)),
-        out_shape=jax.ShapeDtypeStruct((tps, 2 * half, cols), BF16),
+        + [anywhere()],
+        out_specs=[pl.BlockSpec((1, 2 * half, cols), lambda t: (t, 0, 0)), anywhere()],
+        out_shape=[
+            jax.ShapeDtypeStruct((tps, 2 * half, cols), BF16),
+            jax.ShapeDtypeStruct(carried.shape, carried.dtype),
+        ],
+        input_output_aliases={4: 1},
         compiler_params=parallel_params(1),
         name="third_sum",
         cost_estimate=pl.CostEstimate(
             flops=2 * kept_one.size, bytes_accessed=12 * kept_one.size, transcendentals=0
         ),
-    )(kept_one, got_one, kept_two, got_two, *tokens)
+    )(kept_one, got_one, kept_two, got_two, carried)
 
 
 def reduce_first(place, own, other, tokens=()):
@@ -817,16 +833,554 @@
     )
 
 
-def reduce_third(sums, tokens=()):
+def reduce_third(sums, carried):
     send_one, keep_one, send_two, keep_two = sums
-    return third_sum(keep_one, swap(send_one, "a"), keep_two, swap(send_two, "b"), tokens)
+    return third_sum(keep_one, swap(send_one, "a"), keep_two, swap(send_two, "b"), carried)
+
+
+def over_groups(part):
+    return lax.psum(part, "g") if lax.axis_size("g") > 1 else part
 
 
 def reduce_last(summed):
-    part = lax.psum_scatter(summed, "tp", scatter_dimension=0)
-    if lax.axis_size("g") > 1:
-        part = lax.psum(part, "g")
-    return lax.all_gather(part, INNER)
+    return over_groups(lax.psum_scatter(summed, "tp", scatter_dimension=0))
+
+
+def exchange_last(summed):
+    pieces = lax.all_to_all(summed, "tp", 0, 0)
+    return over_groups(jnp.sum(pieces.astype(F32), axis=0).astype(BF16))
+
+
+def unpack_kernel(
+    grads_ref,
+    expand_ref,
+    shrink_ref,
+    input_ref,
+    output_ref,
+    gate_ref,
+    inner_ref,
+    mixer_ref,
+    state_ref,
+):
+    wide = grads_ref.shape[2]
+    deep = D // GROUP
+    width = input_ref.shape[2]
+
+    def rows(low, count):
+        return grads_ref[0, low : low + count].astype(F32)
+
+    down = wide // GROUP
+    for p in range(PIECES):
+        base = 3 * deep * p
+        for i in range(2):
+            expand_ref[i, :, p * wide : (p + 1) * wide] = rows(base + i * deep, deep)
+        for i in range(D // wide):
+            shrink_ref[p, 0, :, i * wide : (i + 1) * wide] = rows(base + 2 * deep + i * down, down)
+    base = 3 * deep * PIECES
+    for k in range(3):
+        part = rows(base + (k % 2) * deep, deep)
+        input_ref[k] = part[:, (k // 2) * width : (k // 2 + 1) * width]
+    part = rows(base + deep, deep)[:, width:]
+    out_rows = width // GROUP
+    for i in range(D // width):
+        output_ref[:, i * width : (i + 1) * width] = part[i * out_rows : (i + 1) * out_rows]
+    base = base + 2 * deep
+    gate_ref[...] = rows(base, deep)
+    inner_ref[...] = rows(base + deep, deep)
+    for i in range(D // wide):
+        mixer_ref[:, i * wide : (i + 1) * wide] = rows(base + 2 * deep + i * down, down)
+    state = rows(base + 3 * deep, deep // 2)
+    half = wide // 2
+    for i in range(2):
+        state_ref[i * deep // 2 : (i + 1) * deep // 2] = state[:, i * half : (i + 1) * half]
+
+
+def unpack(grads, tps):
+    _, total, wide = grads.shape
+    deep, width, down = D // GROUP, D // tps, wide // GROUP
+    shapes = [
+        (2, D, PIECES * wide),
+        (PIECES, GROUP, down, D),
+        (3, D, width),
+        (width, D),
+        (D, wide),
+        (D, wide),
+        (wide, D),
+        (D, wide // 2),
+    ]
+    specs = [
+        pl.BlockSpec((2, deep, PIECES * wide), lambda j: (0, j, 0)),
+        pl.BlockSpec((PIECES, 1, down, D), lambda j: (0, j, 0, 0)),
+        pl.BlockSpec((3, deep, width), lambda j: (0, j, 0)),
+        pl.BlockSpec((width // GROUP, D), lambda j: (j, 0)),
+        pl.BlockSpec((deep, wide), lambda j: (j, 0)),
+        pl.BlockSpec((deep, wide), lambda j: (j, 0)),
+        pl.BlockSpec((down, D), lambda j: (j, 0)),
+        pl.BlockSpec((deep, wide // 2), lambda j: (j, 0)),
+    ]
+    outs = pl.pallas_call(
+        unpack_kernel,
+        grid=(GROUP,),
+        in_specs=[pl.BlockSpec((1, total, wide), lambda j: (j, 0, 0))],
+        out_specs=specs,
+        out_shape=[jax.ShapeDtypeStruct(shape, F32) for shape in shapes],
+        compiler_params=parallel_params(1),
+        name="unpack",
+        cost_estimate=pl.CostEstimate(
+            flops=grads.size, bytes_accessed=6 * grads.size, transcendentals=0
+        ),
+    )(grads)
+    outs = list(outs)
+    outs[1] = outs[1].reshape(PIECES * wide, D)
+    return outs
+
+
+def exact(left, right, dims):
+    return lax.dot_general(
+        left, right, (dims, ((), ())), precision=highest, preferred_element_type=F32
+    )
+
+
+NN, NT, TN = ((1,), (0,)), ((1,), (1,)), ((0,), (0,))
+
+
+def column(array, index):
+    lane = lax.broadcasted_iota(jnp.int32, array.shape, 1)
+    return jnp.sum(jnp.where(lane == index, array, 0.0), axis=1, keepdims=True)
+
+
+def by_head(pair, one, two):
+    lane = lax.broadcasted_iota(jnp.int32, pair, 1)
+    return jnp.where(lane < HEAD_DIM, one, two)
+
+
+def only_head(array, j):
+    lane = lax.broadcasted_iota(jnp.int32, array.shape, 1)
+    return jnp.where((lane // HEAD_DIM) == j, array, 0.0)
+
+
+def pair_of(ref, q):
+    return ref[:, pl.ds(pl.multiple_of(q * 128, 128), 128)]
+
+
+def gate_backward_kernel(
+    returned_ref,
+    weight_ref,
+    gain_ref,
+    gate_ref,
+    mixed_ref,
+    cmat_ref,
+    reach_ref,
+    factor_ref,
+    token_ref,
+    mix_ref,
+    gate_back_ref,
+    gain_grad_ref,
+    out_grad_ref,
+    packed_ref,
+):
+    back = returned_ref[:, :D]
+    extra = returned_ref[:, D:].astype(F32)
+    lane = lax.broadcasted_iota(jnp.int32, extra.shape, 1)
+    squares = jnp.sum(jnp.where(lane % 64 == 0, extra, 0.0), axis=1, keepdims=True)
+    dots = jnp.sum(jnp.where(lane % 64 == 32, extra, 0.0), axis=1, keepdims=True)
+    scale = lax.rsqrt(squares / DI + epsilon)
+    grad = mm_nt(back, weight_ref[...])
+    gate = gate_ref[...]
+    mixed = mixed_ref[...]
+    gain = gain_ref[...]
+    sigma = 1.0 / (1.0 + jnp.exp(-gate))
+    act = gate * sigma
+    normal = mixed * act * scale
+    mix_ref[...] = (normal * gain).astype(BF16)
+    gain_grad_ref[...] = jnp.sum(grad * normal, axis=0, keepdims=True)
+    gated_grad = scale * (grad * gain - normal * (dots / DI))
+    out_grad_ref[...] = gated_grad * act
+    gate_back_ref[...] = (gated_grad * mixed * sigma * (1.0 + gate * (1.0 - sigma))).astype(BF16)
+    reach = reach_ref[...]
+    cmat = cmat_ref[...]
+    width = gate.shape[1]
+    for q in range(width // 128):
+        part = out_grad_ref[:, q * 128 : (q + 1) * 128]
+        part = part * by_head(part.shape, column(reach, 2 * q), column(reach, 2 * q + 1))
+        packed_ref[q * 128 : (q + 1) * 128] = exact(part, cmat, TN).astype(BF16)
+    packed_ref[width:] = factor_ref[...]
+
+
+def gate_backward(returned, weight, gain, gate, mixed, cmat, reach, factors, token):
+    count, width = gate.shape
+    args = (returned, weight, gain, gate, mixed, cmat, reach, factors)
+    shapes = [
+        jax.ShapeDtypeStruct((count, width), BF16),
+        jax.ShapeDtypeStruct((count, width), BF16),
+        jax.ShapeDtypeStruct((1, width), F32),
+        jax.ShapeDtypeStruct((count, width), F32),
+        jax.ShapeDtypeStruct((width + factors.shape[0], STATE), BF16),
+    ]
+    return pl.pallas_call(
+        gate_backward_kernel,
+        grid=(1,),
+        in_specs=[whole(a.shape) for a in args] + [anywhere()],
+        out_specs=[whole(o.shape) for o in shapes],
+        out_shape=shapes,
+        compiler_params=params(),
+        name="gate_backward",
+        cost_estimate=pl.CostEstimate(
+            flops=2 * count * D * width, bytes_accessed=6 << 20, transcendentals=count * width
+        ),
+    )(*args, token)
+
+
+def chunk_backward_kernel(
+    grad_ref,
+    inner_ref,
+    bmat_ref,
+    cmat_ref,
+    logs_ref,
+    logs_row_ref,
+    steps_row_ref,
+    first_ref,
+    first_row_ref,
+    reach_ref,
+    skip_ref,
+    incoming_ref,
+    token_ref,
+    other_token_ref,
+    inner_grad_ref,
+    bmat_grad_ref,
+    cmat_grad_ref,
+    logs_grad_ref,
+    logs_row_grad_ref,
+    steps_row_grad_ref,
+    skip_grad_ref,
+    product_ref,
+    product_grad_ref,
+):
+    count = grad_ref.shape[0]
+    bmat, cmat = bmat_ref[...], cmat_ref[...]
+    product_ref[...] = exact(cmat, bmat, NT)
+    product_grad_ref[...] = jnp.zeros_like(product_grad_ref)
+    cmat_grad_ref[...] = jnp.zeros_like(cmat_grad_ref)
+    logs_grad_ref[...] = jnp.zeros_like(logs_grad_ref)
+    skip_grad_ref[...] = jnp.zeros_like(skip_grad_ref)
+
+    def one_pair(q, carry):
+        inner = pair_of(inner_ref, q)
+        grad = pair_of(grad_ref, q)
+        incoming = incoming_ref[pl.ds(pl.multiple_of(q * 128, 128), 128), :]
+        reading = exact(cmat, incoming, NT)
+        row = lax.broadcasted_iota(jnp.int32, (count, count), 0)
+        col = lax.broadcasted_iota(jnp.int32, (count, count), 1)
+        same = (first_ref[...] == first_row_ref[...]) & (col <= row)
+        logs = logs_ref[...]
+        reach = reach_ref[...]
+        skip = skip_ref[...]
+        total = jnp.zeros_like(inner)
+        reaches = []
+        for j in range(2):
+            h = 2 * q + j
+            own_grad = only_head(grad, j)
+            steps = steps_row_ref[pl.ds(h, 1), :]
+            diff = column(logs, h) - logs_row_ref[pl.ds(h, 1), :]
+            decay = jnp.where(same, jnp.exp(jnp.where(same, diff, 0.0)), 0.0)
+            both = exact(own_grad, inner, NT) * decay
+            mixing = decay * product_ref[...]
+            product_grad_ref[...] += both * steps
+            used = both * product_ref[...]
+            total = total + exact(mixing * steps, own_grad, TN)
+            over_rows = jnp.sum(used, axis=0, keepdims=True)
+            reached_here = column(reach, h)
+            reaches.append(reached_here)
+            logs_grad = jnp.sum(used * steps, axis=1, keepdims=True)
+            logs_grad = logs_grad + reached_here * jnp.sum(
+                own_grad * reading, axis=1, keepdims=True
+            )
+            lane = lax.broadcasted_iota(jnp.int32, logs.shape, 1)
+            logs_grad_ref[...] += jnp.where(lane == h, logs_grad, 0.0)
+            logs_row_grad_ref[pl.ds(h, 1), :] = -steps * over_rows
+            steps_row_grad_ref[pl.ds(h, 1), :] = over_rows
+            lane = lax.broadcasted_iota(jnp.int32, skip.shape, 1)
+            gained = jnp.sum(jnp.sum(own_grad * inner, axis=1, keepdims=True), axis=0, keepdims=True)
+            skip_grad_ref[...] += jnp.where(lane == h, gained, 0.0)
+        gains = by_head((1, 128), column(skip, 2 * q), column(skip, 2 * q + 1))
+        inner_grad_ref[:, pl.ds(pl.multiple_of(q * 128, 128), 128)] = total + gains * grad
+        weighted = grad * by_head(grad.shape, reaches[0], reaches[1])
+        cmat_grad_ref[...] += exact(weighted, incoming, NN)
+        return carry
+
+    lax.fori_loop(0, grad_ref.shape[1] // 128, one_pair, 0)
+    cmat_grad_ref[...] += exact(product_grad_ref[...], bmat, NN)
+    bmat_grad_ref[...] = exact(product_grad_ref[...], cmat, TN)
+
+
+def chunk_backward(args, *tokens):
+    count, width = args[0].shape
+    heads = args[5].shape[0]
+    shapes = [
+        jax.ShapeDtypeStruct((count, width), F32),
+        jax.ShapeDtypeStruct((count, STATE), F32),
+        jax.ShapeDtypeStruct((count, STATE), F32),
+        jax.ShapeDtypeStruct((count, heads), F32),
+        jax.ShapeDtypeStruct((heads, count), F32),
+        jax.ShapeDtypeStruct((heads, count), F32),
+        jax.ShapeDtypeStruct((1, heads), F32),
+    ]
+    return pl.pallas_call(
+        chunk_backward_kernel,
+        grid=(1,),
+        in_specs=[whole(a.shape) for a in args] + [anywhere() for _ in tokens],
+        out_specs=[whole(o.shape) for o in shapes],
+        out_shape=shapes,
+        scratch_shapes=[pltpu.VMEM((count, count), F32), pltpu.VMEM((count, count), F32)],
+        compiler_params=params(),
+        name="chunk_backward",
+        cost_estimate=pl.CostEstimate(
+            flops=24 * count * count * width, bytes_accessed=4 << 20, transcendentals=count * count * heads
+        ),
+    )(*args, *tokens)
+
+
+def front_backward_kernel(
+    later_ref,
+    incoming_ref,
+    inner_ref,
+    bmat_ref,
+    logs_ref,
+    steps_ref,
+    steps_row_ref,
+    raw_row_ref,
+    last_ref,
+    factor_ref,
+    rate_ref,
+    bias_ref,
+    inner_grad_ref,
+    bmat_grad_ref,
+    cmat_grad_ref,
+    logs_grad_ref,
+    logs_row_grad_ref,
+    steps_row_grad_ref,
+    padded_ref,
+    conv_ref,
+    keep_ref,
+    token_ref,
+    raw_grad_ref,
+    head_grad_ref,
+    conv_grad_ref,
+    step_back_ref,
+    bias_grad_ref,
+    decay_grad_ref,
+    act_grad_ref,
+    logs_total_ref,
+    steps_total_ref,
+    padded_grad_ref,
+):
+    count, width = inner_ref.shape
+    bmat = bmat_ref[...]
+    logs, steps, last = logs_ref[...], steps_ref[...], last_ref[...]
+    final = logs[count - 1 : count, :]
+    fading = jnp.exp(final - logs) * last
+    weights = fading * steps
+    logs_total_ref[...] = logs_grad_ref[...]
+    steps_total_ref[...] = jnp.zeros_like(steps_total_ref)
+    bmat_total = bmat_grad_ref[...]
+    lane = lax.broadcasted_iota(jnp.int32, logs.shape, 1)
+    row = lax.broadcasted_iota(jnp.int32, logs.shape, 0)
+    for q in range(width // 128):
+        cols = slice(q * 128, (q + 1) * 128)
+        later = later_ref[cols, :]
+        inner = inner_ref[:, cols]
+        reading = exact(bmat, later, NT)
+        spread = by_head(inner.shape, column(weights, 2 * q), column(weights, 2 * q + 1))
+        act_grad_ref[:, cols] = inner_grad_ref[:, cols] + spread * reading
+        bmat_total = bmat_total + exact(inner * spread, later, NN)
+        crossing = jnp.sum(later * incoming_ref[cols, :], axis=1, keepdims=True)
+        for j in range(2):
+            h = 2 * q + j
+            gained = jnp.sum(only_head(inner * reading, j), axis=1, keepdims=True)
+            part = lax.broadcasted_iota(jnp.int32, crossing.shape, 0) // HEAD_DIM == j
+            crossed = jnp.sum(jnp.where(part, crossing, 0.0), axis=0, keepdims=True)
+            crossed = crossed * column(factor_ref[...], h)
+            steps_total_ref[...] += jnp.where(lane == h, fading * gained, 0.0)
+            moved = column(weights, h) * gained
+            ending = jnp.sum(moved, axis=0, keepdims=True) + crossed
+            change = jnp.where(row == count - 1, ending - moved, -moved)
+            logs_total_ref[...] += jnp.where(lane == h, change, 0.0)
+    act_grad_ref[:, width : width + STATE] = bmat_total
+    act_grad_ref[:, width + STATE :] = cmat_grad_ref[...]
+    t = lax.broadcasted_iota(jnp.int32, (count, count), 0)
+    u = lax.broadcasted_iota(jnp.int32, (count, count), 1)
+    after = (t >= u).astype(F32)
+    here = (t == u).astype(F32)
+    reverse = exact(logs_total_ref[...], after, TN) + exact(logs_row_grad_ref[...], after, NN)
+    rate = rate_ref[...]
+    steps_grad = steps_row_grad_ref[...] + exact(steps_total_ref[...], here, TN) + rate * reverse
+    decay_grad_ref[...] = rate * jnp.sum(steps_row_ref[...] * reverse, axis=1, keepdims=True)
+    raw = raw_row_ref[...] + bias_ref[...]
+    step_grad = steps_grad / (1.0 + jnp.exp(-raw))
+    bias_grad_ref[...] = jnp.sum(step_grad, axis=1, keepdims=True)
+    step_back_ref[...] = step_grad.astype(BF16)
+    top = 8 - (CONV - 1)
+    pre = jnp.zeros(act_grad_ref.shape, F32)
+    keep = keep_ref[...]
+    for k in range(CONV):
+        kept = column(keep, k)
+        pre = pre + conv_ref[k : k + 1, :] * padded_ref[top + k : top + k + count, :] * kept
+    sigma = 1.0 / (1.0 + jnp.exp(-pre))
+    act_grad_ref[...] = act_grad_ref[...] * sigma * (1.0 + pre * (1.0 - sigma))
+    padded_grad_ref[...] = jnp.zeros_like(padded_grad_ref)
+    for k in range(CONV):
+        kept = act_grad_ref[...] * column(keep, k)
+        conv_grad_ref[k : k + 1, :] = jnp.sum(
+            kept * padded_ref[top + k : top + k + count, :], axis=0, keepdims=True
+        )
+        padded_grad_ref[top + k : top + k + count, :] += conv_ref[k : k + 1, :] * kept
+    raw_grad_ref[...] = padded_grad_ref[8:, :]
+    head_grad_ref[...] = padded_grad_ref[:8, :]
+
+
+def front_backward(args, token):
+    count, heads = args[4].shape
+    wide = args[18].shape[1]
+    shapes = [
+        jax.ShapeDtypeStruct((count, wide), F32),
+        jax.ShapeDtypeStruct((8, wide), F32),
+        jax.ShapeDtypeStruct((CONV, wide), F32),
+        jax.ShapeDtypeStruct((heads, count), BF16),
+        jax.ShapeDtypeStruct((heads, 1), F32),
+        jax.ShapeDtypeStruct((heads, 1), F32),
+    ]
+    return pl.pallas_call(
+        front_backward_kernel,
+        grid=(1,),
+        in_specs=[whole(a.shape) for a in args] + [anywhere()],
+        out_specs=[whole(o.shape) for o in shapes],
+        out_shape=shapes,
+        scratch_shapes=[
+            pltpu.VMEM((count, wide), F32),
+            pltpu.VMEM((count, heads), F32),
+            pltpu.VMEM((count, heads), F32),
+            pltpu.VMEM((count + 8, wide), F32),
+        ],
+        compiler_params=params(),
+        name="front_backward",
+        cost_estimate=pl.CostEstimate(
+            flops=24 * count * STATE * wide, bytes_accessed=8 << 20, transcendentals=2 * count * wide
+        ),
+    )(*args, token)
+
+
+def project_backward_kernel(
+    mine_ref,
+    gate_back_ref,
+    inner_back_ref,
+    state_back_ref,
+    step_back_ref,
+    gate_ref,
+    inner_ref,
+    state_ref,
+    step_ref,
+    rows_ref,
+    normed_ref,
+    gain_ref,
+    own_ref,
+    token_ref,
+    blocks_ref,
+    gain_grad_ref,
+    step_grad_ref,
+    total_ref,
+):
+    grad = mm_nt(gate_back_ref[...], gate_ref[...])
+    grad = grad + mm_nt(inner_back_ref[...], inner_ref[...])
+    grad = grad + mm_nt(state_back_ref[...], state_ref[...])
+    grad = grad + mm_tn(step_back_ref[...], step_ref[...])
+    step_grad_ref[...] = mm(step_back_ref[...], normed_ref[...])
+    values = rows_ref[...].astype(F32)
+    scale = inverse_rms(values)
+    normal = values * scale
+    gain_grad_ref[...] = jnp.sum(grad * normal, axis=0, keepdims=True)
+    scaled = grad * gain_ref[...]
+    total_ref[...] = scale * (scaled - normal * jnp.mean(scaled * normal, axis=-1, keepdims=True))
+    share = own_ref.shape[0]
+    at = pl.ds(pl.multiple_of(mine_ref[0] * share, share), share)
+    total_ref[at, :] += own_ref[...]
+    width = blocks_ref.shape[2]
+    for i in range(blocks_ref.shape[0]):
+        blocks_ref[i] = total_ref[:, i * width : (i + 1) * width].astype(BF16)
+
+
+def project_backward(mine, args, tps, token):
+    count = args[0].shape[0]
+    heads = args[3].shape[0]
+    shapes = [
+        jax.ShapeDtypeStruct((tps, count, D // tps), BF16),
+        jax.ShapeDtypeStruct((1, D), F32),
+        jax.ShapeDtypeStruct((heads, D), F32),
+    ]
+    return pl.pallas_call(
+        project_backward_kernel,
+        grid=(1,),
+        in_specs=[scalar_spec()] + [whole(a.shape) for a in args] + [anywhere()],
+        out_specs=[whole(o.shape) for o in shapes],
+        out_shape=shapes,
+        scratch_shapes=[pltpu.VMEM((count, D), F32)],
+        compiler_params=params(),
+        name="project_backward",
+        cost_estimate=pl.CostEstimate(
+            flops=2 * count * D * 1288, bytes_accessed=6 << 20, transcendentals=count
+        ),
+    )(mine, *args, token)
+
+
+def mixer_weight_grads_kernel(
+    core_ref,
+    normed_ref,
+    gate_ref,
+    inner_ref,
+    state_ref,
+    mix_ref,
+    back_ref,
+    token_ref,
+    own_ref,
+    other_ref,
+):
+    core = core_ref[0]
+    normed = normed_ref[...]
+    deep = D // GROUP
+    wide = gate_ref.shape[1]
+    put_halves(core, mm_tn(normed, gate_ref[...]), own_ref, other_ref, 0, deep)
+    put_halves(core, mm_tn(normed, inner_ref[...]), own_ref, other_ref, deep, 2 * deep)
+    rows = wide // GROUP
+    mix = mix_ref[...]
+    for i in range(D // wide):
+        low = 2 * deep + i * rows
+        grad = mm_tn(mix, back_ref[:, i * wide : (i + 1) * wide])
+        put_halves(core, grad, own_ref, other_ref, low, low + rows)
+    low = own_ref.shape[3] - deep // 2
+    own, other = core_halves(core, mm_tn(normed, state_ref[...]).astype(BF16))
+    for i in range(2):
+        cols = slice(i * wide // 2, (i + 1) * wide // 2)
+        rows_in = slice(i * deep // 2, (i + 1) * deep // 2)
+        own_ref[:, :, 0, low:, cols] = own[:, :, rows_in]
+        other_ref[:, :, 0, low:, cols] = other[:, :, rows_in]
+
+
+def mixer_weight_grads(core, normed, gate, inner, state, mix, back, token):
+    wide = gate.shape[1]
+    deep = D // GROUP
+    depth = 2 * deep + D // GROUP + deep // 2
+    args = (normed, gate, inner, state, mix, back)
+    return pl.pallas_call(
+        mixer_weight_grads_kernel,
+        grid=(1,),
+        in_specs=[scalar_spec()] + [whole(a.shape) for a in args] + [anywhere()],
+        out_specs=[halves_spec(depth, wide)] * 2,
+        out_shape=[halves_shape(1, depth, wide)] * 2,
+        compiler_params=params(),
+        name="mixer_weight_grads",
+        cost_estimate=pl.CostEstimate(
+            flops=8 * normed.shape[0] * D * wide, bytes_accessed=8 << 20, transcendentals=0
+        ),
+    )(core, *args, token)
 
 
 def shards(
@@ -874,10 +1428,6 @@
         rows_in = array.shape[0]
         return array.reshape(rows_in, -1, width).transpose(1, 0, 2).reshape(-1, width)
 
-    def unfolded(array, folds):
-        blocks = array.reshape(GROUP, folds, -1, array.shape[-1])
-        return blocks.transpose(0, 2, 1, 3).reshape(-1, folds * array.shape[-1])
-
     attn_in_part = lax.dynamic_slice_in_dim(attn_input, slot * narrow, narrow, 1)
     out_rows = attn_output.shape[0] // GROUP
     attn_out_part = lax.dynamic_slice_in_dim(attn_output, slot * out_rows, out_rows, 0)
@@ -924,26 +1474,13 @@
     padded = jnp.concatenate([before, raw], axis=0)
     conv_weight = jnp.concatenate([conv_inner, conv_state], axis=1)
 
-    def front_local(padded_in, step_in, conv_in, bias_in, decay_in):
-        return front_part(padded_in, step_in, conv_in, bias_in, decay_in, positions, first)
-
-    def summary_local(inner_in, bmat_in, steps_in, rates_in):
-        return block_summary(inner_in, bmat_in, steps_in, rates_in, positions, first)
-
-    def output_local(inner_in, bmat_in, cmat_in, steps_in, rates_in, skip_in, incoming_in):
-        return block_output(
-            inner_in, bmat_in, cmat_in, steps_in, rates_in, skip_in, incoming_in, positions, first
-        )
-
-    front_vals, front_pull = jax.vjp(
-        front_local, padded, step_raw, conv_weight, step_bias, decay_log
-    )
-    inner_vals, bmatrix, cmatrix, steps, rates = front_vals
-    summary, summary_pull = jax.vjp(summary_local, inner_vals, bmatrix, steps, rates)
-    carried, states = summary
+    inner_vals, bmatrix, cmatrix, steps, rates = front_part(
+        padded, step_raw, conv_weight, step_bias, decay_log, positions, first
+    )
+    carried, states = block_summary(inner_vals, bmatrix, steps, rates, positions, first)
     incoming = reached(carried, states, 1)
-    mixed, output_pull = jax.vjp(
-        output_local, inner_vals, bmatrix, cmatrix, steps, rates, skip_gain, incoming
+    mixed = block_output(
+        inner_vals, bmatrix, cmatrix, steps, rates, skip_gain, incoming, positions, first
     )
     gate_act = jax.nn.silu(gate_vals)
     gated = mixed * gate_act
@@ -960,8 +1497,28 @@
     own_patches = lax.dynamic_slice_in_dim(patch_rows, mine * share, share, 0)
     global_out = own_patches.astype(F32) + mixer_rows
 
+    logs = jnp.cumsum(steps * rates[None, :], axis=0)
+    from_before = (first < positions[0]).astype(F32)[:, None]
+    reach = jnp.exp(logs) * from_before
+    factor_high, factor_low = high_low(jnp.broadcast_to(carried[:, None], (carried.size, STATE)))
+    factors = jnp.concatenate([factor_high, factor_low], axis=0)
+    flat_inner = inner_vals.reshape(count, -1)
+    flat_incoming = incoming.reshape(-1, STATE)
+    keep = jnp.stack(
+        [(positions - (CONV - 1 - k) >= first).astype(F32) for k in range(CONV)], axis=1
+    )
+    logs_row, steps_row, raw_row = logs.T, steps.T, step_raw.T
+    last = (first == first[-1]).astype(F32)[:, None]
+    rate_column, bias_column = rates[:, None], step_bias[:, None]
+    wide_padded = jnp.pad(padded, ((8 - tail, 0), (0, 0)))
+    step_weight = proj_step.T
+    prepared = (
+        reach, factors, keep, logs_row, steps_row, raw_row, last, rate_column, bias_column,
+        wide_padded, step_weight, flat_inner, flat_incoming,
+    )
+
     hidden, attn_in, attn_normed, qkv, context = attention_forward(
-        embed_rows, global_out[:, None, :], norm_attn[None, :], weights
+        embed_rows, global_out[:, None, :], norm_attn[None, :], weights, prepared
     )
     ffn_normed, ffn_turned, cot_whole, out_acc, normed_acc, own_first, other_first = (
         feed_forward_first(core, hidden, cot_rows, norm_ffn[None, :], weights)
@@ -981,8 +1538,8 @@
         first_two[0],
     )
     layer_output = to_columns(layer_blocks)
-    first_three = reduce_third(first_two, (hidden_grad,))
-    embed_blocks, own_grad, row_dot, norm_attn_part, own_attn, other_attn = attention_backward(
+    first_three, hidden_grad = reduce_third(first_two, hidden_grad)
+    embed_blocks, own_grad, payload, norm_attn_part, own_attn, other_attn = attention_backward(
         core,
         hidden_grad,
         mixer_rows,
@@ -992,78 +1549,111 @@
         weights,
         qkv,
         context,
-        (first_three, layer_output),
+        own_squares,
+        layer_output,
     )
     last_three = lax.psum_scatter(last_grad, INNER, scatter_dimension=0)
+    embed_columns = to_columns(embed_blocks)
+    embed_grad = embed_columns.astype(F32)
+
     attn_one = reduce_first(place, own_attn, other_attn)
-    embed_grad = to_columns(embed_blocks).astype(F32)
-
-    extra_high, extra_low = high_low(
-        jnp.concatenate(
-            [jnp.broadcast_to(v, (share, 32)) for v in (own_squares, row_dot)], axis=1
+    returned = lax.all_gather(payload, "tp", axis=0, tiled=True)
+    mix_back_in = returned[:, :D]
+    mix_low, gate_back, mixer_gain_grad, mixed_grad, packed = gate_backward(
+        returned,
+        proj_mixer,
+        mixer_gain[None, :],
+        gate_vals,
+        mixed,
+        cmatrix,
+        reach,
+        factors,
+        attn_one[0],
+    )
+    attn_two = reduce_second(place, attn_one, (packed,))
+    ffn_sums = tied(jnp.concatenate([first_three, last_three], axis=1), packed)
+    ffn_part = reduce_last(ffn_sums)
+    chunk_grads = chunk_backward(
+        (
+            mixed_grad,
+            flat_inner,
+            bmatrix,
+            cmatrix,
+            logs,
+            logs_row,
+            steps_row,
+            first[:, None],
+            first[None, :],
+            reach,
+            skip_gain[None, :],
+            flat_incoming,
+        ),
+        attn_two[0],
+        ffn_sums,
+    )
+    skip_gain_grad = chunk_grads[6][0]
+    later_grad = reached_from(packed, -1)
+    raw_grad, head_grad, conv_grad, step_back, step_bias_grad, decay_log_grad = front_backward(
+        (
+            later_grad,
+            flat_incoming,
+            flat_inner,
+            bmatrix,
+            logs,
+            steps,
+            steps_row,
+            raw_row,
+            last,
+            carried[None, :],
+            rate_column,
+            bias_column,
         )
-    )
-    returned = lax.all_gather(
-        jnp.concatenate([own_grad.astype(BF16), extra_high, extra_low], axis=1),
-        "tp",
-        axis=0,
-        tiled=True,
-    )
-    mix_back_in = returned[:, :D]
-    extras = returned[:, D : D + 64].astype(F32) + returned[:, D + 64 :].astype(F32)
-    all_squares, all_dots = tied(extras[:, :1], attn_one[0]), extras[:, 32:33]
-    row_scale = lax.rsqrt(all_squares / DI + epsilon)
-    row_mean = all_dots / DI
-    normed_mix = gated * row_scale
-    mix_low = (normed_mix * mixer_gain[None, :]).astype(jnp.bfloat16)
-    proj_mixer_grad = product(mix_low, mix_back_in, "rc,rd->cd")
-    mix_low_grad = product(mix_back_in, proj_mixer, "rd,cd->rc")
-    mixer_gain_grad = jnp.sum(mix_low_grad * normed_mix, axis=0)
-    scaled_grad = mix_low_grad * mixer_gain[None, :]
-    gated_grad = row_scale * (scaled_grad - normed_mix * row_mean)
-    mixed_grad = gated_grad * gate_act
-    sigma_gate = jax.nn.sigmoid(gate_vals)
-    gate_vals_grad = gated_grad * mixed * sigma_gate * (1.0 + gate_vals * (1.0 - sigma_gate))
-    inner_one, bmat_one, cmat_one, steps_one, rates_one, skip_gain_grad, incoming_grad = (
-        output_pull(mixed_grad)
-    )
-    attn_two = reduce_second(place, attn_one, (incoming_grad,))
-    attn_three = reduce_third(attn_two)
-    later_grad = reached(carried, tied(incoming_grad, attn_two[0]), -1)
-    later_grad = tied(later_grad, attn_three)
-    carried_grad = jnp.sum(later_grad * incoming, axis=(1, 2))
-    inner_two, bmat_two, steps_two, rates_two = summary_pull((carried_grad, later_grad))
-    padded_grad, step_raw_grad, conv_grad, step_bias_grad, decay_log_grad = front_pull(
+        + tuple(chunk_grads[:6])
+        + (
+            wide_padded,
+            conv_weight,
+            keep,
+        ),
+        attn_two[1],
+    )
+    step_bias_grad, decay_log_grad = step_bias_grad[:, 0], decay_log_grad[:, 0]
+    tail_grad = shifted(head_grad, -1)
+    raw_grad = jnp.concatenate(
+        [raw_grad[: count - 8], raw_grad[count - 8 :] + tail_grad], axis=0
+    ).astype(BF16)
+    inner_back, state_back = raw_grad[:, :inner_width], raw_grad[:, inner_width:]
+    own_mixer, other_mixer = mixer_weight_grads(
+        core, normed, gate_back, inner_back, state_back, mix_low, mix_back_in, attn_two[1]
+    )
+    mixer_one = reduce_first(place, own_mixer, other_mixer)
+    attn_three, mixer_kept = reduce_third(attn_two, mixer_one[1])
+    attn_part = reduce_last(tied(attn_three, ffn_part))
+    mixer_two = reduce_second(place, (mixer_one[0], mixer_kept) + tuple(mixer_one[2:]))
+    mixer_three, step_back = reduce_third(mixer_two, step_back)
+    mixer_three = mixer_three[0]
+    mixer_part = over_groups(mixer_three)
+    state_rows = lax.all_gather(mixer_part[3 * narrow :], "tp")
+    state_rows = jnp.sum(state_rows.astype(F32), axis=0).astype(BF16)
+    columns, norm_global_part, step_grad = project_backward(
+        mine.reshape(1),
         (
-            inner_one + inner_two,
-            bmat_one + bmat_two,
-            cmat_one,
-            steps_one + steps_two,
-            rates_one + rates_two,
-        )
-    )
-    tail_grad = shifted(padded_grad[:tail], -1)
-    raw_grad = padded_grad[tail:]
-    raw_grad = jnp.concatenate(
-        [raw_grad[: count - tail], raw_grad[count - tail :] + tail_grad], axis=0
-    )
-    gate_back = gate_vals_grad.astype(jnp.bfloat16)
-    inner_back = raw_grad[:, :inner_width].astype(jnp.bfloat16)
-    state_back = raw_grad[:, inner_width:].astype(jnp.bfloat16)
-    step_back = step_raw_grad.astype(jnp.bfloat16)
-    normed_grad_part = (
-        product(gate_back, proj_gate, "rc,dc->rd")
-        + product(inner_back, proj_inner, "rc,dc->rd")
-        + product(step_back, proj_step, "rc,dc->rd")
-        + product(state_back, proj_state, "rs,ds->rd")
-    )
-    part_in_grad, norm_global_part = norm_backward(normed_grad_part, global_in, norm_global)
-    part_in_grad = lax.dynamic_update_slice_in_dim(
-        part_in_grad,
-        lax.dynamic_slice_in_dim(part_in_grad, mine * share, share, 0) + own_grad,
-        mine * share,
-        0,
-    )
+            gate_back,
+            inner_back,
+            state_back,
+            step_back,
+            proj_gate,
+            proj_inner,
+            proj_state,
+            step_weight,
+            patch_rows,
+            normed,
+            norm_global[None, :],
+            own_grad,
+        ),
+        tps,
+        state_rows,
+    )
+    norm_global_part = norm_global_part[0]
     shared = jnp.concatenate(
         [
             conv_grad[:, inner_width:].reshape(-1),
@@ -1074,7 +1664,6 @@
     ).reshape(-1, quarter)
     shared_high, shared_low = high_low(shared)
     shared_rows = jnp.concatenate([shared_high, shared_low], axis=0)
-    columns = part_in_grad.astype(BF16).reshape(count, tps, quarter).transpose(1, 0, 2)
     returned = lax.all_to_all(
         jnp.concatenate(
             [columns, jnp.broadcast_to(shared_rows[None], (tps,) + shared_rows.shape)], axis=1
@@ -1093,26 +1682,6 @@
         shared[held : held + D],
         shared[held + D : held + 2 * D],
         shared[held + 2 * D :],
-    )
-    state_all = lax.all_gather(state_back, "tp")
-    state_sum = jnp.sum(state_all.astype(F32), axis=0).astype(BF16)
-    early_grads = lax.psum(
-        (
-            product(normed, gate_back, "rd,rc->dc").astype(BF16),
-            proj_mixer_grad.astype(BF16),
-        ),
-        SEQ,
-    )
-    late_grads = lax.psum(
-        (
-            product(normed, inner_back, "rd,rc->dc").astype(BF16),
-            product(normed, state_sum, "rd,rc->dc").astype(BF16),
-        ),
-        SEQ,
-    )
-    proj_grads = (early_grads[0], late_grads[0], late_grads[1], early_grads[1])
-    proj_gate_grad, proj_inner_grad, proj_state_grad, proj_mixer_grad = (
-        g.astype(F32) for g in proj_grads
     )
     (
         conv_state_grad,
@@ -1128,36 +1697,29 @@
     ) = lax.psum(
         shared
         + (
-            product(normed, step_back, "rd,rc->dc"),
+            step_grad.T,
             step_bias_grad,
             decay_log_grad,
             conv_grad[:, :inner_width],
             skip_gain_grad,
-            mixer_gain_grad,
+            mixer_gain_grad[0],
         ),
         SEQ,
     )
     ffn_depth, attn_depth = 3 * narrow, 2 * narrow
-    all_grads = reduce_last(jnp.concatenate([first_three, last_three, attn_three], axis=1))
-    ffn_grads = [all_grads[:, i * ffn_depth : (i + 1) * ffn_depth] for i in range(PIECES)]
-    attn_grad = all_grads[:, PIECES * ffn_depth :]
-    expand_grad = jnp.concatenate(
-        [
-            g[:, : 2 * narrow].reshape(GROUP, 2, narrow, wide).transpose(1, 0, 2, 3).reshape(2, D, wide)
-            for g in ffn_grads
-        ],
-        axis=2,
-    ).astype(F32)
-    shrink_grad = jnp.concatenate(
-        [unfolded(g[:, 2 * narrow :], D // wide) for g in ffn_grads], axis=0
-    ).astype(F32)
-    attn_input_grad = jnp.stack(
-        [
-            attn_grad[:, (k % 2) * narrow : (k % 2 + 1) * narrow, (k // 2) * quarter : (k // 2 + 1) * quarter]
-            for k in range(3)
-        ]
-    ).reshape(3, D, quarter).astype(F32)
-    attn_output_grad = unfolded(attn_grad[:, narrow:, quarter:], D // quarter).astype(F32)
+    all_grads = lax.all_gather(
+        jnp.concatenate([ffn_part, attn_part, mixer_part[: 3 * narrow], state_rows]), INNER
+    )
+    (
+        expand_grad,
+        shrink_grad,
+        attn_input_grad,
+        attn_output_grad,
+        proj_gate_grad,
+        proj_inner_grad,
+        proj_mixer_grad,
+        proj_state_grad,
+    ) = unpack(all_grads, tps)
     return (
         layer_output,
         embed_grad,

time: 739 us -> 678 us (0.917)
  waiting for transfers between devices: 292 us -> 220 us
  Pallas kernels: 113 us -> 147 us
  matrix products: 41.5 us -> 12.6 us
  starting transfers between devices: 50.5 us -> 70.8 us
  other arithmetic: 50.1 us -> 33.1 us
    all_gather x1, waiting for transfers between devices: 48.9 us -> 1.5 us  [shards(): lax.all_gather(jnp.concatenate([ffn_part, attn_part, mixer_part[:3 * narr...]
    all_gather x2, waiting for transfers between devices: 78.9 us -> 37.9 us  [gather_weights(): lax.all_gather(part, INNER + ('tp',)).reshape((GROUP, tps) + part.shape)]
    pallas_call x0 -> x6, Pallas kernels: none -> 37 us  [the longest x1 8.47 us: chunk_backward(): pl.pallas_call(chunk_backward_kernel, grid=(1,), in_specs=[whole(a.shape)...]
    all_gather x1, blocking collectives: 20.3 us -> 51.9 us  [shards(): patch_rows = lax.all_gather(patches, 'tp', axis=1, tiled=True)]
    all_to_all x0 -> x1, waiting for transfers between devices: none -> 31.3 us  [shards(): lax.all_to_all(sent.reshape(tps, share, -1), 'tp', 0, 0).astype(F32)]
    all_to_all x1 -> x0, blocking collectives: 18.9 us -> none  [shards(): lax.all_to_all(sent.reshape(tps, share, -1), 'tp', 0, 0).astype(F32)]
    dot_general x15 -> x5, matrix products: 21.1 us -> 5.56 us  [product(): return jnp.einsum(form, left, right, preferred_element_type=jnp.float32)]
    ppermute x10 -> x15, starting transfers between devices: 9.82 us -> 24.1 us  [swap(): return lax.ppermute(array, axis, [(0, 1), (1, 0)])]
  transfers between devices with their start and end apart: 31 -> 37, of which waited for: 22 -> 20; matrix products, arithmetic and copies ran while one was open for 15% -> 9% of each run, Pallas kernels for 11% -> 16%
where the time goes in v3:
time: 678 us; the launch traced here: 669 us
  waiting for transfers between devices  220 us (32%)
  Pallas kernels  147 us (22%)
  blocking collectives  109 us (16%)
  starting transfers between devices  70.8 us (10%)
  local copies, waits for them, and re-layouts  57.3 us (8%)
  other arithmetic  33.1 us (5%)
  between operations  19 us (3%)
  matrix products  12.6 us (2%)
    ppermute x15, waiting for transfers between devices, swap(): return lax.ppermute(array, axis, [(0, 1), (1, 0)])  122 us
    all_gather x1, blocking collectives, shards(): patch_rows = lax.all_gather(patches, 'tp', axis=1, tiled=True)  51.9 us
    all_gather x2, waiting for transfers between devices, gather_weights(): lax.all_gather(part, INNER + ('tp',)).reshape((GROUP, tps) + part.shape)  37.9 us
    all_to_all x1, waiting for transfers between devices, shards(): lax.all_to_all(sent.reshape(tps, share, -1), 'tp', 0, 0).astype(F32)  31.3 us
    pallas_call x1, Pallas kernels, feed_forward_last(): pl.pallas_call(feed_forward_last_kernel, grid=(tps,), in_specs=[scalar_sp...  30.1 us
    unnamed x160, local copies, waits for them, and re-layouts  27.2 us
    pallas_call x1, Pallas kernels, feed_forward_first(): pl.pallas_call(feed_forward_first_kernel, grid=(tps,), in_specs=[scalar_s...  26.6 us
    pallas_call x1, Pallas kernels, attention_backward(): pl.pallas_call(attention_backward_kernel, grid=(tps,), in_specs=[scalar_s...  26.6 us
  transfers between devices with their start and end apart: 37, of which 20 were waited for; matrix products, arithmetic and copies ran while one was open for 9% of the time, Pallas kernels for 16%

profile of v3, /device:TPU:0, one launch (start us, length us, event | category | flops | bytes accessed | tf_op | source)
XLA Modules:
  0.0 669.1 jit_solution(9290114577788728823)
XLA Ops:
  13.3 6.5 all-to-all-start
  19.8 51.9 %all_gather.28.rows_ref = bf16[256,1024]{1,0:T(8,128)(2,1)S(1)} all-gather(bf16[256,256]{1,0:T(8,128)(2,1)S(1)} %copy-done.52), channel_id=1, replica_groups=mesh['g'=1,'a'=2,'b'=2,'c'=2,'tp'=4] {'tp'}, dimensions={1}, use_global_device_ids=true | all-gather | bytes 655360 | tf_op jit(solution)/shard_map/all_gather | solution.py:1463
  88.3 3.9 collective-permute-start.4
  92.1 2.5 collective-permute-start.3
  94.6 3.4 collective-permute-start.2
  99.8 3.6 fusion.10
  107.5 3.1 multiply_reduce_fusion
  115.2 5.3 all-to-all-start.1
  123.0 31.3 %all-to-all-done.1 = bf16[4,64,1152]{2,1,0:T(8,128)(2,1)S(1)} async-done(((bf16[4,64,1152]{2,1,0:T(8,128)(2,1)}), bf16[4,64,1152]{2,1,0:T(8,128)(2,1)S(1)}, u32[]{:S(2)}, u32[]{:S(2)}) %all-to-all-start.1) | async-done | bytes 589856 | tf_op jit(solution)/shard_map/all_to_all | solution.py:1493
  154.3 4.3 all-to-all-start.2
  165.8 35.5 %all-gather.7.cloned.1.call-done = bf16[20480,512]{1,0:T(8,128)(2,1)} async-done(((bf16[640,512]{1,0:T(8,128)(2,1)}), bf16[20480,512]{1,0:T(8,128)(2,1)}) %all-gather.7.cloned.1.call-update) | async-done | bytes 20971536 | tf_op jit(solution)/shard_map/all_gather | solution.py:1425
  201.3 14.7 %attention_forward.1 = (f32[512,1024]{1,0:T(8,128)}, bf16[512,1024]{1,0:T(8,128)(2,1)}, bf16[512,1024]{1,0:T(8,128)(2,1)}, bf16[4,3,512,256]{3,2,1,0:T(8,128)(2,1)}, bf16[4,512,256]{2,1,0:T(8,128)(2,1)}) custom-call(bf16[4,512,256]{2,1,0:T(8,128)(2,1)} %all-to-all-done.embed_ref, f32[64,1,1024]{2,1,0:T(1,128)} %copy.175.global_ref, f32[1,1024]{1,0:T(1,128)} %bitcast.154, ...), custom_call_target="tpu_custom_call" | custom-call | flops 4294967296 | bytes 14680064 | tf_op jit(solution)/shard_map/attention_forward/pallas_call | solution.py:162
  216.0 26.6 %feed_forward_first.1 = (bf16[512,1024]{1,0:T(8,128)(2,1)}, bf16[1024,512]{1,0:T(8,128)(2,1)}, bf16[512,1024]{1,0:T(8,128)(2,1)}, f32[512,1024]{1,0:T(8,128)}, f...) custom-call(s32[1]{0:T(128)} %bitcast.core_ref, ...), custom_call_target="tpu_custom_call" | custom-call | flops 19327352832 | bytes 33554432 | tf_op jit(solution)/shard_map/feed_forward_first/pallas_call | solution.py:363
  243.0 10.0 %collective-permute-done.5.refs_1_.refs_3_.refs_5_.refs_7_ = bf16[2,2,4,384,512]{4,3,2,1,0:T(8,128)(2,1)S(1)} collective-permute-done((bf16[2,2,4,384,512]{4,3,2,1,0:T(8,128)(2,1)}, bf16[2,2,4,384,512]{4,3,2,1,0:T(8,128)(2,1)S(1)}, u32[]{:S(2)}, u32[]{:S(2)}) %collective-permute-start.5) | collective-permute-done | bytes 6291488 | tf_op jit(solution)/shard_map/ppermute | solution.py:713
  253.1 2.8 copy-done.2
  255.8 2.3 first_sum.3
  258.2 2.9 collective-permute-start.6
  262.9 55.3 %collective-permute-done.6.refs_1_.refs_3_ = bf16[2,4,192,512]{3,2,1,0:T(8,128)(2,1)S(1)} collective-permute-done((bf16[2,4,192,512]{3,2,1,0:T(8,128)(2,1)S(1)}, bf16[2,4,192,512]{3,2,1,0:T(8,128)(2,1)S(1)}, u32[]{:S(2)}, u32[]{:S(2)}) %collective-permute-start.6) | collective-permute-done | bytes 1572896 | tf_op jit(solution)/shard_map/ppermute | solution.py:713
  322.3 2.4 all-gather.9.cloned.1.call-done
  324.6 30.1 %feed_forward_last.1 = (bf16[4,512,256]{2,1,0:T(8,128)(2,1)}, f32[512,1024]{1,0:T(8,128)}, f32[1,1024]{1,0:T(1,128)}, bf16[8,4,384,512]{3,2,1,0:T(8,128)(2,1)}) custom-call(s32[1]{0:T(128)} %bitcast.core_ref, f32[512,1024]{1,0:T(8,128)} %get-tuple-element.104.hidden_ref, bf16[512,1024]{1,0:T(8,128)(2,1)} %get-tuple-element.105.cot_ref, f32[1,1024]{1,0:T(1,128)} %bitcast.165, ...), custom_call_target="tpu_custom_call" | custom-call | flops 19327352832 | bytes 33554432 | tf_op jit(solution)/shard_map/feed_forward_last/pallas_call | solution.py:404
  354.8 4.4 all-to-all-start.3
  361.3 17.9 %collective-permute-done.9.four_ref = bf16[4,192,512]{2,1,0:T(8,128)(2,1)S(1)} collective-permute-done((bf16[4,192,512]{2,1,0:T(8,128)(2,1)}, bf16[4,192,512]{2,1,0:T(8,128)(2,1)S(1)}, u32[]{:S(2)}, u32[]{:S(2)}) %collective-permute-start.9) | collective-permute-done | bytes 786464 | tf_op jit(solution)/shard_map/ppermute | solution.py:713
  385.7 26.6 %attention_backward.1 = (bf16[4,512,256]{2,1,0:T(8,128)(2,1)}, f32[64,1024]{1,0:T(8,128)}, bf16[64,1152]{1,0:T(8,128)(2,1)}, f32[1,1024]{1,0:T(1,128)}, bf16[2,2...) custom-call(s32[1]{0:T(128)} %bitcast.core_ref, f32[512,1024]{1,0:T(8,128)} %copy-done.9, ...), custom_call_target="tpu_custom_call" | custom-call | flops 8589934592 | bytes 27262976 | tf_op jit(solution)/shard_map/attention_backward/pallas_call | solution.py:556
  414.0 17.8 %all_gather.33.returned_ref = bf16[256,1152]{1,0:T(8,128)(2,1)} all-gather(bf16[64,1152]{1,0:T(8,128)(2,1)} %get-tuple-element.128), channel_id=1, replica_groups=mesh['g'=1,'a'=2,'b'=2,'c'=2,'tp'=4] {'tp'}, dimensions={0}, use_global_device_ids=true | all-gather | bytes 737280 | tf_op jit(solution)/shard_map/all_gather | solution.py:1560
  436.8 4.2 gate_backward.1
  442.8 2.7 reduce-scatter.4.cloned.1.call-done
  445.5 4.2 add_convert_fusion.other_token_ref
  455.8 3.3 collective-permute-start.15
  459.1 4.2 collective-permute-start.16
  475.3 10.9 %collective-permute-done.16.refs_5_.refs_7_ = bf16[2,4,128,512]{3,2,1,0:T(8,128)(2,1)} collective-permute-done((bf16[2,4,128,512]{3,2,1,0:T(8,128)(2,1)}, bf16[2,4,128,512]{3,2,1,0:T(8,128)(2,1)}, u32[]{:S(2)}, u32[]{:S(2)}) %collective-permute-start.16) | collective-permute-done | bytes 1048608 | tf_op jit(solution)/shard_map/ppermute | solution.py:713
  486.3 3.1 second_sum.4
  491.8 8.5 %chunk_backward.1 = (f32[256,512]{1,0:T(8,128)}, f32[256,128]{1,0:T(8,128)}, f32[256,128]{1,0:T(8,128)}, f32[256,8]{1,0:T(8,128)}, f32[8,256]{1,0:T(8,128)}, /*index=5*/f32[8,256]{1,0:T(8,128)}, f32[1,8]{1,0:T(1,128)}) custom-call(f32[256,512]{1,0:T(8,128)} %get-tuple-element.134.grad_ref, f32[256,512]{1,0:T(8,128)} %copy-done.25, ...), custom_call_target="tpu_custom_call" | custom-call | flops 805306368 | bytes 4194304 | tf_op jit(solution)/shard_map/chunk_backward/pallas_call | solution.py:1128
  500.3 6.4 front_backward.1
  512.2 4.6 mixer_weight_grads.1
  516.8 3.5 collective-permute-start.20
  520.3 2.6 collective-permute-start.19
  526.5 8.7 %collective-permute-done.19.four_ref = bf16[4,128,512]{2,1,0:T(8,128)(2,1)S(1)} collective-permute-done((bf16[4,128,512]{2,1,0:T(8,128)(2,1)S(1)}, bf16[4,128,512]{2,1,0:T(8,128)(2,1)S(1)}, u32[]{:S(2)}, u32[]{:S(2)}) %collective-permute-start.19) | collective-permute-done | bytes 524320 | tf_op jit(solution)/shard_map/ppermute | solution.py:713
  541.3 10.1 %collective-permute-done.21.refs_1_.refs_3_ = bf16[2,1,224,512]{3,2,1,0:T(8,128)(2,1)S(1)} collective-permute-done((bf16[2,1,224,512]{3,2,1,0:T(8,128)(2,1)S(1)}, bf16[2,1,224,512]{3,2,1,0:T(8,128)(2,1)S(1)}, u32[]{:S(2)}, u32[]{:S(2)}) %collective-permute-start.21) | collective-permute-done | bytes 458784 | tf_op jit(solution)/shard_map/ppermute | solution.py:713
  554.7 4.1 collective-permute-done.23.two_ref
  559.9 15.0 %all_gather.34 = bf16[4,64,512]{2,1,0:T(8,128)(2,1)S(1)} all-gather(bf16[1,64,512]{2,1,0:T(8,128)(2,1)S(1)} %slice.283), channel_id=1, replica_groups=mesh['g'=1,'a'=2,'b'=2,'c'=2,'tp'=4] {'tp'}, dimensions={0}, use_global_device_ids=true | all-gather | bytes 327680 | tf_op jit(solution)/shard_map/all_gather | solution.py:1635
  577.2 3.5 all-to-all-start.4
  582.6 5.1 project_backward.1
  591.1 11.6 %all-to-all-done.4 = bf16[4,512,256]{2,1,0:T(8,128)(2,1)S(1)} async-done(((bf16[4,512,256]{2,1,0:T(8,128)(2,1)}), bf16[4,512,256]{2,1,0:T(8,128)(2,1)S(1)}, u32[]{:S(2)}, u32[]{:S(2)}) %all-to-all-start.4) | async-done | bytes 1048608 | tf_op jit(solution)/shard_map/all_to_all | solution.py:1459
  602.7 3.5 all-to-all-start.5
  608.0 12.2 %all-to-all-done.5 = bf16[4,288,256]{2,1,0:T(8,128)(2,1)S(1)} async-done(((bf16[4,288,256]{2,1,0:T(8,128)(2,1)}), bf16[4,288,256]{2,1,0:T(8,128)(2,1)S(1)}, u32[]{:S(2)}, u32[]{:S(2)}) %all-to-all-start.5) | async-done | bytes 589856 | tf_op jit(solution)/shard_map/all_to_all | solution.py:1667
  621.0 24.7 %all-reduce.1 = (f32[1024]{0:T(1024)}, f32[1024,8]{0,1:T(8,128)}, f32[8]{0:T(128)}, f32[8]{0:T(128)}, f32[4,512]{1,0:T(4,128)}, /*index=5*/f32[4,256]{1,0:T(4,12...) all-reduce(f32[1024]{0:T(1024)S(1)} %bitcast.152, ...), channel_id=1, replica_groups=mesh['g'=1,'a'=2,'b'=2,'c'=2,'tp'=4] {'g','a','b','c'}, use_global_device_ids=true, to_apply=%region_10.11 | all-reduce | flops 14872 | bytes 118976 | tf_op jit(solution)/shard_map/psum | solution.py:1697
  647.2 4.4 copy-done.5
  651.6 8.2 %unpack.1 = (f32[2,1024,1024]{2,1,0:T(8,128)}, f32[2,8,64,1024]{3,2,1,0:T(8,128)}, f32[3,1024,256]{2,1,0:T(8,128)}, f32[256,1024]{1,0:T(8,128)}, f32[1024,512]{1...) custom-call(bf16[8,1472,512]{2,1,0:T(8,128)(2,1)S(1)} %bitcast.108), custom_call_target="tpu_custom_call" | custom-call | flops 6029312 | bytes 36175872 | tf_op jit(solution)/shard_map/unpack/pallas_call | solution.py:921
  (364 shorter events, 115.6 us)
Async XLA Ops:
  7.2 194.1 %all-gather.7.cloned.1.call-start = ((), (), s32[]{:S(2)}) async-start(), calls=%async_computation.12 | async-start | bytes 21626880 | tf_op jit(solution)/shard_map/all_gather | solution.py:1425
  12.3 312.3 %all-gather.9.cloned.1.call-start = ((), (), s32[]{:S(2)}) async-start(), calls=%async_computation.13 | async-start | bytes 12976128 | tf_op jit(solution)/shard_map/all_gather | solution.py:1425
  12.5 59.4 %copy-start.57 = (f32[1024]{0:T(1024)S(1)}, f32[1024]{0:T(1024)}, u32[]{:S(2)}) copy-start(f32[1024]{0:T(1024)} %param.25) | copy-start | bytes 12292
  13.3 58.8 %copy-start.33 = (bf16[1024,256]{1,0:T(8,128)(2,1)S(1)}, bf16[1024,256]{1,0:T(8,128)(2,1)}, u32[]{:S(2)}) copy-start(bf16[1024,256]{1,0:T(8,128)(2,1)} %state_ref.1) | copy-start | bytes 1572868
  13.3 97.2 %all-to-all-start = ((bf16[4,512,256]{2,1,0:T(8,128)(2,1)}), bf16[4,512,256]{2,1,0:T(8,128)(2,1)}, u32[]{:S(2)}, u32[]{:S(2)}) async-start(bf16[4,512,256]{2,1,0:T(8,128)(2,1)} %bitcast.1), calls=%async_computation | async-start | bytes 2097152 | tf_op jit(solution)/shard_map/all_to_all | solution.py:1456
  19.8 52.7 %copy-start.30 = (bf16[1024,512]{1,0:T(8,128)(2,1)S(1)}, bf16[1024,512]{1,0:T(8,128)(2,1)}, u32[]{:S(2)}) copy-start(bf16[1024,512]{1,0:T(8,128)(2,1)} %inner_ref.1) | copy-start | bytes 3145732
  71.7 92.3 %copy-start.26 = (bf16[256,1024]{1,0:T(8,128)(2,1)}, bf16[256,1024]{1,0:T(8,128)(2,1)S(1)}, u32[]{:S(2)}) copy-start(bf16[256,1024]{1,0:T(8,128)(2,1)S(1)} %all_gather.28.rows_ref) | copy-start | bytes 1572868
  72.1 35.4 %copy-start.24 = (bf16[256,1024]{1,0:T(8,128)(2,1)}, bf16[256,1024]{1,0:T(8,128)(2,1)S(1)}, u32[]{:S(2)}) copy-start(bf16[256,1024]{1,0:T(8,128)(2,1)S(1)} %fusion.15.normed_ref) | copy-start | bytes 1572868
  72.9 10.8 %collective-permute-start = (f32[3,768]{1,0:T(4,128)S(1)}, f32[3,768]{1,0:T(4,128)S(1)}, u32[]{:S(2)}, u32[]{:S(2)}) collective-permute-start(f32[3,768]{1,0:T(4,128)S(1)} %fusion.48), channel_id=1, source_target_pairs={{0,4},{4,8},{8,12},{12,16},{16,20},{20,24},{24,28},{1,5},{5,9},{9,... | collective-permute-start | bytes 27656 | tf_op jit(solution)/shard_map/ppermute | solution.py:606
  75.0 47.0 %copy-start.55 = (s32[256]{0:T(256)}, s32[256]{0:T(256)S(1)}, u32[]{:S(2)}) copy-start(s32[256]{0:T(256)S(1)} %select_reduce_fusion) | copy-start | bytes 3076
  88.3 15.7 %collective-permute-start.4 = (bf16[528,128]{1,0:T(8,128)(2,1)S(1)}, bf16[528,128]{1,0:T(8,128)(2,1)S(1)}, u32[]{:S(2)}, u32[]{:S(2)}) collective-permute-start(bf16[528,128]{1,0:T(8,128)(2,1)S(1)} %pad_maximum_fusion.5), channel_id=1, source_target_pairs={{0,16},{4,20},{8,24},{12,28},{1,17},{5,21},{9,25},{13,29},{2,18},{... | collective-permute-start | bytes 405512 | tf_op jit(solution)/shard_map/ppermute | solution.py:700
  92.1 11.5 %collective-permute-start.3 = (bf16[528,128]{1,0:T(8,128)(2,1)S(1)}, bf16[528,128]{1,0:T(8,128)(2,1)S(1)}, u32[]{:S(2)}, u32[]{:S(2)}) collective-permute-start(bf16[528,128]{1,0:T(8,128)(2,1)S(1)} %pad_maximum_fusion.5), channel_id=1, source_target_pairs={{0,12},{4,16},{8,20},{12,24},{16,28},{1,13},{5,17},{9,21},{13,25},... | collective-permute-start | bytes 405512 | tf_op jit(solution)/shard_map/ppermute | solution.py:700
  94.6 8.9 %collective-permute-start.2 = (bf16[528,128]{1,0:T(8,128)(2,1)S(1)}, bf16[528,128]{1,0:T(8,128)(2,1)S(1)}, u32[]{:S(2)}, u32[]{:S(2)}) collective-permute-start(bf16[528,128]{1,0:T(8,128)(2,1)S(1)} %pad_maximum_fusion.5), channel_id=1, source_target_pairs={{0,8},{4,12},{8,16},{12,20},{16,24},{20,28},{1,9},{5,13},{9,17},{1... | collective-permute-start | bytes 405512 | tf_op jit(solution)/shard_map/ppermute | solution.py:700
  98.1 5.3 collective-permute-start.1
  115.2 39.1 %all-to-all-start.1 = ((bf16[4,64,1152]{2,1,0:T(8,128)(2,1)}), bf16[4,64,1152]{2,1,0:T(8,128)(2,1)S(1)}, u32[]{:S(2)}, u32[]{:S(2)}) async-start(bf16[4,64,1152]{2,1,0:T(8,128)(2,1)} %bitcast.23), calls=%async_computation.1 | async-start | bytes 1179648 | tf_op jit(solution)/shard_map/all_to_all | solution.py:1493
  122.0 39.7 %copy-start.35 = (s32[256,1]{1,0:T(8,128)}, s32[256,1]{1,0:T(8,128)S(1)}, u32[]{:S(2)}) copy-start(s32[256,1]{1,0:T(8,128)S(1)} %copy.173.first_ref) | copy-start | bytes 3076
  122.2 39.9 %copy-start.37 = (f32[528,128]{1,0:T(8,128)S(1)}, f32[528,128]{1,0:T(8,128)}, u32[]{:S(2)}) copy-start(f32[528,128]{1,0:T(8,128)} %copy-done.36) | copy-start | bytes 811012
  122.3 39.9 %copy-start.39 = (f32[528,128]{1,0:T(8,128)S(1)}, f32[528,128]{1,0:T(8,128)}, u32[]{:S(2)}) copy-start(f32[528,128]{1,0:T(8,128)} %copy-done.38) | copy-start | bytes 811012
  122.3 39.9 %copy-start.41 = (f32[528,128]{1,0:T(8,128)S(1)}, f32[528,128]{1,0:T(8,128)}, u32[]{:S(2)}) copy-start(f32[528,128]{1,0:T(8,128)} %copy-done.40) | copy-start | bytes 811012
  122.3 39.9 %copy-start.48 = (bf16[528,128]{1,0:T(8,128)(2,1)S(1)}, bf16[528,128]{1,0:T(8,128)(2,1)}, u32[]{:S(2)}) copy-start(bf16[528,128]{1,0:T(8,128)(2,1)} %copy-done.47) | copy-start | bytes 405508
  154.3 61.7 %all-to-all-start.2 = ((bf16[4,512,256]{2,1,0:T(8,128)(2,1)}), bf16[4,512,256]{2,1,0:T(8,128)(2,1)}, u32[]{:S(2)}, u32[]{:S(2)}) async-start(bf16[4,512,256]{2,1,0:T(8,128)(2,1)} %bitcast.128), calls=%async_computation.2 | async-start | bytes 2097152 | tf_op jit(solution)/shard_map/all_to_all | solution.py:1456
  158.6 287.0 %reduce-scatter.4.cloned.1.call-start = ((), (), s32[]{:S(2)}) async-start(), calls=%async_computation.9 | async-start | bytes 14155776 | tf_op jit(solution)/shard_map/reduce_scatter | solution.py:1555
  242.7 10.4 %collective-permute-start.5 = (bf16[2,2,4,384,512]{4,3,2,1,0:T(8,128)(2,1)}, bf16[2,2,4,384,512]{4,3,2,1,0:T(8,128)(2,1)S(1)}, u32[]{:S(2)}, u32[]{:S(2)}) collective-permute-start(bf16[2,2,4,384,512]{4,3,2,1,0:T(8,128)(2,1)} %get-tuple-element.111), channel_id=1, source_target_pairs={{0,4},{4,0},{1,5},{5,1},{2,6},{6,2},{3,7},{7,3},{8,12},{12,8},{9,1... | collective-permute-start | bytes 18874376 | tf_op jit(solution)/shard_map/ppermute | solution.py:713
  258.2 60.0 %collective-permute-start.6 = (bf16[2,4,192,512]{3,2,1,0:T(8,128)(2,1)S(1)}, bf16[2,4,192,512]{3,2,1,0:T(8,128)(2,1)S(1)}, u32[]{:S(2)}, u32[]{:S(2)}) collective-permute-start(bf16[2,4,192,512]{3,2,1,0:T(8,128)(2,1)S(1)} %get-tuple-element.113), channel_id=1, source_target_pairs={{0,8},{8,0},{1,9},{9,1},{2,10},{10,2},{3,11},{11,3},{4,12},{12,4},... | collective-permute-start | bytes 4718600 | tf_op jit(solution)/shard_map/ppermute | solution.py:713
  261.1 57.1 %collective-permute-start.7 = (bf16[2,4,192,512]{3,2,1,0:T(8,128)(2,1)S(1)}, bf16[2,4,192,512]{3,2,1,0:T(8,128)(2,1)S(1)}, u32[]{:S(2)}, u32[]{:S(2)}) collective-permute-start(bf16[2,4,192,512]{3,2,1,0:T(8,128)(2,1)S(1)} %get-tuple-element.115), channel_id=1, source_target_pairs={{0,16},{16,0},{1,17},{17,1},{2,18},{18,2},{3,19},{19,3},{4,20},{20... | collective-permute-start | bytes 4718600 | tf_op jit(solution)/shard_map/ppermute | solution.py:713
  354.8 30.9 %all-to-all-start.3 = ((bf16[4,512,256]{2,1,0:T(8,128)(2,1)}), bf16[4,512,256]{2,1,0:T(8,128)(2,1)}, u32[]{:S(2)}, u32[]{:S(2)}) async-start(bf16[4,512,256]{2,1,0:T(8,128)(2,1)} %get-tuple-element.117), calls=%async_computation.3 | async-start | bytes 2097152 | tf_op jit(solution)/shard_map/all_to_all | solution.py:1459
  359.2 177.7 %reduce-scatter.6.cloned.1.call-start = ((), (), s32[]{:S(2)}) async-start(), calls=%async_computation.10 | async-start | bytes 3932160 | tf_op jit(solution)/shard_map/reduce_scatter | solution.py:846
  359.2 20.0 %collective-permute-start.9 = (bf16[4,192,512]{2,1,0:T(8,128)(2,1)}, bf16[4,192,512]{2,1,0:T(8,128)(2,1)S(1)}, u32[]{:S(2)}, u32[]{:S(2)}) collective-permute-start(bf16[4,192,512]{2,1,0:T(8,128)(2,1)} %copy-done.21), channel_id=1, source_target_pairs={{0,8},{8,0},{1,9},{9,1},{2,10},{10,2},{3,11},{11,3},{4,12},{12,4},... | collective-permute-start | bytes 2359304 | tf_op jit(solution)/shard_map/ppermute | solution.py:713
  360.7 19.6 %collective-permute-start.8 = (bf16[4,192,512]{2,1,0:T(8,128)(2,1)}, bf16[4,192,512]{2,1,0:T(8,128)(2,1)S(1)}, u32[]{:S(2)}, u32[]{:S(2)}) collective-permute-start(bf16[4,192,512]{2,1,0:T(8,128)(2,1)} %copy-done.20), channel_id=1, source_target_pairs={{0,16},{16,0},{1,17},{17,1},{2,18},{18,2},{3,19},{19,3},{4,20},{20... | collective-permute-start | bytes 2359304 | tf_op jit(solution)/shard_map/ppermute | solution.py:713
  412.3 19.5 %collective-permute-start.10 = (bf16[2,2,4,256,512]{4,3,2,1,0:T(8,128)(2,1)}, bf16[2,2,4,256,512]{4,3,2,1,0:T(8,128)(2,1)S(1)}, u32[]{:S(2)}, u32[]{:S(2)}) collective-permute-start(bf16[2,2,4,256,512]{4,3,2,1,0:T(8,128)(2,1)} %get-tuple-element.130), channel_id=1, source_target_pairs={{0,4},{4,0},{1,5},{5,1},{2,6},{6,2},{3,7},{7,3},{8,12},{12,8},{9,1... | collective-permute-start | bytes 12582920 | tf_op jit(solution)/shard_map/ppermute | solution.py:713
  449.7 125.2 %reduce-scatter.8.cloned.1.call-start = ((), (), s32[]{:S(2)}) async-start(), calls=%async_computation.11 | async-start | bytes 1310720 | tf_op jit(solution)/shard_map/reduce_scatter | solution.py:846
  450.6 8.5 %collective-permute-start.13 = (bf16[528,128]{1,0:T(8,128)(2,1)S(1)}, bf16[528,128]{1,0:T(8,128)(2,1)S(1)}, u32[]{:S(2)}, u32[]{:S(2)}) collective-permute-start(bf16[528,128]{1,0:T(8,128)(2,1)S(1)} %copy-done.16), channel_id=1, source_target_pairs={{12,0},{16,4},{20,8},{24,12},{28,16},{13,1},{17,5},{21,9},{25,13},... | collective-permute-start | bytes 405512 | tf_op jit(solution)/shard_map/ppermute | solution.py:700
  451.9 11.4 %collective-permute-start.12 = (bf16[528,128]{1,0:T(8,128)(2,1)S(1)}, bf16[528,128]{1,0:T(8,128)(2,1)S(1)}, u32[]{:S(2)}, u32[]{:S(2)}) collective-permute-start(bf16[528,128]{1,0:T(8,128)(2,1)S(1)} %copy-done.16), channel_id=1, source_target_pairs={{8,0},{12,4},{16,8},{20,12},{24,16},{28,20},{9,1},{13,5},{17,9},{2... | collective-permute-start | bytes 405512 | tf_op jit(solution)/shard_map/ppermute | solution.py:700
  453.2 20.1 %collective-permute-start.14 = (bf16[528,128]{1,0:T(8,128)(2,1)S(1)}, bf16[528,128]{1,0:T(8,128)(2,1)}, u32[]{:S(2)}, u32[]{:S(2)}) collective-permute-start(bf16[528,128]{1,0:T(8,128)(2,1)S(1)} %copy-done.16), channel_id=1, source_target_pairs={{16,0},{20,4},{24,8},{28,12},{17,1},{21,5},{25,9},{29,13},{18,2},{... | collective-permute-start | bytes 405512 | tf_op jit(solution)/shard_map/ppermute | solution.py:700
  454.5 8.9 %collective-permute-start.11 = (bf16[528,128]{1,0:T(8,128)(2,1)S(1)}, bf16[528,128]{1,0:T(8,128)(2,1)S(1)}, u32[]{:S(2)}, u32[]{:S(2)}) collective-permute-start(bf16[528,128]{1,0:T(8,128)(2,1)S(1)} %copy-done.16), channel_id=1, source_target_pairs={{4,0},{8,4},{12,8},{16,12},{20,16},{24,20},{28,24},{5,1},{9,5},{13... | collective-permute-start | bytes 405512 | tf_op jit(solution)/shard_map/ppermute | solution.py:700
  455.8 30.5 %collective-permute-start.15 = (bf16[2,4,128,512]{3,2,1,0:T(8,128)(2,1)}, bf16[2,4,128,512]{3,2,1,0:T(8,128)(2,1)S(1)}, u32[]{:S(2)}, u32[]{:S(2)}) collective-permute-start(bf16[2,4,128,512]{3,2,1,0:T(8,128)(2,1)} %copy-done.11), channel_id=1, source_target_pairs={{0,8},{8,0},{1,9},{9,1},{2,10},{10,2},{3,11},{11,3},{4,12},{12,4},... | collective-permute-start | bytes 3145736 | tf_op jit(solution)/shard_map/ppermute | solution.py:713
  459.1 27.1 %collective-permute-start.16 = (bf16[2,4,128,512]{3,2,1,0:T(8,128)(2,1)}, bf16[2,4,128,512]{3,2,1,0:T(8,128)(2,1)}, u32[]{:S(2)}, u32[]{:S(2)}) collective-permute-start(bf16[2,4,128,512]{3,2,1,0:T(8,128)(2,1)} %copy-done.19), channel_id=1, source_target_pairs={{0,16},{16,0},{1,17},{17,1},{2,18},{18,2},{3,19},{19,3},{4,20},{20... | collective-permute-start | bytes 3145736 | tf_op jit(solution)/shard_map/ppermute | solution.py:713
  506.7 3.3 collective-permute-start.17
  516.8 7.2 %collective-permute-start.20 = (bf16[2,2,1,448,512]{4,3,2,1,0:T(8,128)(2,1)}, bf16[2,2,1,448,512]{4,3,2,1,0:T(8,128)(2,1)S(1)}, u32[]{:S(2)}, u32[]{:S(2)}) collective-permute-start(bf16[2,2,1,448,512]{4,3,2,1,0:T(8,128)(2,1)} %get-tuple-element.154), channel_id=1, source_target_pairs={{0,4},{4,0},{1,5},{5,1},{2,6},{6,2},{3,7},{7,3},{8,12},{12,8},{9,1... | collective-permute-start | bytes 5505032 | tf_op jit(solution)/shard_map/ppermute | solution.py:713
  520.3 14.8 %collective-permute-start.19 = (bf16[4,128,512]{2,1,0:T(8,128)(2,1)S(1)}, bf16[4,128,512]{2,1,0:T(8,128)(2,1)S(1)}, u32[]{:S(2)}, u32[]{:S(2)}) collective-permute-start(bf16[4,128,512]{2,1,0:T(8,128)(2,1)S(1)} %copy-done.23), channel_id=1, source_target_pairs={{0,8},{8,0},{1,9},{9,1},{2,10},{10,2},{3,11},{11,3},{4,12},{12,4},... | collective-permute-start | bytes 1572872 | tf_op jit(solution)/shard_map/ppermute | solution.py:713
  523.0 13.6 %collective-permute-start.18 = (bf16[4,128,512]{2,1,0:T(8,128)(2,1)S(1)}, bf16[4,128,512]{2,1,0:T(8,128)(2,1)S(1)}, u32[]{:S(2)}, u32[]{:S(2)}) collective-permute-start(bf16[4,128,512]{2,1,0:T(8,128)(2,1)S(1)} %copy-done.15), channel_id=1, source_target_pairs={{0,16},{16,0},{1,17},{17,1},{2,18},{18,2},{3,19},{19,3},{4,20},{20... | collective-permute-start | bytes 1572872 | tf_op jit(solution)/shard_map/ppermute | solution.py:713
  540.0 107.2 %all-gather.11.cloned.1.call-start = ((), (), s32[]{:S(2)}) async-start(), calls=%async_computation.14 | async-start | bytes 13565952 | tf_op jit(solution)/shard_map/all_gather | solution.py:1710
  540.0 11.4 %collective-permute-start.21 = (bf16[2,1,224,512]{3,2,1,0:T(8,128)(2,1)S(1)}, bf16[2,1,224,512]{3,2,1,0:T(8,128)(2,1)S(1)}, u32[]{:S(2)}, u32[]{:S(2)}) collective-permute-start(bf16[2,1,224,512]{3,2,1,0:T(8,128)(2,1)S(1)} %get-tuple-element.157), channel_id=1, source_target_pairs={{0,8},{8,0},{1,9},{9,1},{2,10},{10,2},{3,11},{11,3},{4,12},{12,4},... | collective-permute-start | bytes 1376264 | tf_op jit(solution)/shard_map/ppermute | solution.py:713
  540.5 11.4 %collective-permute-start.22 = (bf16[2,1,224,512]{3,2,1,0:T(8,128)(2,1)S(1)}, bf16[2,1,224,512]{3,2,1,0:T(8,128)(2,1)S(1)}, u32[]{:S(2)}, u32[]{:S(2)}) collective-permute-start(bf16[2,1,224,512]{3,2,1,0:T(8,128)(2,1)S(1)} %get-tuple-element.159), channel_id=1, source_target_pairs={{0,16},{16,0},{1,17},{17,1},{2,18},{18,2},{3,19},{19,3},{4,20},{20... | collective-permute-start | bytes 1376264 | tf_op jit(solution)/shard_map/ppermute | solution.py:713
  552.7 6.1 collective-permute-start.23
  553.7 6.0 collective-permute-start.24
  577.2 25.5 %all-to-all-start.4 = ((bf16[4,512,256]{2,1,0:T(8,128)(2,1)}), bf16[4,512,256]{2,1,0:T(8,128)(2,1)S(1)}, u32[]{:S(2)}, u32[]{:S(2)}) async-start(bf16[4,512,256]{2,1,0:T(8,128)(2,1)} %get-tuple-element.127), calls=%async_computation.4 | async-start | bytes 2097152 | tf_op jit(solution)/shard_map/all_to_all | solution.py:1459
  602.7 17.5 %all-to-all-start.5 = ((bf16[4,288,256]{2,1,0:T(8,128)(2,1)}), bf16[4,288,256]{2,1,0:T(8,128)(2,1)S(1)}, u32[]{:S(2)}, u32[]{:S(2)}) async-start(bf16[4,288,256]{2,1,0:T(8,128)(2,1)} %pad_maximum_fusion.3), calls=%async_computation.6 | async-start | bytes 1179648 | tf_op jit(solution)/shard_map/all_to_all | solution.py:1667
  (66 other events, 442.8 us)
Sparse Core Ops, SparseCore 0:
  12.5 188.8 all-gather.6
  204.8 119.7 all-gather.8
  354.9 90.5 reduce-scatter.3
  449.8 60.2 reduce-scatter.5
  540.1 27.1 reduce-scatter.7
  577.3 69.8 all-gather.10

commit v4 on v3

--- a/solution.py
+++ b/solution.py
@@ -1140,8 +1140,12 @@
     )(*args, *tokens)
 
 
-def front_backward_kernel(
-    later_ref,
+def front_backward_kernel(hops, *refs):
+    front_backward_body(refs[:hops], *refs[hops:])
+
+
+def front_backward_body(
+    got_refs,
     incoming_ref,
     inner_ref,
     bmat_ref,
@@ -1173,8 +1177,18 @@
     logs_total_ref,
     steps_total_ref,
     padded_grad_ref,
+    later_ref,
 ):
     count, width = inner_ref.shape
+    heads = width // HEAD_DIM
+    chain = jnp.ones((heads, STATE), F32)
+    for k, got_ref in enumerate(got_refs):
+        for h in range(heads):
+            at = slice(h * HEAD_DIM, (h + 1) * HEAD_DIM)
+            part = chain[h : h + 1] * got_ref[at, :].astype(F32)
+            later_ref[at, :] = part if k == 0 else later_ref[at, :] + part
+        factors = got_ref[width : width + 2 * heads, :].astype(F32)
+        chain = chain * (factors[:heads] + factors[heads:])
     bmat = bmat_ref[...]
     logs, steps, last = logs_ref[...], steps_ref[...], last_ref[...]
     final = logs[count - 1 : count, :]
@@ -1238,9 +1252,9 @@
     head_grad_ref[...] = padded_grad_ref[:8, :]
 
 
-def front_backward(args, token):
-    count, heads = args[4].shape
-    wide = args[18].shape[1]
+def front_backward(gots, args, token):
+    count, heads = args[3].shape
+    wide = args[17].shape[1]
     shapes = [
         jax.ShapeDtypeStruct((count, wide), F32),
         jax.ShapeDtypeStruct((8, wide), F32),
@@ -1250,9 +1264,9 @@
         jax.ShapeDtypeStruct((heads, 1), F32),
     ]
     return pl.pallas_call(
-        front_backward_kernel,
+        functools.partial(front_backward_kernel, len(gots)),
         grid=(1,),
-        in_specs=[whole(a.shape) for a in args] + [anywhere()],
+        in_specs=[whole(a.shape) for a in gots + args] + [anywhere()],
         out_specs=[whole(o.shape) for o in shapes],
         out_shape=shapes,
         scratch_shapes=[
@@ -1260,13 +1274,14 @@
             pltpu.VMEM((count, heads), F32),
             pltpu.VMEM((count, heads), F32),
             pltpu.VMEM((count + 8, wide), F32),
+            pltpu.VMEM(args[0].shape, F32),
         ],
         compiler_params=params(),
         name="front_backward",
         cost_estimate=pl.CostEstimate(
             flops=24 * count * STATE * wide, bytes_accessed=8 << 20, transcendentals=2 * count * wide
         ),
-    )(*args, token)
+    )(*gots, *args, token)
 
 
 def project_backward_kernel(
@@ -1421,9 +1436,6 @@
     narrow = D // GROUP
     slot = lax.axis_index(INNER)
 
-    def gather_weights(part):
-        return lax.all_gather(part, INNER + ("tp",)).reshape((GROUP, tps) + part.shape)
-
     def folded(array, width):
         rows_in = array.shape[0]
         return array.reshape(rows_in, -1, width).transpose(1, 0, 2).reshape(-1, width)
@@ -1448,8 +1460,8 @@
         jnp.concatenate([attn_in_part[0], attn_in_part[2]], axis=1),
         jnp.concatenate([attn_in_part[1], attn_out_part], axis=1),
     ]
-    weights = gather_weights(jnp.concatenate(attn_parts + ffn_parts[0], axis=0))
-    last_weights = gather_weights(jnp.concatenate(ffn_parts[1], axis=0))
+    weights_line = lax.all_gather(jnp.concatenate(attn_parts + ffn_parts[0], axis=0), "tp")
+    last_part = jnp.concatenate(ffn_parts[1], axis=0)
     place = jnp.stack([lax.axis_index("a"), lax.axis_index("b")]).astype(jnp.int32)
 
     def to_rows(array):
@@ -1478,6 +1490,7 @@
         padded, step_raw, conv_weight, step_bias, decay_log, positions, first
     )
     carried, states = block_summary(inner_vals, bmatrix, steps, rates, positions, first)
+    weights = lax.all_gather(tied(weights_line, states), INNER)
     incoming = reached(carried, states, 1)
     mixed = block_output(
         inner_vals, bmatrix, cmatrix, steps, rates, skip_gain, incoming, positions, first
@@ -1493,6 +1506,11 @@
         lax.all_to_all(sent.reshape(tps, share, -1), "tp", 0, 0).astype(F32), axis=0
     )
     own_squares = summed[:, D : D + 1] + summed[:, D + 64 : D + 65]
+    last_part = tied(last_part, own_squares)
+    last_line = lax.all_to_all(
+        jnp.broadcast_to(last_part[None], (tps,) + last_part.shape), "tp", 0, 0
+    )
+    last_weights = lax.all_gather(last_line, INNER)
     mixer_rows = summed[:, :D] * lax.rsqrt(own_squares / DI + epsilon)
     own_patches = lax.dynamic_slice_in_dim(patch_rows, mine * share, share, 0)
     global_out = own_patches.astype(F32) + mixer_rows
@@ -1570,7 +1588,6 @@
         factors,
         attn_one[0],
     )
-    attn_two = reduce_second(place, attn_one, (packed,))
     ffn_sums = tied(jnp.concatenate([first_three, last_three], axis=1), packed)
     ffn_part = reduce_last(ffn_sums)
     chunk_grads = chunk_backward(
@@ -1588,14 +1605,19 @@
             skip_gain[None, :],
             flat_incoming,
         ),
-        attn_two[0],
+        attn_one[0],
         ffn_sums,
     )
+    attn_two = reduce_second(place, attn_one, (chunk_grads[0],))
     skip_gain_grad = chunk_grads[6][0]
-    later_grad = reached_from(packed, -1)
+    devices = lax.axis_size(SEQ)
+    gots = tuple(
+        lax.ppermute(packed, SEQ, [(i + hop, i) for i in range(devices - hop)])
+        for hop in range(1, devices // 2 + 1)
+    )
     raw_grad, head_grad, conv_grad, step_back, step_bias_grad, decay_log_grad = front_backward(
+        gots,
         (
-            later_grad,
             flat_incoming,
             flat_inner,
             bmatrix,

time: 678 us -> 652 us (0.962)
  waiting for transfers between devices: 220 us -> 189 us
  blocking collectives: 109 us -> 120 us
    all_to_all x0 -> x1, blocking collectives: none -> 40.7 us  [shards(): lax.all_to_all(jnp.broadcast_to(last_part[None], (tps,) + last_part.shape...]
    all_gather x1, blocking collectives: 51.9 us -> 20.7 us  [shards(): patch_rows = lax.all_gather(patches, 'tp', axis=1, tiled=True)]
    all_gather x2 -> x3, waiting for transfers between devices: 37.9 us -> 22.3 us  [the longest x1 22.3 us: shards(): lax.all_gather(jnp.concatenate(attn_parts + ffn_parts[0], axis=0), 'tp')]
    all_to_all x1, waiting for transfers between devices: 31.3 us -> 16.9 us  [shards(): lax.all_to_all(sent.reshape(tps, share, -1), 'tp', 0, 0).astype(F32)]
    reduce_scatter x1, starting transfers between devices: 0.25 us -> 11.2 us  [shards(): last_three = lax.psum_scatter(last_grad, INNER, scatter_dimension=0)]
    ppermute x15, waiting for transfers between devices: 122 us -> 114 us  [swap(): return lax.ppermute(array, axis, [(0, 1), (1, 0)])]
    ppermute x15, starting transfers between devices: 24.1 us -> 16.2 us  [swap(): return lax.ppermute(array, axis, [(0, 1), (1, 0)])]
    mul x12 -> x6, local copies, waits for them, and re-layouts: 7.75 us -> 0.44 us  [reached_from(): total = total + chain * got[:-2 * heads].reshape(total.shape)]
  transfers between devices with their start and end apart: 37 -> 38, of which waited for: 20 -> 21; matrix products, arithmetic and copies ran while one was open for 9% -> 8% of each run, Pallas kernels for 16% -> 17%
where the time goes in v4:
time: 652 us; the launch traced here: 642 us
  waiting for transfers between devices  189 us (29%)
  Pallas kernels  147 us (23%)
  blocking collectives  120 us (18%)
  starting transfers between devices  70.7 us (11%)
  local copies, waits for them, and re-layouts  51.2 us (8%)
  other arithmetic  32 us (5%)
  between operations  20.4 us (3%)
  matrix products  12.6 us (2%)
    ppermute x15, waiting for transfers between devices, swap(): return lax.ppermute(array, axis, [(0, 1), (1, 0)])  114 us
    all_to_all x1, blocking collectives, shards(): lax.all_to_all(jnp.broadcast_to(last_part[None], (tps,) + last_part.shape...  40.7 us
    pallas_call x1, Pallas kernels, feed_forward_last(): pl.pallas_call(feed_forward_last_kernel, grid=(tps,), in_specs=[scalar_sp...  29.9 us
    pallas_call x1, Pallas kernels, feed_forward_first(): pl.pallas_call(feed_forward_first_kernel, grid=(tps,), in_specs=[scalar_s...  26.6 us
    pallas_call x1, Pallas kernels, attention_backward(): pl.pallas_call(attention_backward_kernel, grid=(tps,), in_specs=[scalar_s...  26.6 us
    unnamed x180, local copies, waits for them, and re-layouts  26.4 us
    psum x1, blocking collectives, shards(): lax.psum(shared + (step_grad.T, step_bias_grad, decay_log_grad, conv_grad...  25.7 us
    all_gather x1, waiting for transfers between devices, shards(): lax.all_gather(jnp.concatenate(attn_parts + ffn_parts[0], axis=0), 'tp')  22.3 us
  transfers between devices with their start and end apart: 38, of which 21 were waited for; matrix products, arithmetic and copies ran while one was open for 8% of the time, Pallas kernels for 17%

profile of v4, /device:TPU:0, one launch (start us, length us, event | category | flops | bytes accessed | tf_op | source)
XLA Modules:
  0.0 642.5 jit_solution(9153867572253110728)
XLA Ops:
  13.8 20.7 %all_gather.34.rows_ref = bf16[256,1024]{1,0:T(8,128)(2,1)S(1)} all-gather(bf16[256,256]{1,0:T(8,128)(2,1)S(1)} %copy-done.53), channel_id=1, replica_groups=mesh['g'=1,'a'=2,'b'=2,'c'=2,'tp'=4] {'tp'}, dimensions={1}, use_global_device_ids=true | all-gather | bytes 655360 | tf_op jit(solution)/shard_map/all_gather | solution.py:1475
  47.7 2.3 fusion.59
  51.2 22.3 %all-gather.9.cloned.1.call-done = bf16[2560,512]{1,0:T(8,128)(2,1)} async-done(((bf16[640,512]{1,0:T(8,128)(2,1)}), bf16[2560,512]{1,0:T(8,128)(2,1)}) %all-gather.9.cloned.1.call-update) | async-done | bytes 2621456 | tf_op jit(solution)/shard_map/all_gather | solution.py:1463
  73.5 3.7 add_convert_fusion.1
  77.3 4.4 all-to-all-start
  83.7 3.4 collective-permute-start.4
  87.1 2.8 collective-permute-start.3
  94.2 2.6 fusion.10
  96.9 5.1 collective-permute-done.2
  112.7 4.8 all-to-all-start.1
  117.6 16.9 %all-to-all-done.1 = bf16[4,64,1152]{2,1,0:T(8,128)(2,1)S(1)} async-done(((bf16[4,64,1152]{2,1,0:T(8,128)(2,1)}), bf16[4,64,1152]{2,1,0:T(8,128)(2,1)S(1)}, u32[]{:S(2)}, u32[]{:S(2)}) %all-to-all-start.1) | async-done | bytes 589856 | tf_op jit(solution)/shard_map/all_to_all | solution.py:1506
  136.2 40.7 %all_to_all.35 = bf16[4,384,512]{2,1,0:T(8,128)(2,1)} all-to-all(bf16[4,384,512]{2,1,0:T(8,128)(2,1)S(1)} %broadcast_in_dim.74), channel_id=1, replica_groups=mesh['g'=1,'a'=2,'b'=2,'c'=2,'tp'=4] {'tp'}, dimensions={0} | all-to-all | bytes 3145728 | tf_op jit(solution)/shard_map/all_to_all | solution.py:1510
  177.0 4.4 all-to-all-start.2
  181.4 11.2 %reduce-scatter.4.cloned.1.call-start = ((), (), s32[]{:S(2)}) async-start(), calls=%async_computation.10 | async-start | bytes 14155776 | tf_op jit(solution)/shard_map/reduce_scatter | solution.py:1573
  201.1 15.2 %attention_forward.1 = (f32[512,1024]{1,0:T(8,128)}, bf16[512,1024]{1,0:T(8,128)(2,1)}, bf16[512,1024]{1,0:T(8,128)(2,1)}, bf16[4,3,512,256]{3,2,1,0:T(8,128)(2,1)}, bf16[4,512,256]{2,1,0:T(8,128)(2,1)}) custom-call(bf16[4,512,256]{2,1,0:T(8,128)(2,1)} %all-to-all-done.embed_ref, f32[64,1,1024]{2,1,0:T(1,128)} %copy.175.global_ref, f32[1,1024]{1,0:T(1,128)} %bitcast.161, ...), custom_call_target="tpu_custom_call" | custom-call | flops 4294967296 | bytes 14680064 | tf_op jit(solution)/shard_map/attention_forward/pallas_call | solution.py:162
  216.4 26.6 %feed_forward_first.1 = (bf16[512,1024]{1,0:T(8,128)(2,1)}, bf16[1024,512]{1,0:T(8,128)(2,1)}, bf16[512,1024]{1,0:T(8,128)(2,1)}, f32[512,1024]{1,0:T(8,128)}, f...) custom-call(s32[1]{0:T(128)} %bitcast.core_ref, ...), custom_call_target="tpu_custom_call" | custom-call | flops 19327352832 | bytes 33554432 | tf_op jit(solution)/shard_map/feed_forward_first/pallas_call | solution.py:363
  243.1 11.7 %collective-permute-done.5.refs_1_.refs_3_.refs_5_.refs_7_ = bf16[2,2,4,384,512]{4,3,2,1,0:T(8,128)(2,1)S(1)} collective-permute-done((bf16[2,2,4,384,512]{4,3,2,1,0:T(8,128)(2,1)}, bf16[2,2,4,384,512]{4,3,2,1,0:T(8,128)(2,1)S(1)}, u32[]{:S(2)}, u32[]{:S(2)}) %collective-permute-start.5) | collective-permute-done | bytes 6291488 | tf_op jit(solution)/shard_map/ppermute | solution.py:713
  254.8 2.8 copy-done.2
  257.6 2.3 first_sum.3
  260.1 38.7 %collective-permute-done.6.refs_1_.refs_3_ = bf16[2,4,192,512]{3,2,1,0:T(8,128)(2,1)S(1)} collective-permute-done((bf16[2,4,192,512]{3,2,1,0:T(8,128)(2,1)S(1)}, bf16[2,4,192,512]{3,2,1,0:T(8,128)(2,1)S(1)}, u32[]{:S(2)}, u32[]{:S(2)}) %collective-permute-start.6) | collective-permute-done | bytes 1572896 | tf_op jit(solution)/shard_map/ppermute | solution.py:713
  302.8 29.9 %feed_forward_last.1 = (bf16[4,512,256]{2,1,0:T(8,128)(2,1)}, f32[512,1024]{1,0:T(8,128)}, f32[1,1024]{1,0:T(1,128)}, bf16[8,4,384,512]{3,2,1,0:T(8,128)(2,1)}) custom-call(s32[1]{0:T(128)} %bitcast.core_ref, f32[512,1024]{1,0:T(8,128)} %get-tuple-element.104.hidden_ref, bf16[512,1024]{1,0:T(8,128)(2,1)} %get-tuple-element.105.cot_ref, f32[1,1024]{1,0:T(1,128)} %bitcast.172, ...), custom_call_target="tpu_custom_call" | custom-call | flops 19327352832 | bytes 33554432 | tf_op jit(solution)/shard_map/feed_forward_last/pallas_call | solution.py:404
  332.7 4.7 all-to-all-start.4
  339.5 17.2 %collective-permute-done.9.four_ref = bf16[4,192,512]{2,1,0:T(8,128)(2,1)S(1)} collective-permute-done((bf16[4,192,512]{2,1,0:T(8,128)(2,1)}, bf16[4,192,512]{2,1,0:T(8,128)(2,1)S(1)}, u32[]{:S(2)}, u32[]{:S(2)}) %collective-permute-start.9) | collective-permute-done | bytes 786464 | tf_op jit(solution)/shard_map/ppermute | solution.py:713
  363.3 26.6 %attention_backward.1 = (bf16[4,512,256]{2,1,0:T(8,128)(2,1)}, f32[64,1024]{1,0:T(8,128)}, bf16[64,1152]{1,0:T(8,128)(2,1)}, f32[1,1024]{1,0:T(1,128)}, bf16[2,2...) custom-call(s32[1]{0:T(128)} %bitcast.core_ref, f32[512,1024]{1,0:T(8,128)} %copy-done.8, ...), custom_call_target="tpu_custom_call" | custom-call | flops 8589934592 | bytes 27262976 | tf_op jit(solution)/shard_map/attention_backward/pallas_call | solution.py:556
  391.6 17.9 %all_gather.41.returned_ref = bf16[256,1152]{1,0:T(8,128)(2,1)} all-gather(bf16[64,1152]{1,0:T(8,128)(2,1)} %get-tuple-element.128), channel_id=1, replica_groups=mesh['g'=1,'a'=2,'b'=2,'c'=2,'tp'=4] {'tp'}, dimensions={0}, use_global_device_ids=true | all-gather | bytes 737280 | tf_op jit(solution)/shard_map/all_gather | solution.py:1578
  409.5 2.2 copy-done.3
  414.3 4.2 gate_backward.1
  420.3 4.9 reduce-scatter.4.cloned.1.call-done
  425.3 4.2 add_convert_fusion.other_token_ref
  435.5 20.4 %collective-permute-done.16.refs_5_.refs_7_ = bf16[2,4,128,512]{3,2,1,0:T(8,128)(2,1)S(1)} collective-permute-done((bf16[2,4,128,512]{3,2,1,0:T(8,128)(2,1)}, bf16[2,4,128,512]{3,2,1,0:T(8,128)(2,1)S(1)}, u32[]{:S(2)}, u32[]{:S(2)}) %collective-permute-start.16) | collective-permute-done | bytes 1048608 | tf_op jit(solution)/shard_map/ppermute | solution.py:713
  457.1 8.7 %chunk_backward.1 = (f32[256,512]{1,0:T(8,128)}, f32[256,128]{1,0:T(8,128)}, f32[256,128]{1,0:T(8,128)}, f32[256,8]{1,0:T(8,128)}, f32[8,256]{1,0:T(8,128)}, /*index=5*/f32[8,256]{1,0:T(8,128)}, f32[1,8]{1,0:T(1,128)}) custom-call(f32[256,512]{1,0:T(8,128)} %get-tuple-element.134.grad_ref, f32[256,512]{1,0:T(8,128)} %copy-done.25, ...), custom_call_target="tpu_custom_call" | custom-call | flops 805306368 | bytes 4194304 | tf_op jit(solution)/shard_map/chunk_backward/pallas_call | solution.py:1128
  466.9 3.0 second_sum.4
  473.0 6.5 %front_backward.1 = (f32[256,768]{1,0:T(8,128)}, f32[8,768]{1,0:T(8,128)}, f32[4,768]{1,0:T(4,128)}, bf16[8,256]{1,0:T(8,128)(2,1)}, f32[8,1]{1,0:T(8,128)}, /*index=5*/f32[8,1]{1,0:T(8,128)}) custom-call(bf16[528,128]{1,0:T(8,128)(2,1)} %collective-permute-done.11.refs_0_, bf16[528,128]{1,0:T(8,128)(2,1)} %copy-done.51, bf16[528,128]{1,0:T(8,128)(2,1)} %copy-done.50, ...), custom_call_target="tpu_custom_call" | custom-call | flops 603979776 | bytes 8388608 | tf_op jit(solution)/shard_map/front_backward/pallas_call | solution.py:1266
  485.5 4.6 mixer_weight_grads.1
  490.1 3.6 collective-permute-start.20
  499.8 8.0 %collective-permute-done.18.two_ref = bf16[4,128,512]{2,1,0:T(8,128)(2,1)S(1)} collective-permute-done((bf16[4,128,512]{2,1,0:T(8,128)(2,1)S(1)}, bf16[4,128,512]{2,1,0:T(8,128)(2,1)S(1)}, u32[]{:S(2)}, u32[]{:S(2)}) %collective-permute-start.18) | collective-permute-done | bytes 524320 | tf_op jit(solution)/shard_map/ppermute | solution.py:713
  515.9 8.6 %collective-permute-done.21.refs_1_.refs_3_ = bf16[2,1,224,512]{3,2,1,0:T(8,128)(2,1)S(1)} collective-permute-done((bf16[2,1,224,512]{3,2,1,0:T(8,128)(2,1)S(1)}, bf16[2,1,224,512]{3,2,1,0:T(8,128)(2,1)S(1)}, u32[]{:S(2)}, u32[]{:S(2)}) %collective-permute-start.21) | collective-permute-done | bytes 458784 | tf_op jit(solution)/shard_map/ppermute | solution.py:713
  528.4 4.1 collective-permute-done.23.two_ref
  534.0 15.2 %all_gather.42 = bf16[4,64,512]{2,1,0:T(8,128)(2,1)S(1)} all-gather(bf16[1,64,512]{2,1,0:T(8,128)(2,1)S(1)} %slice.235), channel_id=1, replica_groups=mesh['g'=1,'a'=2,'b'=2,'c'=2,'tp'=4] {'tp'}, dimensions={0}, use_global_device_ids=true | all-gather | bytes 327680 | tf_op jit(solution)/shard_map/all_gather | solution.py:1657
  551.5 3.5 all-to-all-start.5
  557.0 5.0 project_backward.1
  565.3 11.0 %all-to-all-done.5 = bf16[4,512,256]{2,1,0:T(8,128)(2,1)S(1)} async-done(((bf16[4,512,256]{2,1,0:T(8,128)(2,1)}), bf16[4,512,256]{2,1,0:T(8,128)(2,1)S(1)}, u32[]{:S(2)}, u32[]{:S(2)}) %all-to-all-start.5) | async-done | bytes 1048608 | tf_op jit(solution)/shard_map/all_to_all | solution.py:1471
  576.3 3.5 all-to-all-start.6
  581.6 11.2 %all-to-all-done.6 = bf16[4,288,256]{2,1,0:T(8,128)(2,1)S(1)} async-done(((bf16[4,288,256]{2,1,0:T(8,128)(2,1)}), bf16[4,288,256]{2,1,0:T(8,128)(2,1)S(1)}, u32[]{:S(2)}, u32[]{:S(2)}) %all-to-all-start.6) | async-done | bytes 589856 | tf_op jit(solution)/shard_map/all_to_all | solution.py:1689
  593.7 25.7 %all-reduce.1 = (f32[1024]{0:T(1024)}, f32[1024,8]{0,1:T(8,128)}, f32[8]{0:T(128)}, f32[8]{0:T(128)}, f32[4,512]{1,0:T(4,128)}, /*index=5*/f32[4,256]{1,0:T(4,12...) all-reduce(f32[1024]{0:T(1024)S(1)} %bitcast.159, ...), channel_id=1, replica_groups=mesh['g'=1,'a'=2,'b'=2,'c'=2,'tp'=4] {'g','a','b','c'}, use_global_device_ids=true, to_apply=%region_10.11 | all-reduce | flops 14872 | bytes 118976 | tf_op jit(solution)/shard_map/psum | solution.py:1719
  620.6 4.4 copy-done.5
  625.0 8.2 %unpack.1 = (f32[2,1024,1024]{2,1,0:T(8,128)}, f32[2,8,64,1024]{3,2,1,0:T(8,128)}, f32[3,1024,256]{2,1,0:T(8,128)}, f32[256,1024]{1,0:T(8,128)}, f32[1024,512]{1...) custom-call(bf16[8,1472,512]{2,1,0:T(8,128)(2,1)S(1)} %bitcast.113), custom_call_target="tpu_custom_call" | custom-call | flops 6029312 | bytes 36175872 | tf_op jit(solution)/shard_map/unpack/pallas_call | solution.py:921
  633.2 2.3 copy.197
  (375 shorter events, 110.6 us)
Async XLA Ops:
  7.2 66.3 %all-gather.9.cloned.1.call-start = ((), (), s32[]{:S(2)}) async-start(), calls=%async_computation.13 | async-start | bytes 3276800 | tf_op jit(solution)/shard_map/all_gather | solution.py:1463
  10.1 24.6 %copy-start.64 = (f32[1024]{0:T(1024)S(1)}, f32[1024]{0:T(1024)}, u32[]{:S(2)}) copy-start(f32[1024]{0:T(1024)} %param.25) | copy-start | bytes 12292
  13.7 187.4 %all-gather.11.cloned.1.call-start = ((), (), s32[]{:S(2)}) async-start(), calls=%async_computation.14 | async-start | bytes 23592960 | tf_op jit(solution)/shard_map/all_gather | solution.py:1493
  34.5 164.9 %copy-start.26 = (bf16[256,1024]{1,0:T(8,128)(2,1)}, bf16[256,1024]{1,0:T(8,128)(2,1)S(1)}, u32[]{:S(2)}) copy-start(bf16[256,1024]{1,0:T(8,128)(2,1)S(1)} %all_gather.34.rows_ref) | copy-start | bytes 1572868
  34.9 70.9 %copy-start.24 = (bf16[256,1024]{1,0:T(8,128)(2,1)}, bf16[256,1024]{1,0:T(8,128)(2,1)S(1)}, u32[]{:S(2)}) copy-start(bf16[256,1024]{1,0:T(8,128)(2,1)S(1)} %fusion.15.normed_ref) | copy-start | bytes 1572868
  37.0 8.8 %collective-permute-start = (f32[3,768]{1,0:T(4,128)S(1)}, f32[3,768]{1,0:T(4,128)S(1)}, u32[]{:S(2)}, u32[]{:S(2)}) collective-permute-start(f32[3,768]{1,0:T(4,128)S(1)} %fusion.46), channel_id=1, source_target_pairs={{0,4},{4,8},{8,12},{12,16},{16,20},{20,24},{24,28},{1,5},{5,9},{9,... | collective-permute-start | bytes 27656 | tf_op jit(solution)/shard_map/ppermute | solution.py:606
  39.1 155.0 %copy-start.56 = (s32[256]{0:T(256)}, s32[256]{0:T(256)S(1)}, u32[]{:S(2)}) copy-start(s32[256]{0:T(256)S(1)} %select_reduce_fusion) | copy-start | bytes 3076
  42.0 52.2 %copy-start.52 = (f32[8,256]{1,0:T(8,128)}, f32[8,256]{1,0:T(8,128)S(1)}, u32[]{:S(2)}) copy-start(f32[8,256]{1,0:T(8,128)S(1)} %get-tuple-element.212.refs_4_.steps_row_ref.refs_9_) | copy-start | bytes 24580
  46.5 56.6 %copy-start.27 = (f32[256,768]{1,0:T(8,128)}, f32[256,768]{1,0:T(8,128)S(1)}, u32[]{:S(2)}) copy-start(f32[256,768]{1,0:T(8,128)S(1)} %divide_multiply_fusion) | copy-start | bytes 2359300
  46.6 30.7 %copy-start.25 = (f32[256,512]{1,0:T(8,128)}, f32[256,512]{1,0:T(8,128)S(1)}, u32[]{:S(2)}) copy-start(f32[256,512]{1,0:T(8,128)S(1)} %slice.260.refs_11_.inner_ref.refs_5_) | copy-start | bytes 1572868
  77.3 30.7 %all-to-all-start = ((bf16[4,512,256]{2,1,0:T(8,128)(2,1)}), bf16[4,512,256]{2,1,0:T(8,128)(2,1)}, u32[]{:S(2)}, u32[]{:S(2)}) async-start(bf16[4,512,256]{2,1,0:T(8,128)(2,1)} %bitcast.134), calls=%async_computation | async-start | bytes 2097152 | tf_op jit(solution)/shard_map/all_to_all | solution.py:1468
  83.7 19.4 %collective-permute-start.4 = (bf16[528,128]{1,0:T(8,128)(2,1)S(1)}, bf16[528,128]{1,0:T(8,128)(2,1)S(1)}, u32[]{:S(2)}, u32[]{:S(2)}) collective-permute-start(bf16[528,128]{1,0:T(8,128)(2,1)S(1)} %pad_maximum_fusion.4), channel_id=1, source_target_pairs={{0,16},{4,20},{8,24},{12,28},{1,17},{5,21},{9,25},{13,29},{2,18},{... | collective-permute-start | bytes 405512 | tf_op jit(solution)/shard_map/ppermute | solution.py:700
  87.1 15.0 %collective-permute-start.3 = (bf16[528,128]{1,0:T(8,128)(2,1)S(1)}, bf16[528,128]{1,0:T(8,128)(2,1)S(1)}, u32[]{:S(2)}, u32[]{:S(2)}) collective-permute-start(bf16[528,128]{1,0:T(8,128)(2,1)S(1)} %pad_maximum_fusion.4), channel_id=1, source_target_pairs={{0,12},{4,16},{8,20},{12,24},{16,28},{1,13},{5,17},{9,21},{13,25},... | collective-permute-start | bytes 405512 | tf_op jit(solution)/shard_map/ppermute | solution.py:700
  89.8 12.2 %collective-permute-start.2 = (bf16[528,128]{1,0:T(8,128)(2,1)S(1)}, bf16[528,128]{1,0:T(8,128)(2,1)S(1)}, u32[]{:S(2)}, u32[]{:S(2)}) collective-permute-start(bf16[528,128]{1,0:T(8,128)(2,1)S(1)} %pad_maximum_fusion.4), channel_id=1, source_target_pairs={{0,8},{4,12},{8,16},{12,20},{16,24},{20,28},{1,9},{5,13},{9,17},{1... | collective-permute-start | bytes 405512 | tf_op jit(solution)/shard_map/ppermute | solution.py:700
  91.8 5.1 collective-permute-start.1
  111.5 24.4 %copy-start.40 = (bf16[2,128,512]{2,1,0:T(8,128)(2,1)S(1)}, bf16[2,128,512]{2,1,0:T(8,128)(2,1)}, u32[]{:S(2)}) copy-start(bf16[2,128,512]{2,1,0:T(8,128)(2,1)} %get-tuple-element.213) | copy-start | bytes 786436
  112.7 21.8 %all-to-all-start.1 = ((bf16[4,64,1152]{2,1,0:T(8,128)(2,1)}), bf16[4,64,1152]{2,1,0:T(8,128)(2,1)S(1)}, u32[]{:S(2)}, u32[]{:S(2)}) async-start(bf16[4,64,1152]{2,1,0:T(8,128)(2,1)} %bitcast.23), calls=%async_computation.1 | async-start | bytes 1179648 | tf_op jit(solution)/shard_map/all_to_all | solution.py:1506
  117.5 185.3 %all-gather.13.cloned.1.call-start = ((), (), s32[]{:S(2)}) async-start(), calls=%async_computation.15 | async-start | bytes 14155776 | tf_op jit(solution)/shard_map/all_gather | solution.py:1513
  134.8 42.1 %copy-start.58 = (f32[64,1]{1,0:T(8,128)}, f32[64,1]{1,0:T(8,128)S(1)}, u32[]{:S(2)}) copy-start(f32[64,1]{1,0:T(8,128)S(1)} %get-tuple-element.204.squares_ref) | copy-start | bytes 772
  177.0 39.4 %all-to-all-start.2 = ((bf16[4,512,256]{2,1,0:T(8,128)(2,1)}), bf16[4,512,256]{2,1,0:T(8,128)(2,1)}, u32[]{:S(2)}, u32[]{:S(2)}) async-start(bf16[4,512,256]{2,1,0:T(8,128)(2,1)} %bitcast.135), calls=%async_computation.2 | async-start | bytes 2097152 | tf_op jit(solution)/shard_map/all_to_all | solution.py:1468
  181.4 243.8 %reduce-scatter.4.cloned.1.call-start = ((), (), s32[]{:S(2)}) async-start(), calls=%async_computation.10 | async-start | bytes 14155776 | tf_op jit(solution)/shard_map/reduce_scatter | solution.py:1573
  243.0 11.8 %collective-permute-start.5 = (bf16[2,2,4,384,512]{4,3,2,1,0:T(8,128)(2,1)}, bf16[2,2,4,384,512]{4,3,2,1,0:T(8,128)(2,1)S(1)}, u32[]{:S(2)}, u32[]{:S(2)}) collective-permute-start(bf16[2,2,4,384,512]{4,3,2,1,0:T(8,128)(2,1)} %get-tuple-element.111), channel_id=1, source_target_pairs={{0,4},{4,0},{1,5},{5,1},{2,6},{6,2},{3,7},{7,3},{8,12},{12,8},{9,1... | collective-permute-start | bytes 18874376 | tf_op jit(solution)/shard_map/ppermute | solution.py:713
  259.9 38.8 %collective-permute-start.6 = (bf16[2,4,192,512]{3,2,1,0:T(8,128)(2,1)S(1)}, bf16[2,4,192,512]{3,2,1,0:T(8,128)(2,1)S(1)}, u32[]{:S(2)}, u32[]{:S(2)}) collective-permute-start(bf16[2,4,192,512]{3,2,1,0:T(8,128)(2,1)S(1)} %get-tuple-element.113), channel_id=1, source_target_pairs={{0,8},{8,0},{1,9},{9,1},{2,10},{10,2},{3,11},{11,3},{4,12},{12,4},... | collective-permute-start | bytes 4718600 | tf_op jit(solution)/shard_map/ppermute | solution.py:713
  260.0 38.7 %collective-permute-start.7 = (bf16[2,4,192,512]{3,2,1,0:T(8,128)(2,1)S(1)}, bf16[2,4,192,512]{3,2,1,0:T(8,128)(2,1)S(1)}, u32[]{:S(2)}, u32[]{:S(2)}) collective-permute-start(bf16[2,4,192,512]{3,2,1,0:T(8,128)(2,1)S(1)} %get-tuple-element.115), channel_id=1, source_target_pairs={{0,16},{16,0},{1,17},{17,1},{2,18},{18,2},{3,19},{19,3},{4,20},{20... | collective-permute-start | bytes 4718600 | tf_op jit(solution)/shard_map/ppermute | solution.py:713
  332.7 25.1 %copy-start.7 = (f32[512,1024]{1,0:T(8,128)S(1)}, f32[512,1024]{1,0:T(8,128)}, u32[]{:S(2)}) copy-start(f32[512,1024]{1,0:T(8,128)} %get-tuple-element.121.refs_0_) | copy-start | bytes 6291460
  332.7 30.6 %all-to-all-start.4 = ((bf16[4,512,256]{2,1,0:T(8,128)(2,1)}), bf16[4,512,256]{2,1,0:T(8,128)(2,1)}, u32[]{:S(2)}, u32[]{:S(2)}) async-start(bf16[4,512,256]{2,1,0:T(8,128)(2,1)} %get-tuple-element.117), calls=%async_computation.4 | async-start | bytes 2097152 | tf_op jit(solution)/shard_map/all_to_all | solution.py:1471
  337.5 172.1 %reduce-scatter.6.cloned.1.call-start = ((), (), s32[]{:S(2)}) async-start(), calls=%async_computation.11 | async-start | bytes 3932160 | tf_op jit(solution)/shard_map/reduce_scatter | solution.py:846
  337.5 19.3 %collective-permute-start.9 = (bf16[4,192,512]{2,1,0:T(8,128)(2,1)}, bf16[4,192,512]{2,1,0:T(8,128)(2,1)S(1)}, u32[]{:S(2)}, u32[]{:S(2)}) collective-permute-start(bf16[4,192,512]{2,1,0:T(8,128)(2,1)} %copy-done.19), channel_id=1, source_target_pairs={{0,8},{8,0},{1,9},{9,1},{2,10},{10,2},{3,11},{11,3},{4,12},{12,4},... | collective-permute-start | bytes 2359304 | tf_op jit(solution)/shard_map/ppermute | solution.py:713
  338.9 18.9 %collective-permute-start.8 = (bf16[4,192,512]{2,1,0:T(8,128)(2,1)}, bf16[4,192,512]{2,1,0:T(8,128)(2,1)S(1)}, u32[]{:S(2)}, u32[]{:S(2)}) collective-permute-start(bf16[4,192,512]{2,1,0:T(8,128)(2,1)} %copy-done.18), channel_id=1, source_target_pairs={{0,16},{16,0},{1,17},{17,1},{2,18},{18,2},{3,19},{19,3},{4,20},{20... | collective-permute-start | bytes 2359304 | tf_op jit(solution)/shard_map/ppermute | solution.py:713
  389.9 19.6 %collective-permute-start.10 = (bf16[2,2,4,256,512]{4,3,2,1,0:T(8,128)(2,1)}, bf16[2,2,4,256,512]{4,3,2,1,0:T(8,128)(2,1)S(1)}, u32[]{:S(2)}, u32[]{:S(2)}) collective-permute-start(bf16[2,2,4,256,512]{4,3,2,1,0:T(8,128)(2,1)} %get-tuple-element.130), channel_id=1, source_target_pairs={{0,4},{4,0},{1,5},{5,1},{2,6},{6,2},{3,7},{7,3},{8,12},{12,8},{9,1... | collective-permute-start | bytes 12582920 | tf_op jit(solution)/shard_map/ppermute | solution.py:713
  429.5 119.8 %reduce-scatter.8.cloned.1.call-start = ((), (), s32[]{:S(2)}) async-start(), calls=%async_computation.12 | async-start | bytes 1310720 | tf_op jit(solution)/shard_map/reduce_scatter | solution.py:846
  429.5 26.3 %collective-permute-start.16 = (bf16[2,4,128,512]{3,2,1,0:T(8,128)(2,1)}, bf16[2,4,128,512]{3,2,1,0:T(8,128)(2,1)S(1)}, u32[]{:S(2)}, u32[]{:S(2)}) collective-permute-start(bf16[2,4,128,512]{3,2,1,0:T(8,128)(2,1)} %copy-done.17), channel_id=1, source_target_pairs={{0,16},{16,0},{1,17},{17,1},{2,18},{18,2},{3,19},{19,3},{4,20},{20... | collective-permute-start | bytes 3145736 | tf_op jit(solution)/shard_map/ppermute | solution.py:713
  430.9 34.9 %collective-permute-start.15 = (bf16[2,4,128,512]{3,2,1,0:T(8,128)(2,1)}, bf16[2,4,128,512]{3,2,1,0:T(8,128)(2,1)}, u32[]{:S(2)}, u32[]{:S(2)}) collective-permute-start(bf16[2,4,128,512]{3,2,1,0:T(8,128)(2,1)} %copy-done.6), channel_id=1, source_target_pairs={{0,8},{8,0},{1,9},{9,1},{2,10},{10,2},{3,11},{11,3},{4,12},{12,4},... | collective-permute-start | bytes 3145736 | tf_op jit(solution)/shard_map/ppermute | solution.py:713
  431.6 40.6 %collective-permute-start.14 = (bf16[528,128]{1,0:T(8,128)(2,1)}, bf16[528,128]{1,0:T(8,128)(2,1)S(1)}, u32[]{:S(2)}, u32[]{:S(2)}) collective-permute-start(bf16[528,128]{1,0:T(8,128)(2,1)} %get-tuple-element.133), channel_id=1, source_target_pairs={{16,0},{20,4},{24,8},{28,12},{17,1},{21,5},{25,9},{29,13},{18,2},{... | collective-permute-start | bytes 405512 | tf_op jit(solution)/shard_map/ppermute | solution.py:1615
  432.9 39.3 %collective-permute-start.13 = (bf16[528,128]{1,0:T(8,128)(2,1)}, bf16[528,128]{1,0:T(8,128)(2,1)S(1)}, u32[]{:S(2)}, u32[]{:S(2)}) collective-permute-start(bf16[528,128]{1,0:T(8,128)(2,1)} %get-tuple-element.133), channel_id=1, source_target_pairs={{12,0},{16,4},{20,8},{24,12},{28,16},{13,1},{17,5},{21,9},{25,13},... | collective-permute-start | bytes 405512 | tf_op jit(solution)/shard_map/ppermute | solution.py:1615
  434.2 38.0 %collective-permute-start.12 = (bf16[528,128]{1,0:T(8,128)(2,1)}, bf16[528,128]{1,0:T(8,128)(2,1)S(1)}, u32[]{:S(2)}, u32[]{:S(2)}) collective-permute-start(bf16[528,128]{1,0:T(8,128)(2,1)} %get-tuple-element.133), channel_id=1, source_target_pairs={{8,0},{12,4},{16,8},{20,12},{24,16},{28,20},{9,1},{13,5},{17,9},{2... | collective-permute-start | bytes 405512 | tf_op jit(solution)/shard_map/ppermute | solution.py:1615
  455.8 16.4 %collective-permute-start.11 = (bf16[528,128]{1,0:T(8,128)(2,1)}, bf16[528,128]{1,0:T(8,128)(2,1)}, u32[]{:S(2)}, u32[]{:S(2)}) collective-permute-start(bf16[528,128]{1,0:T(8,128)(2,1)} %get-tuple-element.133), channel_id=1, source_target_pairs={{4,0},{8,4},{12,8},{16,12},{20,16},{24,20},{28,24},{5,1},{9,5},{13... | collective-permute-start | bytes 405512 | tf_op jit(solution)/shard_map/ppermute | solution.py:1615
  479.4 3.9 collective-permute-start.17
  490.1 7.2 %collective-permute-start.20 = (bf16[2,2,1,448,512]{4,3,2,1,0:T(8,128)(2,1)}, bf16[2,2,1,448,512]{4,3,2,1,0:T(8,128)(2,1)S(1)}, u32[]{:S(2)}, u32[]{:S(2)}) collective-permute-start(bf16[2,2,1,448,512]{4,3,2,1,0:T(8,128)(2,1)} %get-tuple-element.154), channel_id=1, source_target_pairs={{0,4},{4,0},{1,5},{5,1},{2,6},{6,2},{3,7},{7,3},{8,12},{12,8},{9,1... | collective-permute-start | bytes 5505032 | tf_op jit(solution)/shard_map/ppermute | solution.py:713
  493.6 14.1 %collective-permute-start.18 = (bf16[4,128,512]{2,1,0:T(8,128)(2,1)S(1)}, bf16[4,128,512]{2,1,0:T(8,128)(2,1)S(1)}, u32[]{:S(2)}, u32[]{:S(2)}) collective-permute-start(bf16[4,128,512]{2,1,0:T(8,128)(2,1)S(1)} %copy-done.23), channel_id=1, source_target_pairs={{0,16},{16,0},{1,17},{17,1},{2,18},{18,2},{3,19},{19,3},{4,20},{20... | collective-permute-start | bytes 1572872 | tf_op jit(solution)/shard_map/ppermute | solution.py:713
  495.2 14.0 %collective-permute-start.19 = (bf16[4,128,512]{2,1,0:T(8,128)(2,1)S(1)}, bf16[4,128,512]{2,1,0:T(8,128)(2,1)S(1)}, u32[]{:S(2)}, u32[]{:S(2)}) collective-permute-start(bf16[4,128,512]{2,1,0:T(8,128)(2,1)S(1)} %copy-done.21), channel_id=1, source_target_pairs={{0,8},{8,0},{1,9},{9,1},{2,10},{10,2},{3,11},{11,3},{4,12},{12,4},... | collective-permute-start | bytes 1572872 | tf_op jit(solution)/shard_map/ppermute | solution.py:713
  512.6 108.0 %all-gather.15.cloned.1.call-start = ((), (), s32[]{:S(2)}) async-start(), calls=%async_computation.16 | async-start | bytes 13565952 | tf_op jit(solution)/shard_map/all_gather | solution.py:1732
  512.6 11.8 %collective-permute-start.21 = (bf16[2,1,224,512]{3,2,1,0:T(8,128)(2,1)S(1)}, bf16[2,1,224,512]{3,2,1,0:T(8,128)(2,1)S(1)}, u32[]{:S(2)}, u32[]{:S(2)}) collective-permute-start(bf16[2,1,224,512]{3,2,1,0:T(8,128)(2,1)S(1)} %get-tuple-element.157), channel_id=1, source_target_pairs={{0,8},{8,0},{1,9},{9,1},{2,10},{10,2},{3,11},{11,3},{4,12},{12,4},... | collective-permute-start | bytes 1376264 | tf_op jit(solution)/shard_map/ppermute | solution.py:713
  514.2 11.4 %collective-permute-start.22 = (bf16[2,1,224,512]{3,2,1,0:T(8,128)(2,1)S(1)}, bf16[2,1,224,512]{3,2,1,0:T(8,128)(2,1)S(1)}, u32[]{:S(2)}, u32[]{:S(2)}) collective-permute-start(bf16[2,1,224,512]{3,2,1,0:T(8,128)(2,1)S(1)} %get-tuple-element.159), channel_id=1, source_target_pairs={{0,16},{16,0},{1,17},{17,1},{2,18},{18,2},{3,19},{19,3},{4,20},{20... | collective-permute-start | bytes 1376264 | tf_op jit(solution)/shard_map/ppermute | solution.py:713
  526.4 6.1 collective-permute-start.23
  527.8 6.0 collective-permute-start.24
  551.5 24.7 %all-to-all-start.5 = ((bf16[4,512,256]{2,1,0:T(8,128)(2,1)}), bf16[4,512,256]{2,1,0:T(8,128)(2,1)S(1)}, u32[]{:S(2)}, u32[]{:S(2)}) async-start(bf16[4,512,256]{2,1,0:T(8,128)(2,1)} %get-tuple-element.127), calls=%async_computation.5 | async-start | bytes 2097152 | tf_op jit(solution)/shard_map/all_to_all | solution.py:1471
  576.3 16.5 %all-to-all-start.6 = ((bf16[4,288,256]{2,1,0:T(8,128)(2,1)}), bf16[4,288,256]{2,1,0:T(8,128)(2,1)S(1)}, u32[]{:S(2)}, u32[]{:S(2)}) async-start(bf16[4,288,256]{2,1,0:T(8,128)(2,1)} %pad_maximum_fusion.3), calls=%async_computation.7 | async-start | bytes 1179648 | tf_op jit(solution)/shard_map/all_to_all | solution.py:1689
  (77 other events, 620.7 us)
Sparse Core Ops, SparseCore 0:
  13.8 59.5 all-gather.8
  77.4 115.7 all-gather.10
  195.1 74.3 all-gather.12
  332.8 92.3 reduce-scatter.3
  429.6 60.2 reduce-scatter.5
  512.7 28.8 reduce-scatter.7
  551.6 68.8 all-gather.14

commit v5 on v4

--- a/solution.py
+++ b/solution.py
@@ -108,7 +108,7 @@
     scores = mm_nt(query_split, keys) * ((D // HEADS_A) ** -0.5)
     scores = jnp.where(keep, scores, -1e30)
     expo = jnp.exp(scores - jnp.max(scores, axis=-1, keepdims=True))
-    return expo / jnp.sum(expo, axis=-1, keepdims=True)
+    return expo * (1.0 / jnp.sum(expo, axis=-1, keepdims=True))
 
 
 def beside(stacked, heads):
@@ -1588,8 +1588,6 @@
         factors,
         attn_one[0],
     )
-    ffn_sums = tied(jnp.concatenate([first_three, last_three], axis=1), packed)
-    ffn_part = reduce_last(ffn_sums)
     chunk_grads = chunk_backward(
         (
             mixed_grad,
@@ -1606,8 +1604,10 @@
             flat_incoming,
         ),
         attn_one[0],
-        ffn_sums,
-    )
+        own_attn,
+    )
+    ffn_sums = tied(jnp.concatenate([first_three, last_three], axis=1), chunk_grads[6])
+    ffn_part = reduce_last(ffn_sums)
     attn_two = reduce_second(place, attn_one, (chunk_grads[0],))
     skip_gain_grad = chunk_grads[6][0]
     devices = lax.axis_size(SEQ)

time: 652 us -> 645 us (0.989)
    unnamed x180 -> x184, local copies, waits for them, and re-layouts: 26.4 us -> 26.7 us
where the time goes in v5:
time: 645 us; the launch traced here: 636 us
  waiting for transfers between devices  184 us (29%)
  Pallas kernels  145 us (22%)
  blocking collectives  122 us (19%)
  starting transfers between devices  69.2 us (11%)
  local copies, waits for them, and re-layouts  50.4 us (8%)
  other arithmetic  32.1 us (5%)
  between operations  20.5 us (3%)
  matrix products  12.6 us (2%)
    ppermute x15, waiting for transfers between devices, swap(): return lax.ppermute(array, axis, [(0, 1), (1, 0)])  112 us
    all_to_all x1, blocking collectives, shards(): lax.all_to_all(jnp.broadcast_to(last_part[None], (tps,) + last_part.shape...  40.7 us
    pallas_call x1, Pallas kernels, feed_forward_last(): pl.pallas_call(feed_forward_last_kernel, grid=(tps,), in_specs=[scalar_sp...  29.9 us
    unnamed x184, local copies, waits for them, and re-layouts  26.7 us
    pallas_call x1, Pallas kernels, feed_forward_first(): pl.pallas_call(feed_forward_first_kernel, grid=(tps,), in_specs=[scalar_s...  26.7 us
    pallas_call x1, Pallas kernels, attention_backward(): pl.pallas_call(attention_backward_kernel, grid=(tps,), in_specs=[scalar_s...  26.6 us
    psum x1, blocking collectives, shards(): lax.psum(shared + (step_grad.T, step_bias_grad, decay_log_grad, conv_grad...  25.8 us
    all_gather x1, waiting for transfers between devices, shards(): lax.all_gather(jnp.concatenate(attn_parts + ffn_parts[0], axis=0), 'tp')  22.2 us
  transfers between devices with their start and end apart: 38, of which 21 were waited for; matrix products, arithmetic and copies ran while one was open for 8% of the time, Pallas kernels for 17%

profile of v5, /device:TPU:0, one launch (start us, length us, event | category | flops | bytes accessed | tf_op | source)
XLA Modules:
  0.0 635.5 jit_solution(15542864636238201714)
XLA Ops:
  13.8 20.7 %all_gather.34.rows_ref = bf16[256,1024]{1,0:T(8,128)(2,1)S(1)} all-gather(bf16[256,256]{1,0:T(8,128)(2,1)S(1)} %copy-done.54), channel_id=1, replica_groups=mesh['g'=1,'a'=2,'b'=2,'c'=2,'tp'=4] {'tp'}, dimensions={1}, use_global_device_ids=true | all-gather | bytes 655360 | tf_op jit(solution)/shard_map/all_gather | solution.py:1475
  47.8 2.3 fusion.59
  51.2 22.2 %all-gather.9.cloned.1.call-done = bf16[2560,512]{1,0:T(8,128)(2,1)} async-done(((bf16[640,512]{1,0:T(8,128)(2,1)}), bf16[2560,512]{1,0:T(8,128)(2,1)}) %all-gather.9.cloned.1.call-update) | async-done | bytes 2621456 | tf_op jit(solution)/shard_map/all_gather | solution.py:1463
  73.5 3.7 add_convert_fusion.1
  77.3 4.4 all-to-all-start
  83.7 3.4 collective-permute-start.4
  87.1 2.8 collective-permute-start.3
  94.2 2.6 fusion.10
  96.9 5.1 collective-permute-done.2
  112.8 4.8 all-to-all-start.1
  117.6 16.9 %all-to-all-done.1 = bf16[4,64,1152]{2,1,0:T(8,128)(2,1)S(1)} async-done(((bf16[4,64,1152]{2,1,0:T(8,128)(2,1)}), bf16[4,64,1152]{2,1,0:T(8,128)(2,1)S(1)}, u32[]{:S(2)}, u32[]{:S(2)}) %all-to-all-start.1) | async-done | bytes 589856 | tf_op jit(solution)/shard_map/all_to_all | solution.py:1506
  136.2 40.7 %all_to_all.35 = bf16[4,384,512]{2,1,0:T(8,128)(2,1)} all-to-all(bf16[4,384,512]{2,1,0:T(8,128)(2,1)S(1)} %broadcast_in_dim.74), channel_id=1, replica_groups=mesh['g'=1,'a'=2,'b'=2,'c'=2,'tp'=4] {'tp'}, dimensions={0} | all-to-all | bytes 3145728 | tf_op jit(solution)/shard_map/all_to_all | solution.py:1510
  177.1 4.4 all-to-all-start.2
  181.5 11.2 %reduce-scatter.4.cloned.1.call-start = ((), (), s32[]{:S(2)}) async-start(), calls=%async_computation.10 | async-start | bytes 14155776 | tf_op jit(solution)/shard_map/reduce_scatter | solution.py:1573
  201.2 15.2 %attention_forward.1 = (f32[512,1024]{1,0:T(8,128)}, bf16[512,1024]{1,0:T(8,128)(2,1)}, bf16[512,1024]{1,0:T(8,128)(2,1)}, bf16[4,3,512,256]{3,2,1,0:T(8,128)(2,1)}, bf16[4,512,256]{2,1,0:T(8,128)(2,1)}) custom-call(bf16[4,512,256]{2,1,0:T(8,128)(2,1)} %all-to-all-done.embed_ref, f32[64,1,1024]{2,1,0:T(1,128)} %copy.175.global_ref, f32[1,1024]{1,0:T(1,128)} %bitcast.162, ...), custom_call_target="tpu_custom_call" | custom-call | flops 4294967296 | bytes 14680064 | tf_op jit(solution)/shard_map/attention_forward/pallas_call | solution.py:162
  216.4 26.7 %feed_forward_first.1 = (bf16[512,1024]{1,0:T(8,128)(2,1)}, bf16[1024,512]{1,0:T(8,128)(2,1)}, bf16[512,1024]{1,0:T(8,128)(2,1)}, f32[512,1024]{1,0:T(8,128)}, f...) custom-call(s32[1]{0:T(128)} %bitcast.core_ref, ...), custom_call_target="tpu_custom_call" | custom-call | flops 19327352832 | bytes 33554432 | tf_op jit(solution)/shard_map/feed_forward_first/pallas_call | solution.py:363
  243.2 11.4 %collective-permute-done.5.refs_1_.refs_3_.refs_5_.refs_7_ = bf16[2,2,4,384,512]{4,3,2,1,0:T(8,128)(2,1)S(1)} collective-permute-done((bf16[2,2,4,384,512]{4,3,2,1,0:T(8,128)(2,1)}, bf16[2,2,4,384,512]{4,3,2,1,0:T(8,128)(2,1)S(1)}, u32[]{:S(2)}, u32[]{:S(2)}) %collective-permute-start.5) | collective-permute-done | bytes 6291488 | tf_op jit(solution)/shard_map/ppermute | solution.py:713
  254.6 2.8 copy-done.3
  257.3 2.3 first_sum.3
  259.8 38.8 %collective-permute-done.6.refs_1_.refs_3_ = bf16[2,4,192,512]{3,2,1,0:T(8,128)(2,1)S(1)} collective-permute-done((bf16[2,4,192,512]{3,2,1,0:T(8,128)(2,1)S(1)}, bf16[2,4,192,512]{3,2,1,0:T(8,128)(2,1)S(1)}, u32[]{:S(2)}, u32[]{:S(2)}) %collective-permute-start.6) | collective-permute-done | bytes 1572896 | tf_op jit(solution)/shard_map/ppermute | solution.py:713
  302.7 29.9 %feed_forward_last.1 = (bf16[4,512,256]{2,1,0:T(8,128)(2,1)}, f32[512,1024]{1,0:T(8,128)}, f32[1,1024]{1,0:T(1,128)}, bf16[8,4,384,512]{3,2,1,0:T(8,128)(2,1)}) custom-call(s32[1]{0:T(128)} %bitcast.core_ref, f32[512,1024]{1,0:T(8,128)} %get-tuple-element.104.hidden_ref, bf16[512,1024]{1,0:T(8,128)(2,1)} %get-tuple-element.105.cot_ref, f32[1,1024]{1,0:T(1,128)} %bitcast.174, ...), custom_call_target="tpu_custom_call" | custom-call | flops 19327352832 | bytes 33554432 | tf_op jit(solution)/shard_map/feed_forward_last/pallas_call | solution.py:404
  332.7 4.7 all-to-all-start.4
  339.5 17.2 %collective-permute-done.9.four_ref = bf16[4,192,512]{2,1,0:T(8,128)(2,1)S(1)} collective-permute-done((bf16[4,192,512]{2,1,0:T(8,128)(2,1)}, bf16[4,192,512]{2,1,0:T(8,128)(2,1)S(1)}, u32[]{:S(2)}, u32[]{:S(2)}) %collective-permute-start.9) | collective-permute-done | bytes 786464 | tf_op jit(solution)/shard_map/ppermute | solution.py:713
  363.3 26.6 %attention_backward.1 = (bf16[4,512,256]{2,1,0:T(8,128)(2,1)}, f32[64,1024]{1,0:T(8,128)}, bf16[64,1152]{1,0:T(8,128)(2,1)}, f32[1,1024]{1,0:T(1,128)}, bf16[2,2...) custom-call(s32[1]{0:T(128)} %bitcast.core_ref, f32[512,1024]{1,0:T(8,128)} %copy-done.9, ...), custom_call_target="tpu_custom_call" | custom-call | flops 8589934592 | bytes 27262976 | tf_op jit(solution)/shard_map/attention_backward/pallas_call | solution.py:556
  391.6 17.9 %all_gather.41.returned_ref = bf16[256,1152]{1,0:T(8,128)(2,1)} all-gather(bf16[64,1152]{1,0:T(8,128)(2,1)} %get-tuple-element.128), channel_id=1, replica_groups=mesh['g'=1,'a'=2,'b'=2,'c'=2,'tp'=4] {'tp'}, dimensions={0}, use_global_device_ids=true | all-gather | bytes 737280 | tf_op jit(solution)/shard_map/all_gather | solution.py:1578
  409.5 2.2 copy-done.2
  414.3 4.2 gate_backward.1
  418.5 8.4 %chunk_backward.1 = (f32[256,512]{1,0:T(8,128)}, f32[256,128]{1,0:T(8,128)}, f32[256,128]{1,0:T(8,128)}, f32[256,8]{1,0:T(8,128)}, f32[8,256]{1,0:T(8,128)}, /*index=5*/f32[8,256]{1,0:T(8,128)}, f32[1,8]{1,0:T(1,128)}) custom-call(f32[256,512]{1,0:T(8,128)} %get-tuple-element.134.grad_ref, f32[256,512]{1,0:T(8,128)} %copy-done.26, ...), custom_call_target="tpu_custom_call" | custom-call | flops 805306368 | bytes 4194304 | tf_op jit(solution)/shard_map/chunk_backward/pallas_call | solution.py:1128
  427.7 4.2 add_convert_fusion
  438.5 18.9 %collective-permute-done.16.refs_5_.refs_7_ = bf16[2,4,128,512]{3,2,1,0:T(8,128)(2,1)S(1)} collective-permute-done((bf16[2,4,128,512]{3,2,1,0:T(8,128)(2,1)}, bf16[2,4,128,512]{3,2,1,0:T(8,128)(2,1)S(1)}, u32[]{:S(2)}, u32[]{:S(2)}) %collective-permute-start.16) | collective-permute-done | bytes 1048608 | tf_op jit(solution)/shard_map/ppermute | solution.py:713
  463.0 6.6 %front_backward.1 = (f32[256,768]{1,0:T(8,128)}, f32[8,768]{1,0:T(8,128)}, f32[4,768]{1,0:T(4,128)}, bf16[8,256]{1,0:T(8,128)(2,1)}, f32[8,1]{1,0:T(8,128)}, /*index=5*/f32[8,1]{1,0:T(8,128)}) custom-call(bf16[528,128]{1,0:T(8,128)(2,1)} %copy-done.53, bf16[528,128]{1,0:T(8,128)(2,1)} %copy-done.52, bf16[528,128]{1,0:T(8,128)(2,1)} %copy-done.51, ...), custom_call_target="tpu_custom_call" | custom-call | flops 603979776 | bytes 8388608 | tf_op jit(solution)/shard_map/front_backward/pallas_call | solution.py:1266
  472.9 2.7 collective-permute-done.17
  477.7 4.6 mixer_weight_grads.1
  482.3 2.9 collective-permute-start.20
  492.9 6.1 collective-permute-done.18.two_ref
  506.7 9.1 %collective-permute-done.21.refs_1_.refs_3_ = bf16[2,1,224,512]{3,2,1,0:T(8,128)(2,1)S(1)} collective-permute-done((bf16[2,1,224,512]{3,2,1,0:T(8,128)(2,1)S(1)}, bf16[2,1,224,512]{3,2,1,0:T(8,128)(2,1)S(1)}, u32[]{:S(2)}, u32[]{:S(2)}) %collective-permute-start.21) | collective-permute-done | bytes 458784 | tf_op jit(solution)/shard_map/ppermute | solution.py:713
  519.2 4.1 collective-permute-done.23.two_ref
  524.7 16.8 %all_gather.42 = bf16[4,64,512]{2,1,0:T(8,128)(2,1)S(1)} all-gather(bf16[1,64,512]{2,1,0:T(8,128)(2,1)S(1)} %slice.234), channel_id=1, replica_groups=mesh['g'=1,'a'=2,'b'=2,'c'=2,'tp'=4] {'tp'}, dimensions={0}, use_global_device_ids=true | all-gather | bytes 327680 | tf_op jit(solution)/shard_map/all_gather | solution.py:1657
  541.7 2.2 pad_maximum_fusion
  543.9 3.5 all-to-all-start.5
  549.4 5.1 project_backward.1
  557.8 11.4 %all-to-all-done.5 = bf16[4,512,256]{2,1,0:T(8,128)(2,1)S(1)} async-done(((bf16[4,512,256]{2,1,0:T(8,128)(2,1)}), bf16[4,512,256]{2,1,0:T(8,128)(2,1)S(1)}, u32[]{:S(2)}, u32[]{:S(2)}) %all-to-all-start.5) | async-done | bytes 1048608 | tf_op jit(solution)/shard_map/all_to_all | solution.py:1471
  569.2 3.5 all-to-all-start.6
  574.5 11.9 %all-to-all-done.6 = bf16[4,288,256]{2,1,0:T(8,128)(2,1)S(1)} async-done(((bf16[4,288,256]{2,1,0:T(8,128)(2,1)}), bf16[4,288,256]{2,1,0:T(8,128)(2,1)S(1)}, u32[]{:S(2)}, u32[]{:S(2)}) %all-to-all-start.6) | async-done | bytes 589856 | tf_op jit(solution)/shard_map/all_to_all | solution.py:1689
  587.3 25.8 %all-reduce.1 = (f32[1024]{0:T(1024)}, f32[1024,8]{0,1:T(8,128)}, f32[8]{0:T(128)}, f32[8]{0:T(128)}, f32[4,512]{1,0:T(4,128)}, /*index=5*/f32[4,256]{1,0:T(4,12...) all-reduce(f32[1024]{0:T(1024)S(1)} %bitcast.160, ...), channel_id=1, replica_groups=mesh['g'=1,'a'=2,'b'=2,'c'=2,'tp'=4] {'g','a','b','c'}, use_global_device_ids=true, to_apply=%region_9.10 | all-reduce | flops 14872 | bytes 118976 | tf_op jit(solution)/shard_map/psum | solution.py:1719
  613.6 4.4 copy-done.5
  618.1 8.2 %unpack.1 = (f32[2,1024,1024]{2,1,0:T(8,128)}, f32[2,8,64,1024]{3,2,1,0:T(8,128)}, f32[3,1024,256]{2,1,0:T(8,128)}, f32[256,1024]{1,0:T(8,128)}, f32[1024,512]{1...) custom-call(bf16[8,1472,512]{2,1,0:T(8,128)(2,1)S(1)} %bitcast.114), custom_call_target="tpu_custom_call" | custom-call | flops 6029312 | bytes 36175872 | tf_op jit(solution)/shard_map/unpack/pallas_call | solution.py:921
  626.2 2.3 copy.197
  (378 shorter events, 107.2 us)
Async XLA Ops:
  7.2 66.3 %all-gather.9.cloned.1.call-start = ((), (), s32[]{:S(2)}) async-start(), calls=%async_computation.13 | async-start | bytes 3276800 | tf_op jit(solution)/shard_map/all_gather | solution.py:1463
  10.1 24.6 %copy-start.66 = (f32[1024]{0:T(1024)S(1)}, f32[1024]{0:T(1024)}, u32[]{:S(2)}) copy-start(f32[1024]{0:T(1024)} %param.25) | copy-start | bytes 12292
  13.7 187.5 %all-gather.11.cloned.1.call-start = ((), (), s32[]{:S(2)}) async-start(), calls=%async_computation.14 | async-start | bytes 23592960 | tf_op jit(solution)/shard_map/all_gather | solution.py:1493
  34.5 164.9 %copy-start.27 = (bf16[256,1024]{1,0:T(8,128)(2,1)}, bf16[256,1024]{1,0:T(8,128)(2,1)S(1)}, u32[]{:S(2)}) copy-start(bf16[256,1024]{1,0:T(8,128)(2,1)S(1)} %all_gather.34.rows_ref) | copy-start | bytes 1572868
  34.9 70.9 %copy-start.25 = (bf16[256,1024]{1,0:T(8,128)(2,1)}, bf16[256,1024]{1,0:T(8,128)(2,1)S(1)}, u32[]{:S(2)}) copy-start(bf16[256,1024]{1,0:T(8,128)(2,1)S(1)} %fusion.15.normed_ref) | copy-start | bytes 1572868
  37.0 8.9 %collective-permute-start = (f32[3,768]{1,0:T(4,128)S(1)}, f32[3,768]{1,0:T(4,128)S(1)}, u32[]{:S(2)}, u32[]{:S(2)}) collective-permute-start(f32[3,768]{1,0:T(4,128)S(1)} %fusion.46), channel_id=1, source_target_pairs={{0,4},{4,8},{8,12},{12,16},{16,20},{20,24},{24,28},{1,5},{5,9},{9,... | collective-permute-start | bytes 27656 | tf_op jit(solution)/shard_map/ppermute | solution.py:606
  39.1 155.1 %copy-start.58 = (s32[256]{0:T(256)}, s32[256]{0:T(256)S(1)}, u32[]{:S(2)}) copy-start(s32[256]{0:T(256)S(1)} %select_reduce_fusion) | copy-start | bytes 3076
  42.0 52.3 %copy-start.55 = (f32[8,256]{1,0:T(8,128)}, f32[8,256]{1,0:T(8,128)S(1)}, u32[]{:S(2)}) copy-start(f32[8,256]{1,0:T(8,128)S(1)} %get-tuple-element.212.refs_4_.steps_row_ref.refs_9_) | copy-start | bytes 24580
  46.6 56.5 %copy-start.28 = (f32[256,768]{1,0:T(8,128)}, f32[256,768]{1,0:T(8,128)S(1)}, u32[]{:S(2)}) copy-start(f32[256,768]{1,0:T(8,128)S(1)} %divide_multiply_fusion) | copy-start | bytes 2359300
  46.6 30.6 %copy-start.26 = (f32[256,512]{1,0:T(8,128)}, f32[256,512]{1,0:T(8,128)S(1)}, u32[]{:S(2)}) copy-start(f32[256,512]{1,0:T(8,128)S(1)} %slice.260.refs_11_.inner_ref.refs_5_) | copy-start | bytes 1572868
  77.3 30.7 %all-to-all-start = ((bf16[4,512,256]{2,1,0:T(8,128)(2,1)}), bf16[4,512,256]{2,1,0:T(8,128)(2,1)}, u32[]{:S(2)}, u32[]{:S(2)}) async-start(bf16[4,512,256]{2,1,0:T(8,128)(2,1)} %bitcast.135), calls=%async_computation | async-start | bytes 2097152 | tf_op jit(solution)/shard_map/all_to_all | solution.py:1468
  83.7 19.4 %collective-permute-start.4 = (bf16[528,128]{1,0:T(8,128)(2,1)S(1)}, bf16[528,128]{1,0:T(8,128)(2,1)S(1)}, u32[]{:S(2)}, u32[]{:S(2)}) collective-permute-start(bf16[528,128]{1,0:T(8,128)(2,1)S(1)} %pad_maximum_fusion.4), channel_id=1, source_target_pairs={{0,16},{4,20},{8,24},{12,28},{1,17},{5,21},{9,25},{13,29},{2,18},{... | collective-permute-start | bytes 405512 | tf_op jit(solution)/shard_map/ppermute | solution.py:700
  87.1 15.0 %collective-permute-start.3 = (bf16[528,128]{1,0:T(8,128)(2,1)S(1)}, bf16[528,128]{1,0:T(8,128)(2,1)S(1)}, u32[]{:S(2)}, u32[]{:S(2)}) collective-permute-start(bf16[528,128]{1,0:T(8,128)(2,1)S(1)} %pad_maximum_fusion.4), channel_id=1, source_target_pairs={{0,12},{4,16},{8,20},{12,24},{16,28},{1,13},{5,17},{9,21},{13,25},... | collective-permute-start | bytes 405512 | tf_op jit(solution)/shard_map/ppermute | solution.py:700
  89.8 12.2 %collective-permute-start.2 = (bf16[528,128]{1,0:T(8,128)(2,1)S(1)}, bf16[528,128]{1,0:T(8,128)(2,1)S(1)}, u32[]{:S(2)}, u32[]{:S(2)}) collective-permute-start(bf16[528,128]{1,0:T(8,128)(2,1)S(1)} %pad_maximum_fusion.4), channel_id=1, source_target_pairs={{0,8},{4,12},{8,16},{12,20},{16,24},{20,28},{1,9},{5,13},{9,17},{1... | collective-permute-start | bytes 405512 | tf_op jit(solution)/shard_map/ppermute | solution.py:700
  91.8 5.1 collective-permute-start.1
  112.8 21.8 %all-to-all-start.1 = ((bf16[4,64,1152]{2,1,0:T(8,128)(2,1)}), bf16[4,64,1152]{2,1,0:T(8,128)(2,1)S(1)}, u32[]{:S(2)}, u32[]{:S(2)}) async-start(bf16[4,64,1152]{2,1,0:T(8,128)(2,1)} %bitcast.23), calls=%async_computation.1 | async-start | bytes 1179648 | tf_op jit(solution)/shard_map/all_to_all | solution.py:1506
  117.5 185.2 %all-gather.13.cloned.1.call-start = ((), (), s32[]{:S(2)}) async-start(), calls=%async_computation.15 | async-start | bytes 14155776 | tf_op jit(solution)/shard_map/all_gather | solution.py:1513
  134.8 42.1 %copy-start.60 = (f32[64,1]{1,0:T(8,128)}, f32[64,1]{1,0:T(8,128)S(1)}, u32[]{:S(2)}) copy-start(f32[64,1]{1,0:T(8,128)S(1)} %get-tuple-element.204.squares_ref) | copy-start | bytes 772
  177.1 39.3 %all-to-all-start.2 = ((bf16[4,512,256]{2,1,0:T(8,128)(2,1)}), bf16[4,512,256]{2,1,0:T(8,128)(2,1)}, u32[]{:S(2)}, u32[]{:S(2)}) async-start(bf16[4,512,256]{2,1,0:T(8,128)(2,1)} %bitcast.136), calls=%async_computation.2 | async-start | bytes 2097152 | tf_op jit(solution)/shard_map/all_to_all | solution.py:1468
  181.5 246.2 %reduce-scatter.4.cloned.1.call-start = ((), (), s32[]{:S(2)}) async-start(), calls=%async_computation.10 | async-start | bytes 14155776 | tf_op jit(solution)/shard_map/reduce_scatter | solution.py:1573
  243.1 11.5 %collective-permute-start.5 = (bf16[2,2,4,384,512]{4,3,2,1,0:T(8,128)(2,1)}, bf16[2,2,4,384,512]{4,3,2,1,0:T(8,128)(2,1)S(1)}, u32[]{:S(2)}, u32[]{:S(2)}) collective-permute-start(bf16[2,2,4,384,512]{4,3,2,1,0:T(8,128)(2,1)} %get-tuple-element.111), channel_id=1, source_target_pairs={{0,4},{4,0},{1,5},{5,1},{2,6},{6,2},{3,7},{7,3},{8,12},{12,8},{9,1... | collective-permute-start | bytes 18874376 | tf_op jit(solution)/shard_map/ppermute | solution.py:713
  259.7 39.0 %collective-permute-start.6 = (bf16[2,4,192,512]{3,2,1,0:T(8,128)(2,1)S(1)}, bf16[2,4,192,512]{3,2,1,0:T(8,128)(2,1)S(1)}, u32[]{:S(2)}, u32[]{:S(2)}) collective-permute-start(bf16[2,4,192,512]{3,2,1,0:T(8,128)(2,1)S(1)} %get-tuple-element.113), channel_id=1, source_target_pairs={{0,8},{8,0},{1,9},{9,1},{2,10},{10,2},{3,11},{11,3},{4,12},{12,4},... | collective-permute-start | bytes 4718600 | tf_op jit(solution)/shard_map/ppermute | solution.py:713
  259.8 38.9 %collective-permute-start.7 = (bf16[2,4,192,512]{3,2,1,0:T(8,128)(2,1)S(1)}, bf16[2,4,192,512]{3,2,1,0:T(8,128)(2,1)S(1)}, u32[]{:S(2)}, u32[]{:S(2)}) collective-permute-start(bf16[2,4,192,512]{3,2,1,0:T(8,128)(2,1)S(1)} %get-tuple-element.115), channel_id=1, source_target_pairs={{0,16},{16,0},{1,17},{17,1},{2,18},{18,2},{3,19},{19,3},{4,20},{20... | collective-permute-start | bytes 4718600 | tf_op jit(solution)/shard_map/ppermute | solution.py:713
  332.7 25.1 %copy-start.8 = (f32[512,1024]{1,0:T(8,128)S(1)}, f32[512,1024]{1,0:T(8,128)}, u32[]{:S(2)}) copy-start(f32[512,1024]{1,0:T(8,128)} %get-tuple-element.121.refs_0_) | copy-start | bytes 6291460
  332.7 30.6 %all-to-all-start.4 = ((bf16[4,512,256]{2,1,0:T(8,128)(2,1)}), bf16[4,512,256]{2,1,0:T(8,128)(2,1)}, u32[]{:S(2)}, u32[]{:S(2)}) async-start(bf16[4,512,256]{2,1,0:T(8,128)(2,1)} %get-tuple-element.117), calls=%async_computation.4 | async-start | bytes 2097152 | tf_op jit(solution)/shard_map/all_to_all | solution.py:1471
  337.4 163.2 %reduce-scatter.6.cloned.1.call-start = ((), (), s32[]{:S(2)}) async-start(), calls=%async_computation.11 | async-start | bytes 3932160 | tf_op jit(solution)/shard_map/reduce_scatter | solution.py:846
  337.5 19.3 %collective-permute-start.9 = (bf16[4,192,512]{2,1,0:T(8,128)(2,1)}, bf16[4,192,512]{2,1,0:T(8,128)(2,1)S(1)}, u32[]{:S(2)}, u32[]{:S(2)}) collective-permute-start(bf16[4,192,512]{2,1,0:T(8,128)(2,1)} %copy-done.20), channel_id=1, source_target_pairs={{0,8},{8,0},{1,9},{9,1},{2,10},{10,2},{3,11},{11,3},{4,12},{12,4},... | collective-permute-start | bytes 2359304 | tf_op jit(solution)/shard_map/ppermute | solution.py:713
  338.9 18.9 %collective-permute-start.8 = (bf16[4,192,512]{2,1,0:T(8,128)(2,1)}, bf16[4,192,512]{2,1,0:T(8,128)(2,1)S(1)}, u32[]{:S(2)}, u32[]{:S(2)}) collective-permute-start(bf16[4,192,512]{2,1,0:T(8,128)(2,1)} %copy-done.19), channel_id=1, source_target_pairs={{0,16},{16,0},{1,17},{17,1},{2,18},{18,2},{3,19},{19,3},{4,20},{20... | collective-permute-start | bytes 2359304 | tf_op jit(solution)/shard_map/ppermute | solution.py:713
  389.9 19.6 %collective-permute-start.10 = (bf16[2,2,4,256,512]{4,3,2,1,0:T(8,128)(2,1)}, bf16[2,2,4,256,512]{4,3,2,1,0:T(8,128)(2,1)S(1)}, u32[]{:S(2)}, u32[]{:S(2)}) collective-permute-start(bf16[2,2,4,256,512]{4,3,2,1,0:T(8,128)(2,1)} %get-tuple-element.130), channel_id=1, source_target_pairs={{0,4},{4,0},{1,5},{5,1},{2,6},{6,2},{3,7},{7,3},{8,12},{12,8},{9,1... | collective-permute-start | bytes 12582920 | tf_op jit(solution)/shard_map/ppermute | solution.py:713
  431.9 109.8 %reduce-scatter.8.cloned.1.call-start = ((), (), s32[]{:S(2)}) async-start(), calls=%async_computation.12 | async-start | bytes 1310720 | tf_op jit(solution)/shard_map/reduce_scatter | solution.py:846
  431.9 25.5 %collective-permute-start.16 = (bf16[2,4,128,512]{3,2,1,0:T(8,128)(2,1)}, bf16[2,4,128,512]{3,2,1,0:T(8,128)(2,1)S(1)}, u32[]{:S(2)}, u32[]{:S(2)}) collective-permute-start(bf16[2,4,128,512]{3,2,1,0:T(8,128)(2,1)} %copy-done.18), channel_id=1, source_target_pairs={{0,16},{16,0},{1,17},{17,1},{2,18},{18,2},{3,19},{19,3},{4,20},{20... | collective-permute-start | bytes 3145736 | tf_op jit(solution)/shard_map/ppermute | solution.py:713
  433.1 26.1 %collective-permute-start.15 = (bf16[2,4,128,512]{3,2,1,0:T(8,128)(2,1)S(1)}, bf16[2,4,128,512]{3,2,1,0:T(8,128)(2,1)S(1)}, u32[]{:S(2)}, u32[]{:S(2)}) collective-permute-start(bf16[2,4,128,512]{3,2,1,0:T(8,128)(2,1)S(1)} %copy-done.7), channel_id=1, source_target_pairs={{0,8},{8,0},{1,9},{9,1},{2,10},{10,2},{3,11},{11,3},{4,12},{12,4},... | collective-permute-start | bytes 3145736 | tf_op jit(solution)/shard_map/ppermute | solution.py:713
  434.5 27.7 %collective-permute-start.14 = (bf16[528,128]{1,0:T(8,128)(2,1)}, bf16[528,128]{1,0:T(8,128)(2,1)S(1)}, u32[]{:S(2)}, u32[]{:S(2)}) collective-permute-start(bf16[528,128]{1,0:T(8,128)(2,1)} %get-tuple-element.133), channel_id=1, source_target_pairs={{16,0},{20,4},{24,8},{28,12},{17,1},{21,5},{25,9},{29,13},{18,2},{... | collective-permute-start | bytes 405512 | tf_op jit(solution)/shard_map/ppermute | solution.py:1615
  435.8 26.4 %collective-permute-start.13 = (bf16[528,128]{1,0:T(8,128)(2,1)}, bf16[528,128]{1,0:T(8,128)(2,1)S(1)}, u32[]{:S(2)}, u32[]{:S(2)}) collective-permute-start(bf16[528,128]{1,0:T(8,128)(2,1)} %get-tuple-element.133), channel_id=1, source_target_pairs={{12,0},{16,4},{20,8},{24,12},{28,16},{13,1},{17,5},{21,9},{25,13},... | collective-permute-start | bytes 405512 | tf_op jit(solution)/shard_map/ppermute | solution.py:1615
  437.1 25.1 %collective-permute-start.12 = (bf16[528,128]{1,0:T(8,128)(2,1)}, bf16[528,128]{1,0:T(8,128)(2,1)S(1)}, u32[]{:S(2)}, u32[]{:S(2)}) collective-permute-start(bf16[528,128]{1,0:T(8,128)(2,1)} %get-tuple-element.133), channel_id=1, source_target_pairs={{8,0},{12,4},{16,8},{20,12},{24,16},{28,20},{9,1},{13,5},{17,9},{2... | collective-permute-start | bytes 405512 | tf_op jit(solution)/shard_map/ppermute | solution.py:1615
  457.4 4.8 collective-permute-start.11
  469.5 6.1 collective-permute-start.17
  482.3 6.5 %collective-permute-start.20 = (bf16[2,2,1,448,512]{4,3,2,1,0:T(8,128)(2,1)}, bf16[2,2,1,448,512]{4,3,2,1,0:T(8,128)(2,1)S(1)}, u32[]{:S(2)}, u32[]{:S(2)}) collective-permute-start(bf16[2,2,1,448,512]{4,3,2,1,0:T(8,128)(2,1)} %get-tuple-element.152), channel_id=1, source_target_pairs={{0,4},{4,0},{1,5},{5,1},{2,6},{6,2},{3,7},{7,3},{8,12},{12,8},{9,1... | collective-permute-start | bytes 5505032 | tf_op jit(solution)/shard_map/ppermute | solution.py:713
  485.2 13.8 %collective-permute-start.18 = (bf16[4,128,512]{2,1,0:T(8,128)(2,1)S(1)}, bf16[4,128,512]{2,1,0:T(8,128)(2,1)S(1)}, u32[]{:S(2)}, u32[]{:S(2)}) collective-permute-start(bf16[4,128,512]{2,1,0:T(8,128)(2,1)S(1)} %get-tuple-element.147), channel_id=1, source_target_pairs={{0,16},{16,0},{1,17},{17,1},{2,18},{18,2},{3,19},{19,3},{4,20},{20... | collective-permute-start | bytes 1572872 | tf_op jit(solution)/shard_map/ppermute | solution.py:713
  486.3 14.1 %collective-permute-start.19 = (bf16[4,128,512]{2,1,0:T(8,128)(2,1)S(1)}, bf16[4,128,512]{2,1,0:T(8,128)(2,1)S(1)}, u32[]{:S(2)}, u32[]{:S(2)}) collective-permute-start(bf16[4,128,512]{2,1,0:T(8,128)(2,1)S(1)} %get-tuple-element.149), channel_id=1, source_target_pairs={{0,8},{8,0},{1,9},{9,1},{2,10},{10,2},{3,11},{11,3},{4,12},{12,4},... | collective-permute-start | bytes 1572872 | tf_op jit(solution)/shard_map/ppermute | solution.py:713
  503.8 109.8 %all-gather.15.cloned.1.call-start = ((), (), s32[]{:S(2)}) async-start(), calls=%async_computation.16 | async-start | bytes 13565952 | tf_op jit(solution)/shard_map/all_gather | solution.py:1732
  503.9 11.9 %collective-permute-start.21 = (bf16[2,1,224,512]{3,2,1,0:T(8,128)(2,1)S(1)}, bf16[2,1,224,512]{3,2,1,0:T(8,128)(2,1)S(1)}, u32[]{:S(2)}, u32[]{:S(2)}) collective-permute-start(bf16[2,1,224,512]{3,2,1,0:T(8,128)(2,1)S(1)} %copy-done.24), channel_id=1, source_target_pairs={{0,8},{8,0},{1,9},{9,1},{2,10},{10,2},{3,11},{11,3},{4,12},{12,4},... | collective-permute-start | bytes 1376264 | tf_op jit(solution)/shard_map/ppermute | solution.py:713
  505.0 11.4 %collective-permute-start.22 = (bf16[2,1,224,512]{3,2,1,0:T(8,128)(2,1)S(1)}, bf16[2,1,224,512]{3,2,1,0:T(8,128)(2,1)S(1)}, u32[]{:S(2)}, u32[]{:S(2)}) collective-permute-start(bf16[2,1,224,512]{3,2,1,0:T(8,128)(2,1)S(1)} %copy-done.22), channel_id=1, source_target_pairs={{0,16},{16,0},{1,17},{17,1},{2,18},{18,2},{3,19},{19,3},{4,20},{20... | collective-permute-start | bytes 1376264 | tf_op jit(solution)/shard_map/ppermute | solution.py:713
  517.2 24.5 %copy-start.42 = (bf16[1,768,512]{2,1,0:T(8,128)(2,1)S(1)}, bf16[1,768,512]{2,1,0:T(8,128)(2,1)}, u32[]{:S(2)}) copy-start(bf16[1,768,512]{2,1,0:T(8,128)(2,1)} %reduce-scatter.6.cloned.1.call-done) | copy-start | bytes 2359300
  517.2 6.1 collective-permute-start.23
  518.6 6.0 collective-permute-start.24
  543.9 25.3 %all-to-all-start.5 = ((bf16[4,512,256]{2,1,0:T(8,128)(2,1)}), bf16[4,512,256]{2,1,0:T(8,128)(2,1)S(1)}, u32[]{:S(2)}, u32[]{:S(2)}) async-start(bf16[4,512,256]{2,1,0:T(8,128)(2,1)} %get-tuple-element.127), calls=%async_computation.5 | async-start | bytes 2097152 | tf_op jit(solution)/shard_map/all_to_all | solution.py:1471
  569.2 17.3 %all-to-all-start.6 = ((bf16[4,288,256]{2,1,0:T(8,128)(2,1)}), bf16[4,288,256]{2,1,0:T(8,128)(2,1)S(1)}, u32[]{:S(2)}, u32[]{:S(2)}) async-start(bf16[4,288,256]{2,1,0:T(8,128)(2,1)} %pad_maximum_fusion.3), calls=%async_computation.6 | async-start | bytes 1179648 | tf_op jit(solution)/shard_map/all_to_all | solution.py:1689
  (79 other events, 616.1 us)
Sparse Core Ops, SparseCore 0:
  13.8 59.5 all-gather.8
  77.4 115.7 all-gather.10
  195.1 74.4 all-gather.12
  332.8 92.3 reduce-scatter.3
  432.0 59.6 reduce-scatter.5
  503.9 31.1 reduce-scatter.7
  544.0 69.5 all-gather.14

commit v6 on v5

--- a/solution.py
+++ b/solution.py
@@ -705,8 +705,15 @@
 
 
 def tied(array, *tokens):
-    zero = sum(t[(0,) * t.ndim].astype(F32) * 0.0 for t in tokens)
-    return (array.astype(F32) + zero).astype(array.dtype)
+    return pl.pallas_call(
+        lambda *refs: None,
+        in_specs=[anywhere()] * (1 + len(tokens)),
+        out_specs=anywhere(),
+        out_shape=jax.ShapeDtypeStruct(array.shape, array.dtype),
+        input_output_aliases={0: 0},
+        name="tied",
+        cost_estimate=pl.CostEstimate(flops=0, bytes_accessed=0, transcendentals=0),
+    )(array, *tokens)
 
 
 def swap(array, axis):

time: 645 us -> 638 us (0.989)
    convert_element_type x4 -> x0, other arithmetic: 9.15 us -> none  [tied(): return (array.astype(F32) + zero).astype(array.dtype)]
    unnamed x184 -> x176, local copies, waits for them, and re-layouts: 26.7 us -> 26 us
  transfers between devices with their start and end apart: 38 -> 38, of which waited for: 21 -> 22; matrix products, arithmetic and copies ran while one was open for 8% -> 8% of each run, Pallas kernels for 17% -> 17%
where the time goes in v6:
time: 638 us; the launch traced here: 629 us
  waiting for transfers between devices  185 us (29%)
  Pallas kernels  145 us (23%)
  blocking collectives  123 us (19%)
  starting transfers between devices  69.1 us (11%)
  local copies, waits for them, and re-layouts  48.4 us (8%)
  other arithmetic  28 us (4%)
  between operations  17.8 us (3%)
  matrix products  12.7 us (2%)
    ppermute x15, waiting for transfers between devices, swap(): return lax.ppermute(array, axis, [(0, 1), (1, 0)])  113 us
    all_to_all x1, blocking collectives, shards(): lax.all_to_all(jnp.broadcast_to(last_part[None], (tps,) + last_part.shape...  40.7 us
    pallas_call x1, Pallas kernels, feed_forward_last(): pl.pallas_call(feed_forward_last_kernel, grid=(tps,), in_specs=[scalar_sp...  29.9 us
    pallas_call x1, Pallas kernels, feed_forward_first(): pl.pallas_call(feed_forward_first_kernel, grid=(tps,), in_specs=[scalar_s...  26.6 us
    pallas_call x1, Pallas kernels, attention_backward(): pl.pallas_call(attention_backward_kernel, grid=(tps,), in_specs=[scalar_s...  26.6 us
    psum x1, blocking collectives, shards(): lax.psum(shared + (step_grad.T, step_bias_grad, decay_log_grad, conv_grad...  26.1 us
    unnamed x176, local copies, waits for them, and re-layouts  26 us
    all_gather x1, waiting for transfers between devices, shards(): lax.all_gather(jnp.concatenate(attn_parts + ffn_parts[0], axis=0), 'tp')  23.4 us
  transfers between devices with their start and end apart: 38, of which 22 were waited for; matrix products, arithmetic and copies ran while one was open for 8% of the time, Pallas kernels for 17%

profile of v6, /device:TPU:0, one launch (start us, length us, event | category | flops | bytes accessed | tf_op | source)
XLA Modules:
  0.0 629.0 jit_solution(10575269061634137343)
XLA Ops:
  13.8 20.7 %all_gather.34.rows_ref = bf16[256,1024]{1,0:T(8,128)(2,1)S(1)} all-gather(bf16[256,256]{1,0:T(8,128)(2,1)S(1)} %copy-done.51), channel_id=1, replica_groups=mesh['g'=1,'a'=2,'b'=2,'c'=2,'tp'=4] {'tp'}, dimensions={1}, use_global_device_ids=true | all-gather | bytes 655360 | tf_op jit(solution)/shard_map/all_gather | solution.py:1482
  47.7 2.4 fusion.59
  50.1 23.4 %all-gather.9.cloned.1.call-done = bf16[2560,512]{1,0:T(8,128)(2,1)} async-done(((bf16[640,512]{1,0:T(8,128)(2,1)}), bf16[2560,512]{1,0:T(8,128)(2,1)}) %all-gather.9.cloned.1.call-update) | async-done | bytes 2621456 | tf_op jit(solution)/shard_map/all_gather | solution.py:1470
  73.5 4.4 all-to-all-start
  79.9 3.4 collective-permute-start.4
  83.3 2.8 collective-permute-start.3
  88.0 2.1 collective-permute-start.1
  90.5 2.6 fusion.10
  93.2 5.1 collective-permute-done.2
  109.0 4.7 all-to-all-start.1
  114.7 16.1 %all-to-all-done.1 = bf16[4,64,1152]{2,1,0:T(8,128)(2,1)S(1)} async-done(((bf16[4,64,1152]{2,1,0:T(8,128)(2,1)}), bf16[4,64,1152]{2,1,0:T(8,128)(2,1)S(1)}, u32[]{:S(2)}, u32[]{:S(2)}) %all-to-all-start.1) | async-done | bytes 589856 | tf_op jit(solution)/shard_map/all_to_all | solution.py:1513
  132.8 40.7 %all_to_all.35 = bf16[4,384,512]{2,1,0:T(8,128)(2,1)} all-to-all(bf16[4,384,512]{2,1,0:T(8,128)(2,1)S(1)} %broadcast_in_dim.74), channel_id=1, replica_groups=mesh['g'=1,'a'=2,'b'=2,'c'=2,'tp'=4] {'tp'}, dimensions={0} | all-to-all | bytes 3145728 | tf_op jit(solution)/shard_map/all_to_all | solution.py:1517
  173.6 4.4 all-to-all-start.2
  178.0 11.2 %reduce-scatter.4.cloned.1.call-start = ((), (), s32[]{:S(2)}) async-start(), calls=%async_computation.10 | async-start | bytes 14155776 | tf_op jit(solution)/shard_map/reduce_scatter | solution.py:1580
  197.8 15.2 %attention_forward.1 = (f32[512,1024]{1,0:T(8,128)}, bf16[512,1024]{1,0:T(8,128)(2,1)}, bf16[512,1024]{1,0:T(8,128)(2,1)}, bf16[4,3,512,256]{3,2,1,0:T(8,128)(2,1)}, bf16[4,512,256]{2,1,0:T(8,128)(2,1)}) custom-call(bf16[4,512,256]{2,1,0:T(8,128)(2,1)} %all-to-all-done.embed_ref, f32[64,1,1024]{2,1,0:T(1,128)} %copy.180.global_ref, f32[1,1024]{1,0:T(1,128)} %bitcast.157, ...), custom_call_target="tpu_custom_call" | custom-call | flops 4294967296 | bytes 14680064 | tf_op jit(solution)/shard_map/attention_forward/pallas_call | solution.py:162
  213.0 26.6 %feed_forward_first.1 = (bf16[512,1024]{1,0:T(8,128)(2,1)}, bf16[1024,512]{1,0:T(8,128)(2,1)}, bf16[512,1024]{1,0:T(8,128)(2,1)}, f32[512,1024]{1,0:T(8,128)}, f...) custom-call(s32[1]{0:T(128)} %bitcast.core_ref, ...), custom_call_target="tpu_custom_call" | custom-call | flops 19327352832 | bytes 33554432 | tf_op jit(solution)/shard_map/feed_forward_first/pallas_call | solution.py:363
  239.7 10.6 %collective-permute-done.5.refs_1_.refs_3_.refs_5_.refs_7_ = bf16[2,2,4,384,512]{4,3,2,1,0:T(8,128)(2,1)S(1)} collective-permute-done((bf16[2,2,4,384,512]{4,3,2,1,0:T(8,128)(2,1)}, bf16[2,2,4,384,512]{4,3,2,1,0:T(8,128)(2,1)S(1)}, u32[]{:S(2)}, u32[]{:S(2)}) %collective-permute-start.5) | collective-permute-done | bytes 6291488 | tf_op jit(solution)/shard_map/ppermute | solution.py:720
  250.3 2.8 copy-done.3
  253.0 2.3 first_sum.3
  255.5 39.5 %collective-permute-done.6.refs_1_.refs_3_ = bf16[2,4,192,512]{3,2,1,0:T(8,128)(2,1)S(1)} collective-permute-done((bf16[2,4,192,512]{3,2,1,0:T(8,128)(2,1)S(1)}, bf16[2,4,192,512]{3,2,1,0:T(8,128)(2,1)S(1)}, u32[]{:S(2)}, u32[]{:S(2)}) %collective-permute-start.6) | collective-permute-done | bytes 1572896 | tf_op jit(solution)/shard_map/ppermute | solution.py:720
  299.1 29.9 %feed_forward_last.1 = (bf16[4,512,256]{2,1,0:T(8,128)(2,1)}, f32[512,1024]{1,0:T(8,128)}, f32[1,1024]{1,0:T(1,128)}, bf16[8,4,384,512]{3,2,1,0:T(8,128)(2,1)}) custom-call(s32[1]{0:T(128)} %bitcast.core_ref, f32[512,1024]{1,0:T(8,128)} %get-tuple-element.104.hidden_ref, bf16[512,1024]{1,0:T(8,128)(2,1)} %get-tuple-element.105.cot_ref, f32[1,1024]{1,0:T(1,128)} %bitcast.168, ...), custom_call_target="tpu_custom_call" | custom-call | flops 19327352832 | bytes 33554432 | tf_op jit(solution)/shard_map/feed_forward_last/pallas_call | solution.py:404
  329.0 4.7 all-to-all-start.4
  335.8 17.2 %collective-permute-done.9.four_ref = bf16[4,192,512]{2,1,0:T(8,128)(2,1)S(1)} collective-permute-done((bf16[4,192,512]{2,1,0:T(8,128)(2,1)}, bf16[4,192,512]{2,1,0:T(8,128)(2,1)S(1)}, u32[]{:S(2)}, u32[]{:S(2)}) %collective-permute-start.9) | collective-permute-done | bytes 786464 | tf_op jit(solution)/shard_map/ppermute | solution.py:720
  359.6 26.6 %attention_backward.1 = (bf16[4,512,256]{2,1,0:T(8,128)(2,1)}, f32[64,1024]{1,0:T(8,128)}, bf16[64,1152]{1,0:T(8,128)(2,1)}, f32[1,1024]{1,0:T(1,128)}, bf16[2,2...) custom-call(s32[1]{0:T(128)} %bitcast.core_ref, f32[512,1024]{1,0:T(8,128)} %copy-done.10, ...), custom_call_target="tpu_custom_call" | custom-call | flops 8589934592 | bytes 27262976 | tf_op jit(solution)/shard_map/attention_backward/pallas_call | solution.py:556
  387.9 17.9 %all_gather.41.returned_ref = bf16[256,1152]{1,0:T(8,128)(2,1)} all-gather(bf16[64,1152]{1,0:T(8,128)(2,1)} %get-tuple-element.128), channel_id=1, replica_groups=mesh['g'=1,'a'=2,'b'=2,'c'=2,'tp'=4] {'tp'}, dimensions={0}, use_global_device_ids=true | all-gather | bytes 737280 | tf_op jit(solution)/shard_map/all_gather | solution.py:1585
  405.8 2.2 copy-done.2
  410.6 4.1 gate_backward.1
  414.8 8.4 %chunk_backward.1 = (f32[256,512]{1,0:T(8,128)}, f32[256,128]{1,0:T(8,128)}, f32[256,128]{1,0:T(8,128)}, f32[256,8]{1,0:T(8,128)}, f32[8,256]{1,0:T(8,128)}, /*index=5*/f32[8,256]{1,0:T(8,128)}, f32[1,8]{1,0:T(1,128)}) custom-call(f32[256,512]{1,0:T(8,128)} %get-tuple-element.134.grad_ref, f32[256,512]{1,0:T(8,128)} %copy-done.23, ...), custom_call_target="tpu_custom_call" | custom-call | flops 805306368 | bytes 4194304 | tf_op jit(solution)/shard_map/chunk_backward/pallas_call | solution.py:1135
  423.3 3.8 pad_maximum_fusion.refs_0_
  433.6 19.1 %collective-permute-done.16.refs_5_.refs_7_ = bf16[2,4,128,512]{3,2,1,0:T(8,128)(2,1)S(1)} collective-permute-done((bf16[2,4,128,512]{3,2,1,0:T(8,128)(2,1)}, bf16[2,4,128,512]{3,2,1,0:T(8,128)(2,1)S(1)}, u32[]{:S(2)}, u32[]{:S(2)}) %collective-permute-start.16) | collective-permute-done | bytes 1048608 | tf_op jit(solution)/shard_map/ppermute | solution.py:720
  458.3 6.6 %front_backward.1 = (f32[256,768]{1,0:T(8,128)}, f32[8,768]{1,0:T(8,128)}, f32[4,768]{1,0:T(4,128)}, bf16[8,256]{1,0:T(8,128)(2,1)}, f32[8,1]{1,0:T(8,128)}, /*index=5*/f32[8,1]{1,0:T(8,128)}) custom-call(bf16[528,128]{1,0:T(8,128)(2,1)} %copy-done.50, bf16[528,128]{1,0:T(8,128)(2,1)} %copy-done.49, bf16[528,128]{1,0:T(8,128)(2,1)} %copy-done.48, ...), custom_call_target="tpu_custom_call" | custom-call | flops 603979776 | bytes 8388608 | tf_op jit(solution)/shard_map/front_backward/pallas_call | solution.py:1273
  468.2 2.6 collective-permute-done.17
  473.0 4.6 mixer_weight_grads.1
  477.5 2.9 collective-permute-start.20
  486.6 7.7 %collective-permute-done.18.two_ref = bf16[4,128,512]{2,1,0:T(8,128)(2,1)S(1)} collective-permute-done((bf16[4,128,512]{2,1,0:T(8,128)(2,1)S(1)}, bf16[4,128,512]{2,1,0:T(8,128)(2,1)S(1)}, u32[]{:S(2)}, u32[]{:S(2)}) %collective-permute-start.18) | collective-permute-done | bytes 524320 | tf_op jit(solution)/shard_map/ppermute | solution.py:720
  499.7 9.1 %collective-permute-done.21.refs_1_.refs_3_ = bf16[2,1,224,512]{3,2,1,0:T(8,128)(2,1)S(1)} collective-permute-done((bf16[2,1,224,512]{3,2,1,0:T(8,128)(2,1)S(1)}, bf16[2,1,224,512]{3,2,1,0:T(8,128)(2,1)S(1)}, u32[]{:S(2)}, u32[]{:S(2)}) %collective-permute-start.21) | collective-permute-done | bytes 458784 | tf_op jit(solution)/shard_map/ppermute | solution.py:720
  512.2 4.1 collective-permute-done.23.two_ref
  517.8 17.6 %all_gather.42 = bf16[4,64,512]{2,1,0:T(8,128)(2,1)S(1)} all-gather(bf16[1,64,512]{2,1,0:T(8,128)(2,1)S(1)} %slice.220), channel_id=1, replica_groups=mesh['g'=1,'a'=2,'b'=2,'c'=2,'tp'=4] {'tp'}, dimensions={0}, use_global_device_ids=true | all-gather | bytes 327680 | tf_op jit(solution)/shard_map/all_gather | solution.py:1664
  535.5 2.2 pad_maximum_fusion.1
  537.7 3.5 all-to-all-start.5
  543.2 5.1 project_backward.1
  551.6 11.3 %all-to-all-done.5 = bf16[4,512,256]{2,1,0:T(8,128)(2,1)S(1)} async-done(((bf16[4,512,256]{2,1,0:T(8,128)(2,1)}), bf16[4,512,256]{2,1,0:T(8,128)(2,1)S(1)}, u32[]{:S(2)}, u32[]{:S(2)}) %all-to-all-start.5) | async-done | bytes 1048608 | tf_op jit(solution)/shard_map/all_to_all | solution.py:1478
  562.8 3.5 all-to-all-start.6
  568.1 11.8 %all-to-all-done.6 = bf16[4,288,256]{2,1,0:T(8,128)(2,1)S(1)} async-done(((bf16[4,288,256]{2,1,0:T(8,128)(2,1)}), bf16[4,288,256]{2,1,0:T(8,128)(2,1)S(1)}, u32[]{:S(2)}, u32[]{:S(2)}) %all-to-all-start.6) | async-done | bytes 589856 | tf_op jit(solution)/shard_map/all_to_all | solution.py:1696
  580.8 26.1 %all-reduce.1 = (f32[1024]{0:T(1024)}, f32[1024,8]{0,1:T(8,128)}, f32[8]{0:T(128)}, f32[8]{0:T(128)}, f32[4,512]{1,0:T(4,128)}, /*index=5*/f32[4,256]{1,0:T(4,12...) all-reduce(f32[1024]{0:T(1024)S(1)} %bitcast.155, ...), channel_id=1, replica_groups=mesh['g'=1,'a'=2,'b'=2,'c'=2,'tp'=4] {'g','a','b','c'}, use_global_device_ids=true, to_apply=%region_9.10 | all-reduce | flops 14872 | bytes 118976 | tf_op jit(solution)/shard_map/psum | solution.py:1726
  607.1 4.4 copy-done.5
  611.5 8.2 %unpack.1 = (f32[2,1024,1024]{2,1,0:T(8,128)}, f32[2,8,64,1024]{3,2,1,0:T(8,128)}, f32[3,1024,256]{2,1,0:T(8,128)}, f32[256,1024]{1,0:T(8,128)}, f32[1024,512]{1...) custom-call(bf16[8,1472,512]{2,1,0:T(8,128)(2,1)S(1)} %bitcast.109), custom_call_target="tpu_custom_call" | custom-call | flops 6029312 | bytes 36175872 | tf_op jit(solution)/shard_map/unpack/pallas_call | solution.py:928
  619.7 2.3 copy.206
  (369 shorter events, 103.1 us)
Async XLA Ops:
  7.2 66.3 %all-gather.9.cloned.1.call-start = ((), (), s32[]{:S(2)}) async-start(), calls=%async_computation.13 | async-start | bytes 3276800 | tf_op jit(solution)/shard_map/all_gather | solution.py:1470
  10.1 24.6 %copy-start.62 = (f32[1024]{0:T(1024)S(1)}, f32[1024]{0:T(1024)}, u32[]{:S(2)}) copy-start(f32[1024]{0:T(1024)} %param.25) | copy-start | bytes 12292
  12.8 22.1 %copy-start.32 = (bf16[1024,256]{1,0:T(8,128)(2,1)S(1)}, bf16[1024,256]{1,0:T(8,128)(2,1)}, u32[]{:S(2)}) copy-start(bf16[1024,256]{1,0:T(8,128)(2,1)} %state_ref.1) | copy-start | bytes 1572868
  13.7 184.0 %all-gather.11.cloned.1.call-start = ((), (), s32[]{:S(2)}) async-start(), calls=%async_computation.14 | async-start | bytes 23592960 | tf_op jit(solution)/shard_map/all_gather | solution.py:1500
  34.5 161.5 %copy-start.24 = (bf16[256,1024]{1,0:T(8,128)(2,1)}, bf16[256,1024]{1,0:T(8,128)(2,1)S(1)}, u32[]{:S(2)}) copy-start(bf16[256,1024]{1,0:T(8,128)(2,1)S(1)} %all_gather.34.rows_ref) | copy-start | bytes 1572868
  34.9 67.2 %copy-start.22 = (bf16[256,1024]{1,0:T(8,128)(2,1)}, bf16[256,1024]{1,0:T(8,128)(2,1)S(1)}, u32[]{:S(2)}) copy-start(bf16[256,1024]{1,0:T(8,128)(2,1)S(1)} %fusion.15.normed_ref) | copy-start | bytes 1572868
  37.0 8.8 %collective-permute-start = (f32[3,768]{1,0:T(4,128)S(1)}, f32[3,768]{1,0:T(4,128)S(1)}, u32[]{:S(2)}, u32[]{:S(2)}) collective-permute-start(f32[3,768]{1,0:T(4,128)S(1)} %fusion.46), channel_id=1, source_target_pairs={{0,4},{4,8},{8,12},{12,16},{16,20},{20,24},{24,28},{1,5},{5,9},{9,... | collective-permute-start | bytes 27656 | tf_op jit(solution)/shard_map/ppermute | solution.py:606
  39.1 151.7 %copy-start.55 = (s32[256]{0:T(256)}, s32[256]{0:T(256)S(1)}, u32[]{:S(2)}) copy-start(s32[256]{0:T(256)S(1)} %select_reduce_fusion) | copy-start | bytes 3076
  42.0 48.5 %copy-start.52 = (f32[8,256]{1,0:T(8,128)}, f32[8,256]{1,0:T(8,128)S(1)}, u32[]{:S(2)}) copy-start(f32[8,256]{1,0:T(8,128)S(1)} %get-tuple-element.212.refs_4_.steps_row_ref.refs_9_) | copy-start | bytes 24580
  46.5 52.8 %copy-start.25 = (f32[256,768]{1,0:T(8,128)}, f32[256,768]{1,0:T(8,128)S(1)}, u32[]{:S(2)}) copy-start(f32[256,768]{1,0:T(8,128)S(1)} %divide_multiply_fusion) | copy-start | bytes 2359300
  46.6 26.9 %copy-start.23 = (f32[256,512]{1,0:T(8,128)}, f32[256,512]{1,0:T(8,128)S(1)}, u32[]{:S(2)}) copy-start(f32[256,512]{1,0:T(8,128)S(1)} %slice.244.refs_11_.inner_ref.refs_5_) | copy-start | bytes 1572868
  73.5 30.7 %all-to-all-start = ((bf16[4,512,256]{2,1,0:T(8,128)(2,1)}), bf16[4,512,256]{2,1,0:T(8,128)(2,1)}, u32[]{:S(2)}, u32[]{:S(2)}) async-start(bf16[4,512,256]{2,1,0:T(8,128)(2,1)} %bitcast.132), calls=%async_computation | async-start | bytes 2097152 | tf_op jit(solution)/shard_map/all_to_all | solution.py:1475
  79.9 19.4 %collective-permute-start.4 = (bf16[528,128]{1,0:T(8,128)(2,1)S(1)}, bf16[528,128]{1,0:T(8,128)(2,1)S(1)}, u32[]{:S(2)}, u32[]{:S(2)}) collective-permute-start(bf16[528,128]{1,0:T(8,128)(2,1)S(1)} %pad_maximum_fusion.6), channel_id=1, source_target_pairs={{0,16},{4,20},{8,24},{12,28},{1,17},{5,21},{9,25},{13,29},{2,18},{... | collective-permute-start | bytes 405512 | tf_op jit(solution)/shard_map/ppermute | solution.py:700
  83.3 15.0 %collective-permute-start.3 = (bf16[528,128]{1,0:T(8,128)(2,1)S(1)}, bf16[528,128]{1,0:T(8,128)(2,1)S(1)}, u32[]{:S(2)}, u32[]{:S(2)}) collective-permute-start(bf16[528,128]{1,0:T(8,128)(2,1)S(1)} %pad_maximum_fusion.6), channel_id=1, source_target_pairs={{0,12},{4,16},{8,20},{12,24},{16,28},{1,13},{5,17},{9,21},{13,25},... | collective-permute-start | bytes 405512 | tf_op jit(solution)/shard_map/ppermute | solution.py:700
  86.1 12.1 %collective-permute-start.2 = (bf16[528,128]{1,0:T(8,128)(2,1)S(1)}, bf16[528,128]{1,0:T(8,128)(2,1)S(1)}, u32[]{:S(2)}, u32[]{:S(2)}) collective-permute-start(bf16[528,128]{1,0:T(8,128)(2,1)S(1)} %pad_maximum_fusion.6), channel_id=1, source_target_pairs={{0,8},{4,12},{8,16},{12,20},{16,24},{20,28},{1,9},{5,13},{9,17},{1... | collective-permute-start | bytes 405512 | tf_op jit(solution)/shard_map/ppermute | solution.py:700
  88.0 5.1 collective-permute-start.1
  109.0 21.8 %all-to-all-start.1 = ((bf16[4,64,1152]{2,1,0:T(8,128)(2,1)}), bf16[4,64,1152]{2,1,0:T(8,128)(2,1)S(1)}, u32[]{:S(2)}, u32[]{:S(2)}) async-start(bf16[4,64,1152]{2,1,0:T(8,128)(2,1)} %bitcast.23), calls=%async_computation.1 | async-start | bytes 1179648 | tf_op jit(solution)/shard_map/all_to_all | solution.py:1513
  113.8 185.3 %all-gather.13.cloned.1.call-start = ((), (), s32[]{:S(2)}) async-start(), calls=%async_computation.15 | async-start | bytes 14155776 | tf_op jit(solution)/shard_map/all_gather | solution.py:1520
  173.6 39.3 %all-to-all-start.2 = ((bf16[4,512,256]{2,1,0:T(8,128)(2,1)}), bf16[4,512,256]{2,1,0:T(8,128)(2,1)}, u32[]{:S(2)}, u32[]{:S(2)}) async-start(bf16[4,512,256]{2,1,0:T(8,128)(2,1)} %bitcast.133), calls=%async_computation.2 | async-start | bytes 2097152 | tf_op jit(solution)/shard_map/all_to_all | solution.py:1475
  178.0 245.2 %reduce-scatter.4.cloned.1.call-start = ((), (), s32[]{:S(2)}) async-start(), calls=%async_computation.10 | async-start | bytes 14155776 | tf_op jit(solution)/shard_map/reduce_scatter | solution.py:1580
  239.6 10.7 %collective-permute-start.5 = (bf16[2,2,4,384,512]{4,3,2,1,0:T(8,128)(2,1)}, bf16[2,2,4,384,512]{4,3,2,1,0:T(8,128)(2,1)S(1)}, u32[]{:S(2)}, u32[]{:S(2)}) collective-permute-start(bf16[2,2,4,384,512]{4,3,2,1,0:T(8,128)(2,1)} %get-tuple-element.111), channel_id=1, source_target_pairs={{0,4},{4,0},{1,5},{5,1},{2,6},{6,2},{3,7},{7,3},{8,12},{12,8},{9,1... | collective-permute-start | bytes 18874376 | tf_op jit(solution)/shard_map/ppermute | solution.py:720
  255.4 39.6 %collective-permute-start.6 = (bf16[2,4,192,512]{3,2,1,0:T(8,128)(2,1)S(1)}, bf16[2,4,192,512]{3,2,1,0:T(8,128)(2,1)S(1)}, u32[]{:S(2)}, u32[]{:S(2)}) collective-permute-start(bf16[2,4,192,512]{3,2,1,0:T(8,128)(2,1)S(1)} %get-tuple-element.113), channel_id=1, source_target_pairs={{0,8},{8,0},{1,9},{9,1},{2,10},{10,2},{3,11},{11,3},{4,12},{12,4},... | collective-permute-start | bytes 4718600 | tf_op jit(solution)/shard_map/ppermute | solution.py:720
  255.5 39.6 %collective-permute-start.7 = (bf16[2,4,192,512]{3,2,1,0:T(8,128)(2,1)S(1)}, bf16[2,4,192,512]{3,2,1,0:T(8,128)(2,1)S(1)}, u32[]{:S(2)}, u32[]{:S(2)}) collective-permute-start(bf16[2,4,192,512]{3,2,1,0:T(8,128)(2,1)S(1)} %get-tuple-element.115), channel_id=1, source_target_pairs={{0,16},{16,0},{1,17},{17,1},{2,18},{18,2},{3,19},{19,3},{4,20},{20... | collective-permute-start | bytes 4718600 | tf_op jit(solution)/shard_map/ppermute | solution.py:720
  329.0 25.1 %copy-start.9 = (f32[512,1024]{1,0:T(8,128)S(1)}, f32[512,1024]{1,0:T(8,128)}, u32[]{:S(2)}) copy-start(f32[512,1024]{1,0:T(8,128)} %get-tuple-element.121.refs_0_) | copy-start | bytes 6291460
  329.0 30.6 %all-to-all-start.4 = ((bf16[4,512,256]{2,1,0:T(8,128)(2,1)}), bf16[4,512,256]{2,1,0:T(8,128)(2,1)}, u32[]{:S(2)}, u32[]{:S(2)}) async-start(bf16[4,512,256]{2,1,0:T(8,128)(2,1)} %get-tuple-element.117), calls=%async_computation.4 | async-start | bytes 2097152 | tf_op jit(solution)/shard_map/all_to_all | solution.py:1478
  333.8 163.1 %reduce-scatter.6.cloned.1.call-start = ((), (), s32[]{:S(2)}) async-start(), calls=%async_computation.11 | async-start | bytes 3932160 | tf_op jit(solution)/shard_map/reduce_scatter | solution.py:853
  333.8 19.3 %collective-permute-start.9 = (bf16[4,192,512]{2,1,0:T(8,128)(2,1)}, bf16[4,192,512]{2,1,0:T(8,128)(2,1)S(1)}, u32[]{:S(2)}, u32[]{:S(2)}) collective-permute-start(bf16[4,192,512]{2,1,0:T(8,128)(2,1)} %copy-done.21), channel_id=1, source_target_pairs={{0,8},{8,0},{1,9},{9,1},{2,10},{10,2},{3,11},{11,3},{4,12},{12,4},... | collective-permute-start | bytes 2359304 | tf_op jit(solution)/shard_map/ppermute | solution.py:720
  335.2 18.9 %collective-permute-start.8 = (bf16[4,192,512]{2,1,0:T(8,128)(2,1)}, bf16[4,192,512]{2,1,0:T(8,128)(2,1)S(1)}, u32[]{:S(2)}, u32[]{:S(2)}) collective-permute-start(bf16[4,192,512]{2,1,0:T(8,128)(2,1)} %copy-done.20), channel_id=1, source_target_pairs={{0,16},{16,0},{1,17},{17,1},{2,18},{18,2},{3,19},{19,3},{4,20},{20... | collective-permute-start | bytes 2359304 | tf_op jit(solution)/shard_map/ppermute | solution.py:720
  386.2 19.6 %collective-permute-start.10 = (bf16[2,2,4,256,512]{4,3,2,1,0:T(8,128)(2,1)}, bf16[2,2,4,256,512]{4,3,2,1,0:T(8,128)(2,1)S(1)}, u32[]{:S(2)}, u32[]{:S(2)}) collective-permute-start(bf16[2,2,4,256,512]{4,3,2,1,0:T(8,128)(2,1)} %get-tuple-element.130), channel_id=1, source_target_pairs={{0,4},{4,0},{1,5},{5,1},{2,6},{6,2},{3,7},{7,3},{8,12},{12,8},{9,1... | collective-permute-start | bytes 12582920 | tf_op jit(solution)/shard_map/ppermute | solution.py:720
  427.0 108.4 %reduce-scatter.8.cloned.1.call-start = ((), (), s32[]{:S(2)}) async-start(), calls=%async_computation.12 | async-start | bytes 1310720 | tf_op jit(solution)/shard_map/reduce_scatter | solution.py:853
  427.1 25.5 %collective-permute-start.16 = (bf16[2,4,128,512]{3,2,1,0:T(8,128)(2,1)}, bf16[2,4,128,512]{3,2,1,0:T(8,128)(2,1)S(1)}, u32[]{:S(2)}, u32[]{:S(2)}) collective-permute-start(bf16[2,4,128,512]{3,2,1,0:T(8,128)(2,1)} %copy-done.19), channel_id=1, source_target_pairs={{0,16},{16,0},{1,17},{17,1},{2,18},{18,2},{3,19},{19,3},{4,20},{20... | collective-permute-start | bytes 3145736 | tf_op jit(solution)/shard_map/ppermute | solution.py:720
  428.2 26.1 %collective-permute-start.15 = (bf16[2,4,128,512]{3,2,1,0:T(8,128)(2,1)S(1)}, bf16[2,4,128,512]{3,2,1,0:T(8,128)(2,1)S(1)}, u32[]{:S(2)}, u32[]{:S(2)}) collective-permute-start(bf16[2,4,128,512]{3,2,1,0:T(8,128)(2,1)S(1)} %copy-done.8), channel_id=1, source_target_pairs={{0,8},{8,0},{1,9},{9,1},{2,10},{10,2},{3,11},{11,3},{4,12},{12,4},... | collective-permute-start | bytes 3145736 | tf_op jit(solution)/shard_map/ppermute | solution.py:720
  429.7 27.8 %collective-permute-start.14 = (bf16[528,128]{1,0:T(8,128)(2,1)}, bf16[528,128]{1,0:T(8,128)(2,1)S(1)}, u32[]{:S(2)}, u32[]{:S(2)}) collective-permute-start(bf16[528,128]{1,0:T(8,128)(2,1)} %get-tuple-element.133), channel_id=1, source_target_pairs={{16,0},{20,4},{24,8},{28,12},{17,1},{21,5},{25,9},{29,13},{18,2},{... | collective-permute-start | bytes 405512 | tf_op jit(solution)/shard_map/ppermute | solution.py:1622
  431.0 26.6 %collective-permute-start.13 = (bf16[528,128]{1,0:T(8,128)(2,1)}, bf16[528,128]{1,0:T(8,128)(2,1)S(1)}, u32[]{:S(2)}, u32[]{:S(2)}) collective-permute-start(bf16[528,128]{1,0:T(8,128)(2,1)} %get-tuple-element.133), channel_id=1, source_target_pairs={{12,0},{16,4},{20,8},{24,12},{28,16},{13,1},{17,5},{21,9},{25,13},... | collective-permute-start | bytes 405512 | tf_op jit(solution)/shard_map/ppermute | solution.py:1622
  432.3 25.3 %collective-permute-start.12 = (bf16[528,128]{1,0:T(8,128)(2,1)}, bf16[528,128]{1,0:T(8,128)(2,1)S(1)}, u32[]{:S(2)}, u32[]{:S(2)}) collective-permute-start(bf16[528,128]{1,0:T(8,128)(2,1)} %get-tuple-element.133), channel_id=1, source_target_pairs={{8,0},{12,4},{16,8},{20,12},{24,16},{28,20},{9,1},{13,5},{17,9},{2... | collective-permute-start | bytes 405512 | tf_op jit(solution)/shard_map/ppermute | solution.py:1622
  452.6 4.9 collective-permute-start.11
  464.9 5.9 collective-permute-start.17
  477.5 6.5 %collective-permute-start.20 = (bf16[2,2,1,448,512]{4,3,2,1,0:T(8,128)(2,1)}, bf16[2,2,1,448,512]{4,3,2,1,0:T(8,128)(2,1)S(1)}, u32[]{:S(2)}, u32[]{:S(2)}) collective-permute-start(bf16[2,2,1,448,512]{4,3,2,1,0:T(8,128)(2,1)} %get-tuple-element.152), channel_id=1, source_target_pairs={{0,4},{4,0},{1,5},{5,1},{2,6},{6,2},{3,7},{7,3},{8,12},{12,8},{9,1... | collective-permute-start | bytes 5505032 | tf_op jit(solution)/shard_map/ppermute | solution.py:720
  480.4 13.8 %collective-permute-start.18 = (bf16[4,128,512]{2,1,0:T(8,128)(2,1)S(1)}, bf16[4,128,512]{2,1,0:T(8,128)(2,1)S(1)}, u32[]{:S(2)}, u32[]{:S(2)}) collective-permute-start(bf16[4,128,512]{2,1,0:T(8,128)(2,1)S(1)} %get-tuple-element.147), channel_id=1, source_target_pairs={{0,16},{16,0},{1,17},{17,1},{2,18},{18,2},{3,19},{19,3},{4,20},{20... | collective-permute-start | bytes 1572872 | tf_op jit(solution)/shard_map/ppermute | solution.py:720
  481.5 14.1 %collective-permute-start.19 = (bf16[4,128,512]{2,1,0:T(8,128)(2,1)S(1)}, bf16[4,128,512]{2,1,0:T(8,128)(2,1)S(1)}, u32[]{:S(2)}, u32[]{:S(2)}) collective-permute-start(bf16[4,128,512]{2,1,0:T(8,128)(2,1)S(1)} %get-tuple-element.149), channel_id=1, source_target_pairs={{0,8},{8,0},{1,9},{9,1},{2,10},{10,2},{3,11},{11,3},{4,12},{12,4},... | collective-permute-start | bytes 1572872 | tf_op jit(solution)/shard_map/ppermute | solution.py:720
  496.9 110.2 %all-gather.15.cloned.1.call-start = ((), (), s32[]{:S(2)}) async-start(), calls=%async_computation.16 | async-start | bytes 13565952 | tf_op jit(solution)/shard_map/all_gather | solution.py:1739
  496.9 11.9 %collective-permute-start.21 = (bf16[2,1,224,512]{3,2,1,0:T(8,128)(2,1)S(1)}, bf16[2,1,224,512]{3,2,1,0:T(8,128)(2,1)S(1)}, u32[]{:S(2)}, u32[]{:S(2)}) collective-permute-start(bf16[2,1,224,512]{3,2,1,0:T(8,128)(2,1)S(1)} %get-tuple-element.155), channel_id=1, source_target_pairs={{0,8},{8,0},{1,9},{9,1},{2,10},{10,2},{3,11},{11,3},{4,12},{12,4},... | collective-permute-start | bytes 1376264 | tf_op jit(solution)/shard_map/ppermute | solution.py:720
  498.1 11.4 %collective-permute-start.22 = (bf16[2,1,224,512]{3,2,1,0:T(8,128)(2,1)S(1)}, bf16[2,1,224,512]{3,2,1,0:T(8,128)(2,1)S(1)}, u32[]{:S(2)}, u32[]{:S(2)}) collective-permute-start(bf16[2,1,224,512]{3,2,1,0:T(8,128)(2,1)S(1)} %get-tuple-element.157), channel_id=1, source_target_pairs={{0,16},{16,0},{1,17},{17,1},{2,18},{18,2},{3,19},{19,3},{4,20},{20... | collective-permute-start | bytes 1376264 | tf_op jit(solution)/shard_map/ppermute | solution.py:720
  510.3 25.2 %copy-start.31 = (bf16[1,768,512]{2,1,0:T(8,128)(2,1)S(1)}, bf16[1,768,512]{2,1,0:T(8,128)(2,1)}, u32[]{:S(2)}) copy-start(bf16[1,768,512]{2,1,0:T(8,128)(2,1)} %reduce-scatter.6.cloned.1.call-done) | copy-start | bytes 2359300
  510.3 6.1 collective-permute-start.23
  511.6 6.0 collective-permute-start.24
  537.7 25.1 %all-to-all-start.5 = ((bf16[4,512,256]{2,1,0:T(8,128)(2,1)}), bf16[4,512,256]{2,1,0:T(8,128)(2,1)S(1)}, u32[]{:S(2)}, u32[]{:S(2)}) async-start(bf16[4,512,256]{2,1,0:T(8,128)(2,1)} %get-tuple-element.127), calls=%async_computation.5 | async-start | bytes 2097152 | tf_op jit(solution)/shard_map/all_to_all | solution.py:1478
  562.8 17.1 %all-to-all-start.6 = ((bf16[4,288,256]{2,1,0:T(8,128)(2,1)}), bf16[4,288,256]{2,1,0:T(8,128)(2,1)S(1)}, u32[]{:S(2)}, u32[]{:S(2)}) async-start(bf16[4,288,256]{2,1,0:T(8,128)(2,1)} %pad_maximum_fusion.4), calls=%async_computation.6 | async-start | bytes 1179648 | tf_op jit(solution)/shard_map/all_to_all | solution.py:1696
  (75 other events, 572.4 us)
Sparse Core Ops, SparseCore 0:
  13.8 59.5 all-gather.8
  75.4 114.1 all-gather.10
  191.4 75.1 all-gather.12
  329.1 92.3 reduce-scatter.3
  427.2 59.6 reduce-scatter.5
  497.0 31.5 reduce-scatter.7
  537.8 69.2 all-gather.14
